TPU v7x, 32 devices: a whole 2x2x4 slice. The times are simulated.
32 devices in a mesh: gx: 16 (over z, x, core), gy: 2 (over y).
Axes of the slice: x: 2, y: 2, z: 4, core: 2. Of those that a mesh axis runs over, the one named last changes fastest.
Arguments:
- right_side: float32 [2, 512, 64, 256], P(None, 'gx', 'gy'), may hold values from -8 to 8
- diagonal: float32 [512, 64, 256], P('gx', 'gy'), may hold values from 0.005 to 0.3
- aggregates: int32 [16], replicated, may hold values from 0 to 3, never falling along the last dimension, each value on 1 to 8 neighbouring positions
Outputs:
- solution: float32 [2, 512, 64, 256], P(None, 'gx', 'gy')
Inputs may be any that keep to these rules, and one draw needn't show every extreme that they name: aggregates never falls from one index of gx to the next; each aggregate holds between 1 and 8 consecutive indices, and one holds exactly 8.
All inputs are finite; a program needn't handle non-finite values.
Results may differ from a plain program's by a relative error of at most 0.000071.
Values sent between devices are 32-bit elements; how exact they have to be, the bound alone decides.
No kernel may reach another device: no remote copies, remote signals or barrier semaphores. Data moves between devices by JAX's collectives and lax.ppermute only.
A program may use at most 128 MiB of HBM per device.

v0:
```python
import jax
import jax.numpy as jnp
from jax import lax
from jax.sharding import PartitionSpec as P

DEGREE = 3
COARSE_DEG = 6


FINE_LOWER = 3.0
FINE_UPPER = 12.4
COARSE_LOWER = 0.5
COARSE_UPPER = 13.4


def with_halo(cells, sides, width):
    for axis, dim in sides:
        count = lax.axis_size(axis)
        ends = count - 1
        head = lax.slice_in_dim(cells, 0, width, axis=dim)
        tail = lax.slice_in_dim(cells, cells.shape[dim] - width, cells.shape[dim], axis=dim)
        cells = jnp.concatenate(
            [
                lax.ppermute(tail, axis, [(i, (i + 1) % count) for i in range(ends)]),
                cells,
                lax.ppermute(head, axis, [((i + 1) % count, i) for i in range(ends)]),
            ],
            axis=dim,
        )
    return cells


def cheb_pairs(lower, upper, count):
    middle = (upper + lower) / 2.0
    halfwidth = (upper - lower) / 2.0
    ratio_mid = middle / halfwidth
    rho_old = 1.0 / ratio_mid
    result = [(0.0, 1.0 / middle)]
    for repeat in range(count - 1):
        rho_new = 1.0 / (2.0 * ratio_mid - rho_old)
        result.append((rho_new * rho_old, 2.0 * rho_new / halfwidth))
        rho_old = rho_new
    return result


def neighbours(padded):
    center = padded[:, 1:-1, 1:-1]
    deeper = jnp.pad(center, ((0, 0), (0, 0), (0, 0), (1, 1)))
    nearby = padded[:, 2:, 1:-1] + padded[:, :-2, 1:-1]
    nearby = nearby + padded[:, 1:-1, 2:] + padded[:, 1:-1, :-2]
    nearby = nearby + deeper[..., 2:] + deeper[..., :-2]
    return (nearby, center)


def fine_apply(field, diagonal):
    padded = with_halo(field, (("gx", 1), ("gy", 2)), 1)
    nearby, center = neighbours(padded)
    return (6.0 + diagonal) * center - nearby


def pick_entry(table, where):
    places = jnp.arange(table.shape[0], dtype=jnp.int32)
    return jnp.sum(jnp.where(places == where, table, 0))


def pair_along_depth(field, pairing):
    return jnp.dot(
        field, pairing, precision=lax.Precision.HIGHEST, preferred_element_type=jnp.float32
    )


def on_device(right_side, diagonal, aggregates):
    fine_pairs = cheb_pairs(FINE_LOWER, FINE_UPPER, DEGREE)
    coarse_pairs = cheb_pairs(COARSE_LOWER, COARSE_UPPER, COARSE_DEG)
    rows_x = right_side.shape[1]
    rows_y = right_side.shape[2]
    depth_z = right_side.shape[3]
    solution = jnp.zeros_like(right_side)
    residual = right_side
    update = jnp.zeros_like(right_side)
    for scale_old, scale_res in fine_pairs:
        update = scale_old * update + scale_res * residual
        solution = solution + update
        residual = residual - fine_apply(update, diagonal)
    half_x = rows_x // 2
    half_y = rows_y // 2
    half_z = depth_z // 2
    fine_idx = jnp.arange(depth_z, dtype=jnp.int32)
    coarse_idx = jnp.arange(half_z, dtype=jnp.int32)
    pairing = (fine_idx[:, None] // 2 == coarse_idx[None, :]).astype(jnp.float32)
    paired_res = pair_along_depth(residual, pairing)
    coarse_rhs = 0.5 * paired_res.reshape(2, half_x, 2, half_y, 2, half_z).sum((2, 4))
    paired_diag = pair_along_depth(diagonal, pairing)
    coarse_diag = 0.5 * paired_diag.reshape(half_x, 2, half_y, 2, half_z).sum((1, 3))
    own_row = lax.axis_index("gx")
    agg_here = pick_entry(aggregates, own_row)
    link_lower = (pick_entry(aggregates, own_row - 1) == agg_here).astype(jnp.float32)
    link_upper = (pick_entry(aggregates, own_row + 1) == agg_here).astype(jnp.float32)
    plane_mask = jnp.concatenate(
        [link_lower[None], jnp.ones((half_x,), jnp.float32), link_upper[None]]
    )
    plane_mask = plane_mask[None, :, None, None]
    coarse_stack = jnp.concatenate([coarse_rhs, coarse_diag[None]], 0)
    slab = lax.all_gather(coarse_stack, "gy", axis=2, tiled=True)
    slab_rhs = slab[:2]
    slab_diag = slab[2]
    correction = jnp.zeros_like(slab_rhs)
    coarse_res = slab_rhs
    coarse_upd = jnp.zeros_like(slab_rhs)
    for position, (scale_old, scale_res) in enumerate(coarse_pairs):
        coarse_upd = scale_old * coarse_upd + scale_res * coarse_res
        correction = correction + coarse_upd
        if position + 1 < COARSE_DEG:
            padded = with_halo(coarse_upd, (("gx", 1),), 1)
            padded = jnp.pad(padded * plane_mask, ((0, 0), (0, 0), (1, 1), (0, 0)))
            nearby, center = neighbours(padded)
            coarse_res = coarse_res - ((6.0 + slab_diag) * center - nearby)
    correction = lax.dynamic_slice_in_dim(correction, lax.axis_index("gy") * half_y, half_y, 2)
    deep_spread = pair_along_depth(correction, pairing.T)
    spread = jnp.repeat(jnp.repeat(deep_spread, 2, axis=1), 2, axis=2)
    solution = solution + spread
    residual = right_side - fine_apply(solution, diagonal)
    update = jnp.zeros_like(right_side)
    for position, (scale_old, scale_res) in enumerate(fine_pairs):
        update = scale_old * update + scale_res * residual
        solution = solution + update
        if position + 1 < DEGREE:
            residual = residual - fine_apply(update, diagonal)
    return solution


def solution(mesh):
    return jax.shard_map(
        on_device,
        mesh=mesh,
        in_specs=(P(None, "gx", "gy", None), P("gx", "gy", None), P()),
        out_specs=P(None, "gx", "gy", None),
        check_vma=False,
    )
```

profile of v0, /device:TPU:21, one launch (start us, length us, event | category | flops | bytes accessed | tf_op | source)
XLA Modules:
  0.0 206.5 jit_solution(16018338480842723376)
XLA Ops:
  0.0 3.0 %copy_multiply_fusion = f32[2,32,32,256]{3,1,2,0:T(8,128)S(1)} fusion(f32[2,32,32,256]{3,2,1,0:T(8,128)} %param.3), kind=kLoop, calls=%fused_computation.111 | loop fusion | flops 524288 | bytes 4194304 | tf_op jit(solution)/shard_map/mul | solution.py:82
  3.1 3.7 %collective-permute-start.1 = (f32[2,1,32,256]{3,1,2,0:T(1,128)S(1)}, f32[2,1,32,256]{3,1,2,0:T(1,128)S(1)}, u32[]{:S(2)}, u32[]{:S(2)}) collective-permute-start(f32[2,1,32,256]{3,1,2,0:T(1,128)S(1)} %get-tuple-element.46), channel_id=1, source_target_pairs={{0,2},{2,4},{4,6},{6,8},{8,10},{10,12},{12,14},{14,16},{16,18},{18... | collective-permute-start | bytes 196616 | tf_op jit(solution)/shard_map/ppermute | solution.py:24
  6.8 1.9 collective-permute-start
  8.7 1.4 broadcast_add_fusion
  10.7 1.6 collective-permute-done
  12.4 2.1 %collective-permute-start.2 = (f32[2,34,1,256]{3,1,2,0:T(8,128)S(1)}, f32[2,34,1,256]{3,1,2,0:T(8,128)S(1)}, u32[]{:S(2)}, u32[]{:S(2)}) collective-permute-start(f32[2,34,1,256]{3,1,2,0:T(8,128)S(1)} %get-tuple-element.34), channel_id=1, source_target_pairs={{1,0},{3,2},{5,4},{7,6},{9,8},{11,10},{13,12},{15,14},{17,16},{19,... | collective-permute-start | bytes 208904 | tf_op jit(solution)/shard_map/ppermute | solution.py:26
  16.5 3.8 %collective-permute-done.3 = f32[2,34,1,256]{3,1,2,0:T(8,128)S(1)} collective-permute-done((f32[2,34,1,256]{3,1,2,0:T(8,128)S(1)}, f32[2,34,1,256]{3,1,2,0:T(8,128)S(1)}, u32[]{:S(2)}, u32[]{:S(2)}) %collective-permute-start.3) | collective-permute-done | bytes 69664 | tf_op jit(solution)/shard_map/ppermute | solution.py:24
  20.3 5.2 %multiply_add_fusion.2 = (f32[2,32,32,256]{3,1,2,0:T(8,128)S(1)}, f32[2,32,32,256]{3,1,2,0:T(8,128)}) fusion(f32[2,32,32,256]{3,2,1,0:T(8,128)S(1)} %copy-done, f32[2,32,32,256]{3,1,2,0:T(8,128)S(1)} %copy_multiply_fusion, f32[2,1,32,256]{3,1,2,0:T(1,128)S(1)} %collective-permute-done, f32[2,1,32,256]{3,1,2,0:T(1,128)S(1)} %collective-permute-done.1, ...), kind=kLoop, calls=%fused_computation.110 | loop fusion | flops 9961472 | bytes 9707520 | tf_op jit(solution)/shard_map/add | solution.py:82
  25.6 2.9 %collective-permute-start.5 = (f32[2,1,32,256]{3,1,2,0:T(1,128)S(1)}, f32[2,1,32,256]{3,1,2,0:T(1,128)S(1)}, u32[]{:S(2)}, u32[]{:S(2)}) collective-permute-start(f32[2,1,32,256]{3,1,2,0:T(1,128)S(1)} %get-tuple-element.44), channel_id=1, source_target_pairs={{0,2},{2,4},{4,6},{6,8},{8,10},{10,12},{12,14},{14,16},{16,18},{18... | collective-permute-start | bytes 196616 | tf_op jit(solution)/shard_map/ppermute | solution.py:24
  28.5 1.9 collective-permute-start.4
  30.4 1.5 fusion.86
  31.9 1.4 reduce_sum.46
  34.8 1.9 collective-permute-start.6
  38.0 2.0 copy.9
  40.0 2.2 %collective-permute-done.7 = f32[2,34,1,256]{3,1,2,0:T(8,128)} collective-permute-done((f32[2,34,1,256]{3,1,2,0:T(8,128)}, f32[2,34,1,256]{3,1,2,0:T(8,128)}, u32[]{:S(2)}, u32[]{:S(2)}) %collective-permute-start.7) | collective-permute-done | bytes 69664 | tf_op jit(solution)/shard_map/ppermute | solution.py:24
  42.2 4.9 %multiply_add_fusion.1 = (f32[2,32,32,256]{3,1,2,0:T(8,128)S(1)}, f32[2,32,32,256]{3,1,2,0:T(8,128)}) fusion(f32[2,32,32,256]{3,1,2,0:T(8,128)S(1)} %get-tuple-element.22, f32[2,32,32,256]{3,1,2,0:T(8,128)S(1)} %copy-done.6, f32[2,1,32,256]{3,1,2,0:T(1,128)S(1)} %collective-permute-done.4, f32[2,1,32,256]{3,1,2,0:T(1,128)S(1)} %collective-permute-done.5, ...), kind=kLoop, calls=%fused_computation.109 | loop fusion | flops 9961472 | bytes 9707520 | tf_op jit(solution)/shard_map/add | solution.py:82
  47.0 1.3 copy-done.2
  48.5 4.3 %collective-permute-start.9 = (f32[2,1,32,256]{3,1,2,0:T(1,128)S(1)}, f32[2,1,32,256]{3,1,2,0:T(1,128)S(1)}, u32[]{:S(2)}, u32[]{:S(2)}) collective-permute-start(f32[2,1,32,256]{3,1,2,0:T(1,128)S(1)} %get-tuple-element.42), channel_id=1, source_target_pairs={{0,2},{2,4},{4,6},{6,8},{8,10},{10,12},{12,14},{14,16},{16,18},{18... | collective-permute-start | bytes 196616 | tf_op jit(solution)/shard_map/ppermute | solution.py:24
  52.8 2.7 %collective-permute-start.8 = (f32[2,1,32,256]{3,1,2,0:T(1,128)S(1)}, f32[2,1,32,256]{3,1,2,0:T(1,128)S(1)}, u32[]{:S(2)}, u32[]{:S(2)}) collective-permute-start(f32[2,1,32,256]{3,1,2,0:T(1,128)S(1)} %get-tuple-element.43), channel_id=1, source_target_pairs={{2,0},{4,2},{6,4},{8,6},{10,8},{12,10},{14,12},{16,14},{18,16},{20... | collective-permute-start | bytes 196616 | tf_op jit(solution)/shard_map/ppermute | solution.py:26
  59.7 1.7 collective-permute-start.10
  61.4 1.5 collective-permute-start.11
  63.0 3.6 %collective-permute-done.11 = f32[2,34,1,256]{3,1,2,0:T(8,128)S(1)} collective-permute-done((f32[2,34,1,256]{3,1,2,0:T(8,128)S(1)}, f32[2,34,1,256]{3,1,2,0:T(8,128)S(1)}, u32[]{:S(2)}, u32[]{:S(2)}) %collective-permute-start.11) | collective-permute-done | bytes 69664 | tf_op jit(solution)/shard_map/ppermute | solution.py:24
  66.6 4.2 %fusion.11 = f32[2,32,32,256]{3,1,2,0:T(8,128)S(1)} fusion(f32[2,32,32,256]{3,1,2,0:T(8,128)} %get-tuple-element.21, f32[2,32,32,256]{3,1,2,0:T(8,128)S(1)} %copy-done.3, f32[2,34,1,256]{3,1,2,0:T(8,128)S(1)} %collective-permute-done.11, f32[2,1,32,256]{3,1,2,0:T(1,128)S(1)} %collective-permute-done.8, f32[2,1,32,256]{3,1,2,0:T(1,128)S(1)} %collective-permute-done.9, ...), kind=kLoop, calls=%fused_computation.23 | loop fusion | flops 8388608 | bytes 7610368 | tf_op jit(solution)/shard_map/sub | solution.py:84
  70.8 3.3 %fusion.45 = f32[2,32,32,128]{3,2,1,0:T(8,128)} fusion(f32[2,32,32,256]{3,1,2,0:T(8,128)S(1)} %fusion.11, s32[256]{0:T(256)S(1)} %and_select_fusion), kind=kOutput, calls=%fused_computation.105 | convolution fusion | flops 805339136 | bytes 3146752 | tf_op jit(solution)/shard_map/dot_general | solution.py:67
  74.1 2.0 reduce_sum.45
  76.2 7.3 %all_gather.3 = f32[3,16,32,128]{3,2,1,0:T(8,128)S(1)} all-gather(f32[3,16,16,128]{3,2,1,0:T(8,128)S(1)} %pad_maximum_fusion.48), channel_id=1, replica_groups=mesh['gx'=16,'gy'=2] {'gy'}, dimensions={2}, use_global_device_ids=true | all-gather | bytes 1179648 | tf_op jit(solution)/shard_map/all_gather | solution.py:104
  83.6 9.7 %collective-permute-start.12 = (f32[2,1,32,128]{3,2,1,0:T(8,128)S(1)}, f32[2,1,32,128]{3,2,1,0:T(8,128)S(1)}, u32[]{:S(2)}, u32[]{:S(2)}) collective-permute-start(f32[2,1,32,128]{3,2,1,0:T(8,128)S(1)} %get-tuple-element.60), channel_id=1, source_target_pairs={{0,2},{2,4},{4,6},{6,8},{8,10},{10,12},{12,14},{14,16},{16,18},{18... | collective-permute-start | bytes 98312 | tf_op jit(solution)/shard_map/ppermute | solution.py:24
  93.2 1.9 collective-permute-start.13
  95.2 3.3 %collective-permute-done.13 = f32[2,1,32,128]{3,2,1,0:T(8,128)S(1)} collective-permute-done((f32[2,1,32,128]{3,2,1,0:T(8,128)S(1)}, f32[2,1,32,128]{3,2,1,0:T(8,128)S(1)}, u32[]{:S(2)}, u32[]{:S(2)}) %collective-permute-start.13) | collective-permute-done | bytes 32800 | tf_op jit(solution)/shard_map/ppermute | solution.py:26
  99.1 1.9 collective-permute-start.14
  101.0 2.4 %collective-permute-start.15 = (f32[2,1,32,128]{3,2,1,0:T(8,128)S(1)}, f32[2,1,32,128]{3,2,1,0:T(8,128)S(1)}, u32[]{:S(2)}, u32[]{:S(2)}) collective-permute-start(f32[2,1,32,128]{3,2,1,0:T(8,128)S(1)} %get-tuple-element.59), channel_id=1, source_target_pairs={{2,0},{4,2},{6,4},{8,6},{10,8},{12,10},{14,12},{16,14},{18,16},{20... | collective-permute-start | bytes 98312 | tf_op jit(solution)/shard_map/ppermute | solution.py:26
  103.5 2.8 %collective-permute-done.15 = f32[2,1,32,128]{3,2,1,0:T(8,128)S(1)} collective-permute-done((f32[2,1,32,128]{3,2,1,0:T(8,128)S(1)}, f32[2,1,32,128]{3,2,1,0:T(8,128)S(1)}, u32[]{:S(2)}, u32[]{:S(2)}) %collective-permute-start.15) | collective-permute-done | bytes 32800 | tf_op jit(solution)/shard_map/ppermute | solution.py:26
  106.9 1.9 collective-permute-start.16
  108.8 2.4 %collective-permute-start.17 = (f32[2,1,32,128]{3,2,1,0:T(8,128)S(1)}, f32[2,1,32,128]{3,2,1,0:T(8,128)S(1)}, u32[]{:S(2)}, u32[]{:S(2)}) collective-permute-start(f32[2,1,32,128]{3,2,1,0:T(8,128)S(1)} %get-tuple-element.57), channel_id=1, source_target_pairs={{2,0},{4,2},{6,4},{8,6},{10,8},{12,10},{14,12},{16,14},{18,16},{20... | collective-permute-start | bytes 98312 | tf_op jit(solution)/shard_map/ppermute | solution.py:26
  111.2 3.0 %collective-permute-done.17 = f32[2,1,32,128]{3,2,1,0:T(8,128)S(1)} collective-permute-done((f32[2,1,32,128]{3,2,1,0:T(8,128)S(1)}, f32[2,1,32,128]{3,2,1,0:T(8,128)S(1)}, u32[]{:S(2)}, u32[]{:S(2)}) %collective-permute-start.17) | collective-permute-done | bytes 32800 | tf_op jit(solution)/shard_map/ppermute | solution.py:26
  116.4 1.9 collective-permute-start.18
  118.3 2.4 %collective-permute-start.19 = (f32[2,1,32,128]{3,2,1,0:T(8,128)S(1)}, f32[2,1,32,128]{3,2,1,0:T(8,128)S(1)}, u32[]{:S(2)}, u32[]{:S(2)}) collective-permute-start(f32[2,1,32,128]{3,2,1,0:T(8,128)S(1)} %get-tuple-element.55), channel_id=1, source_target_pairs={{2,0},{4,2},{6,4},{8,6},{10,8},{12,10},{14,12},{16,14},{18,16},{20... | collective-permute-start | bytes 98312 | tf_op jit(solution)/shard_map/ppermute | solution.py:26
  120.8 3.7 %collective-permute-done.19 = f32[2,1,32,128]{3,2,1,0:T(8,128)S(1)} collective-permute-done((f32[2,1,32,128]{3,2,1,0:T(8,128)S(1)}, f32[2,1,32,128]{3,2,1,0:T(8,128)S(1)}, u32[]{:S(2)}, u32[]{:S(2)}) %collective-permute-start.19) | collective-permute-done | bytes 32800 | tf_op jit(solution)/shard_map/ppermute | solution.py:26
  126.1 1.9 collective-permute-start.20
  128.0 2.6 %collective-permute-start.21 = (f32[2,1,32,128]{3,2,1,0:T(8,128)S(1)}, f32[2,1,32,128]{3,2,1,0:T(8,128)S(1)}, u32[]{:S(2)}, u32[]{:S(2)}) collective-permute-start(f32[2,1,32,128]{3,2,1,0:T(8,128)S(1)} %get-tuple-element.53), channel_id=1, source_target_pairs={{2,0},{4,2},{6,4},{8,6},{10,8},{12,10},{14,12},{16,14},{18,16},{20... | collective-permute-start | bytes 98312 | tf_op jit(solution)/shard_map/ppermute | solution.py:26
  130.7 3.5 %collective-permute-done.21 = f32[2,1,32,128]{3,2,1,0:T(8,128)S(1)} collective-permute-done((f32[2,1,32,128]{3,2,1,0:T(8,128)S(1)}, f32[2,1,32,128]{3,2,1,0:T(8,128)S(1)}, u32[]{:S(2)}, u32[]{:S(2)}) %collective-permute-start.21) | collective-permute-done | bytes 32800 | tf_op jit(solution)/shard_map/ppermute | solution.py:26
  136.4 1.4 broadcast_in_dim.44
  137.8 2.9 %reshape.62 = f32[2,32,16,256]{3,1,2,0:T(8,128)} reshape(f32[2,16,2,16,256]{4,2,1,3,0:T(2,128)} %broadcast_in_dim.44) | data formatting | bytes 2097152 | tf_op jit(solution)/shard_map/reshape | solution.py:120
  140.7 1.6 broadcast_in_dim.45
  142.6 3.5 %add_add_fusion = f32[2,32,32,256]{3,1,2,0:T(8,128)S(1)} fusion(f32[2,32,32,256]{3,1,2,0:T(8,128)S(1)} %bitcast.23, f32[2,32,32,256]{3,1,2,0:T(8,128)S(1)} %get-tuple-element.22, f32[2,32,32,256]{3,2,1,0:T(8,128)S(1)} %copy-done.1, f32[2,32,32,256]{3,1,2,0:T(8,128)} %get-tuple-element.21), kind=kLoop, calls=%fused_computation.108 | loop fusion | flops 3670016 | bytes 10485760 | tf_op jit(solution)/shard_map/add | solution.py:121
  146.3 1.9 collective-permute-start.23
  148.2 2.4 %collective-permute-start.22 = (f32[2,1,32,256]{3,1,2,0:T(1,128)S(1)}, f32[2,1,32,256]{3,1,2,0:T(1,128)S(1)}, u32[]{:S(2)}, u32[]{:S(2)}) collective-permute-start(f32[2,1,32,256]{3,1,2,0:T(1,128)S(1)} %get-tuple-element.41), channel_id=1, source_target_pairs={{2,0},{4,2},{6,4},{8,6},{10,8},{12,10},{14,12},{16,14},{18,16},{20... | collective-permute-start | bytes 196616 | tf_op jit(solution)/shard_map/ppermute | solution.py:26
  150.6 4.1 %collective-permute-done.22 = f32[2,1,32,256]{3,1,2,0:T(1,128)S(1)} collective-permute-done((f32[2,1,32,256]{3,1,2,0:T(1,128)S(1)}, f32[2,1,32,256]{3,1,2,0:T(1,128)S(1)}, u32[]{:S(2)}, u32[]{:S(2)}) %collective-permute-start.22) | collective-permute-done | bytes 65568 | tf_op jit(solution)/shard_map/ppermute | solution.py:26
  154.7 1.6 collective-permute-start.24
  158.3 3.8 %collective-permute-done.25 = f32[2,34,1,256]{3,1,2,0:T(8,128)S(1)} collective-permute-done((f32[2,34,1,256]{3,1,2,0:T(8,128)S(1)}, f32[2,34,1,256]{3,1,2,0:T(8,128)S(1)}, u32[]{:S(2)}, u32[]{:S(2)}) %collective-permute-start.25) | collective-permute-done | bytes 69664 | tf_op jit(solution)/shard_map/ppermute | solution.py:24
  162.1 4.3 %broadcast_multiply_fusion = (f32[2,32,32,256]{3,1,2,0:T(8,128)S(1)}, f32[2,32,32,256]{3,1,2,0:T(8,128)S(1)}) fusion(f32[2,32,32,256]{3,1,2,0:T(8,128)S(1)} %add_add_fusion, f32[2,1,32,256]{3,1,2,0:T(1,128)S(1)} %collective-permute-done.22, f32[2,1,32,256]{3,1,2,0:T(1,128)S(1)} %collective-permute-done.23, ...), kind=kLoop, calls=%fused_computation.122 | loop fusion | flops 8912896 | bytes 9707520 | tf_op jit(solution)/shard_map/mul | solution.py:125
  166.5 2.9 %collective-permute-start.27 = (f32[2,1,32,256]{3,1,2,0:T(1,128)S(1)}, f32[2,1,32,256]{3,1,2,0:T(1,128)S(1)}, u32[]{:S(2)}, u32[]{:S(2)}) collective-permute-start(f32[2,1,32,256]{3,1,2,0:T(1,128)S(1)} %get-tuple-element.38), channel_id=1, source_target_pairs={{0,2},{2,4},{4,6},{6,8},{8,10},{10,12},{12,14},{14,16},{16,18},{18... | collective-permute-start | bytes 196616 | tf_op jit(solution)/shard_map/ppermute | solution.py:24
  169.4 2.1 %collective-permute-start.26 = (f32[2,1,32,256]{3,1,2,0:T(1,128)S(1)}, f32[2,1,32,256]{3,1,2,0:T(1,128)S(1)}, u32[]{:S(2)}, u32[]{:S(2)}) collective-permute-start(f32[2,1,32,256]{3,1,2,0:T(1,128)S(1)} %get-tuple-element.39), channel_id=1, source_target_pairs={{2,0},{4,2},{6,4},{8,6},{10,8},{12,10},{14,12},{16,14},{18,16},{20... | collective-permute-start | bytes 196616 | tf_op jit(solution)/shard_map/ppermute | solution.py:26
  171.5 3.5 %collective-permute-done.26 = f32[2,1,32,256]{3,1,2,0:T(1,128)S(1)} collective-permute-done((f32[2,1,32,256]{3,1,2,0:T(1,128)S(1)}, f32[2,1,32,256]{3,1,2,0:T(1,128)S(1)}, u32[]{:S(2)}, u32[]{:S(2)}) %collective-permute-start.26) | collective-permute-done | bytes 65568 | tf_op jit(solution)/shard_map/ppermute | solution.py:26
  175.0 1.3 collective-permute-start.28
  177.7 3.7 %collective-permute-done.29 = f32[2,34,1,256]{3,1,2,0:T(8,128)S(1)} collective-permute-done((f32[2,34,1,256]{3,1,2,0:T(8,128)S(1)}, f32[2,34,1,256]{3,1,2,0:T(8,128)S(1)}, u32[]{:S(2)}, u32[]{:S(2)}) %collective-permute-start.29) | collective-permute-done | bytes 69664 | tf_op jit(solution)/shard_map/ppermute | solution.py:24
  181.5 3.0 %multiply_add_fusion = (f32[2,32,32,256]{3,1,2,0:T(8,128)S(1)}, f32[2,32,32,256]{3,1,2,0:T(8,128)S(1)}) fusion(f32[2,32,32,256]{3,1,2,0:T(8,128)S(1)} %get-tuple-element.11, f32[2,32,32,256]{3,1,2,0:T(8,128)S(1)} %get-tuple-element.10, f32[2,1,32,256]{3,1,2,0:T(1,128)S(1)} %collective-permute-done.26, f32[2,1,32,256]{3,1,2,0:T(1,128)S(1)} %collective-permute-done.27, ...), kind=kLoop, calls=%fused_computation.107 | loop fusion | flops 9961472 | bytes 9707520 | tf_op jit(solution)/shard_map/add | solution.py:125
  184.5 3.3 %collective-permute-start.31 = (f32[2,1,32,256]{3,1,2,0:T(1,128)S(1)}, f32[2,1,32,256]{3,1,2,0:T(1,128)S(1)}, u32[]{:S(2)}, u32[]{:S(2)}) collective-permute-start(f32[2,1,32,256]{3,1,2,0:T(1,128)S(1)} %get-tuple-element.36), channel_id=1, source_target_pairs={{0,2},{2,4},{4,6},{6,8},{8,10},{10,12},{12,14},{14,16},{16,18},{18... | collective-permute-start | bytes 196616 | tf_op jit(solution)/shard_map/ppermute | solution.py:24
  187.8 2.9 %collective-permute-start.30 = (f32[2,1,32,256]{3,1,2,0:T(1,128)S(1)}, f32[2,1,32,256]{3,1,2,0:T(1,128)S(1)}, u32[]{:S(2)}, u32[]{:S(2)}) collective-permute-start(f32[2,1,32,256]{3,1,2,0:T(1,128)S(1)} %get-tuple-element.37), channel_id=1, source_target_pairs={{2,0},{4,2},{6,4},{8,6},{10,8},{12,10},{14,12},{16,14},{18,16},{20... | collective-permute-start | bytes 196616 | tf_op jit(solution)/shard_map/ppermute | solution.py:26
  190.7 3.1 %collective-permute-done.30 = f32[2,1,32,256]{3,1,2,0:T(1,128)S(1)} collective-permute-done((f32[2,1,32,256]{3,1,2,0:T(1,128)S(1)}, f32[2,1,32,256]{3,1,2,0:T(1,128)S(1)}, u32[]{:S(2)}, u32[]{:S(2)}) %collective-permute-start.30) | collective-permute-done | bytes 65568 | tf_op jit(solution)/shard_map/ppermute | solution.py:26
  193.9 1.6 collective-permute-start.32
  196.9 3.7 %collective-permute-done.33 = f32[2,34,1,256]{3,1,2,0:T(8,128)S(1)} collective-permute-done((f32[2,34,1,256]{3,1,2,0:T(8,128)S(1)}, f32[2,34,1,256]{3,1,2,0:T(8,128)S(1)}, u32[]{:S(2)}, u32[]{:S(2)}) %collective-permute-start.33) | collective-permute-done | bytes 69664 | tf_op jit(solution)/shard_map/ppermute | solution.py:24
  200.6 3.3 %fusion.26 = f32[2,32,32,256]{3,1,2,0:T(8,128)S(1)} fusion(f32[2,32,32,256]{3,1,2,0:T(8,128)S(1)} %get-tuple-element.9, f32[2,32,32,256]{3,1,2,0:T(8,128)S(1)} %get-tuple-element.8, f32[2,34,1,256]{3,1,2,0:T(8,128)S(1)} %collective-permute-done.33, f32[2,1,32,256]{3,1,2,0:T(1,128)S(1)} %collective-permute-done.30, ...), kind=kLoop, calls=%fused_computation.38 | loop fusion | flops 12058624 | bytes 11804672 | tf_op jit(solution)/shard_map/add | solution.py:126
  204.0 2.5 %copy.13 = f32[2,32,32,256]{3,2,1,0:T(8,128)} copy(f32[2,32,32,256]{3,1,2,0:T(8,128)S(1)} %fusion.26) | data formatting | bytes 4194304 | tf_op jit(solution)/shard_map/add | solution.py:126
  (104 shorter events, 20.2 us)
Async XLA Ops:
  0.0 8.7 %copy-start.13 = (f32[32,32,256]{2,1,0:T(8,128)S(1)}, f32[32,32,256]{2,1,0:T(8,128)}, u32[]{:S(2)}) copy-start(f32[32,32,256]{2,1,0:T(8,128)} %param.4) | copy-start | bytes 3145732
  3.1 7.6 %collective-permute-start.1 = (f32[2,1,32,256]{3,1,2,0:T(1,128)S(1)}, f32[2,1,32,256]{3,1,2,0:T(1,128)S(1)}, u32[]{:S(2)}, u32[]{:S(2)}) collective-permute-start(f32[2,1,32,256]{3,1,2,0:T(1,128)S(1)} %get-tuple-element.46), channel_id=1, source_target_pairs={{0,2},{2,4},{4,6},{6,8},{8,10},{10,12},{12,14},{14,16},{16,18},{18... | collective-permute-start | bytes 196616 | tf_op jit(solution)/shard_map/ppermute | solution.py:24
  6.8 5.6 %collective-permute-start = (f32[2,1,32,256]{3,1,2,0:T(1,128)S(1)}, f32[2,1,32,256]{3,1,2,0:T(1,128)S(1)}, u32[]{:S(2)}, u32[]{:S(2)}) collective-permute-start(f32[2,1,32,256]{3,1,2,0:T(1,128)S(1)} %get-tuple-element.47), channel_id=1, source_target_pairs={{2,0},{4,2},{6,4},{8,6},{10,8},{12,10},{14,12},{16,14},{18,16},{20... | collective-permute-start | bytes 196616 | tf_op jit(solution)/shard_map/ppermute | solution.py:26
  10.1 10.2 %copy-start = (f32[2,32,32,256]{3,2,1,0:T(8,128)S(1)}, f32[2,32,32,256]{3,2,1,0:T(8,128)}, u32[]{:S(2)}) copy-start(f32[2,32,32,256]{3,2,1,0:T(8,128)} %param.3) | copy-start | bytes 6291460
  10.7 14.8 %copy-start.4 = (f32[32,32,256]{2,0,1:T(8,128)}, f32[32,32,256]{2,0,1:T(8,128)S(1)}, u32[]{:S(2)}) copy-start(f32[32,32,256]{2,0,1:T(8,128)S(1)} %copy.6) | copy-start | bytes 3145732
  12.4 4.1 %collective-permute-start.2 = (f32[2,34,1,256]{3,1,2,0:T(8,128)S(1)}, f32[2,34,1,256]{3,1,2,0:T(8,128)S(1)}, u32[]{:S(2)}, u32[]{:S(2)}) collective-permute-start(f32[2,34,1,256]{3,1,2,0:T(8,128)S(1)} %get-tuple-element.34), channel_id=1, source_target_pairs={{1,0},{3,2},{5,4},{7,6},{9,8},{11,10},{13,12},{15,14},{17,16},{19,... | collective-permute-start | bytes 208904 | tf_op jit(solution)/shard_map/ppermute | solution.py:26
  14.5 5.8 %collective-permute-start.3 = (f32[2,34,1,256]{3,1,2,0:T(8,128)S(1)}, f32[2,34,1,256]{3,1,2,0:T(8,128)S(1)}, u32[]{:S(2)}, u32[]{:S(2)}) collective-permute-start(f32[2,34,1,256]{3,1,2,0:T(8,128)S(1)} %get-tuple-element.35), channel_id=1, source_target_pairs={{0,1},{2,3},{4,5},{6,7},{8,9},{10,11},{12,13},{14,15},{16,17},{18,... | collective-permute-start | bytes 208904 | tf_op jit(solution)/shard_map/ppermute | solution.py:24
  25.6 7.7 %collective-permute-start.5 = (f32[2,1,32,256]{3,1,2,0:T(1,128)S(1)}, f32[2,1,32,256]{3,1,2,0:T(1,128)S(1)}, u32[]{:S(2)}, u32[]{:S(2)}) collective-permute-start(f32[2,1,32,256]{3,1,2,0:T(1,128)S(1)} %get-tuple-element.44), channel_id=1, source_target_pairs={{0,2},{2,4},{4,6},{6,8},{8,10},{10,12},{12,14},{14,16},{16,18},{18... | collective-permute-start | bytes 196616 | tf_op jit(solution)/shard_map/ppermute | solution.py:24
  28.5 5.6 %collective-permute-start.4 = (f32[2,1,32,256]{3,1,2,0:T(1,128)S(1)}, f32[2,1,32,256]{3,1,2,0:T(1,128)S(1)}, u32[]{:S(2)}, u32[]{:S(2)}) collective-permute-start(f32[2,1,32,256]{3,1,2,0:T(1,128)S(1)} %get-tuple-element.45), channel_id=1, source_target_pairs={{2,0},{4,2},{6,4},{8,6},{10,8},{12,10},{14,12},{16,14},{18,16},{20... | collective-permute-start | bytes 196616 | tf_op jit(solution)/shard_map/ppermute | solution.py:26
  34.8 5.2 %collective-permute-start.6 = (f32[2,34,1,256]{3,1,2,0:T(8,128)}, f32[2,34,1,256]{3,1,2,0:T(8,128)}, u32[]{:S(2)}, u32[]{:S(2)}) collective-permute-start(f32[2,34,1,256]{3,1,2,0:T(8,128)} %get-tuple-element.32), channel_id=1, source_target_pairs={{1,0},{3,2},{5,4},{7,6},{9,8},{11,10},{13,12},{15,14},{17,16},{19,... | collective-permute-start | bytes 208904 | tf_op jit(solution)/shard_map/ppermute | solution.py:26
  36.7 5.5 %collective-permute-start.7 = (f32[2,34,1,256]{3,1,2,0:T(8,128)}, f32[2,34,1,256]{3,1,2,0:T(8,128)}, u32[]{:S(2)}, u32[]{:S(2)}) collective-permute-start(f32[2,34,1,256]{3,1,2,0:T(8,128)} %get-tuple-element.33), channel_id=1, source_target_pairs={{0,1},{2,3},{4,5},{6,7},{8,9},{10,11},{12,13},{14,15},{16,17},{18,... | collective-permute-start | bytes 208904 | tf_op jit(solution)/shard_map/ppermute | solution.py:24
  38.0 4.2 %copy-start.6 = (f32[2,32,32,256]{3,1,2,0:T(8,128)S(1)}, f32[2,32,32,256]{3,1,2,0:T(8,128)}, u32[]{:S(2)}) copy-start(f32[2,32,32,256]{3,1,2,0:T(8,128)} %get-tuple-element.23) | copy-start | bytes 6291460
  42.2 13.4 %copy-start.17 = (s32[16]{0:T(128)S(1)}, s32[16]{0:T(128)}, u32[]{:S(2)}) copy-start(s32[16]{0:T(128)} %param.5) | copy-start | bytes 196
  47.0 1.3 copy-start.2
  48.5 10.2 %collective-permute-start.9 = (f32[2,1,32,256]{3,1,2,0:T(1,128)S(1)}, f32[2,1,32,256]{3,1,2,0:T(1,128)S(1)}, u32[]{:S(2)}, u32[]{:S(2)}) collective-permute-start(f32[2,1,32,256]{3,1,2,0:T(1,128)S(1)} %get-tuple-element.42), channel_id=1, source_target_pairs={{0,2},{2,4},{4,6},{6,8},{8,10},{10,12},{12,14},{14,16},{16,18},{18... | collective-permute-start | bytes 196616 | tf_op jit(solution)/shard_map/ppermute | solution.py:24
  52.8 5.9 %collective-permute-start.8 = (f32[2,1,32,256]{3,1,2,0:T(1,128)S(1)}, f32[2,1,32,256]{3,1,2,0:T(1,128)S(1)}, u32[]{:S(2)}, u32[]{:S(2)}) collective-permute-start(f32[2,1,32,256]{3,1,2,0:T(1,128)S(1)} %get-tuple-element.43), channel_id=1, source_target_pairs={{2,0},{4,2},{6,4},{8,6},{10,8},{12,10},{14,12},{16,14},{18,16},{20... | collective-permute-start | bytes 196616 | tf_op jit(solution)/shard_map/ppermute | solution.py:26
  58.7 8.0 %copy-start.3 = (f32[2,32,32,256]{3,1,2,0:T(8,128)S(1)}, f32[2,32,32,256]{3,1,2,0:T(8,128)}, u32[]{:S(2)}) copy-start(f32[2,32,32,256]{3,1,2,0:T(8,128)} %copy-done.2) | copy-start | bytes 6291460
  59.7 3.3 %collective-permute-start.10 = (f32[2,34,1,256]{3,1,2,0:T(8,128)S(1)}, f32[2,34,1,256]{3,1,2,0:T(8,128)S(1)}, u32[]{:S(2)}, u32[]{:S(2)}) collective-permute-start(f32[2,34,1,256]{3,1,2,0:T(8,128)S(1)} %get-tuple-element.30), channel_id=1, source_target_pairs={{1,0},{3,2},{5,4},{7,6},{9,8},{11,10},{13,12},{15,14},{17,16},{19,... | collective-permute-start | bytes 208904 | tf_op jit(solution)/shard_map/ppermute | solution.py:26
  61.4 5.2 %collective-permute-start.11 = (f32[2,34,1,256]{3,1,2,0:T(8,128)S(1)}, f32[2,34,1,256]{3,1,2,0:T(8,128)S(1)}, u32[]{:S(2)}, u32[]{:S(2)}) collective-permute-start(f32[2,34,1,256]{3,1,2,0:T(8,128)S(1)} %get-tuple-element.31), channel_id=1, source_target_pairs={{0,1},{2,3},{4,5},{6,7},{8,9},{10,11},{12,13},{14,15},{16,17},{18,... | collective-permute-start | bytes 208904 | tf_op jit(solution)/shard_map/ppermute | solution.py:24
  83.6 15.0 %copy-start.14 = (f32[2,16,32,128]{3,2,1,0:T(8,128)}, f32[2,16,32,128]{3,2,1,0:T(8,128)S(1)}, u32[]{:S(2)}) copy-start(f32[2,16,32,128]{3,2,1,0:T(8,128)S(1)} %slice_multiply_fusion) | copy-start | bytes 1572868
  83.6 11.6 %collective-permute-start.12 = (f32[2,1,32,128]{3,2,1,0:T(8,128)S(1)}, f32[2,1,32,128]{3,2,1,0:T(8,128)S(1)}, u32[]{:S(2)}, u32[]{:S(2)}) collective-permute-start(f32[2,1,32,128]{3,2,1,0:T(8,128)S(1)} %get-tuple-element.60), channel_id=1, source_target_pairs={{0,2},{2,4},{4,6},{6,8},{8,10},{10,12},{12,14},{14,16},{16,18},{18... | collective-permute-start | bytes 98312 | tf_op jit(solution)/shard_map/ppermute | solution.py:24
  93.2 5.2 %collective-permute-start.13 = (f32[2,1,32,128]{3,2,1,0:T(8,128)S(1)}, f32[2,1,32,128]{3,2,1,0:T(8,128)S(1)}, u32[]{:S(2)}, u32[]{:S(2)}) collective-permute-start(f32[2,1,32,128]{3,2,1,0:T(8,128)S(1)} %get-tuple-element.61), channel_id=1, source_target_pairs={{2,0},{4,2},{6,4},{8,6},{10,8},{12,10},{14,12},{16,14},{18,16},{20... | collective-permute-start | bytes 98312 | tf_op jit(solution)/shard_map/ppermute | solution.py:26
  99.1 7.8 %copy-start.7 = (f32[2,16,32,128]{3,2,1,0:T(8,128)}, f32[2,16,32,128]{3,2,1,0:T(8,128)S(1)}, u32[]{:S(2)}) copy-start(f32[2,16,32,128]{3,2,1,0:T(8,128)S(1)} %get-tuple-element.18) | copy-start | bytes 1572868
  99.1 4.3 %collective-permute-start.14 = (f32[2,1,32,128]{3,2,1,0:T(8,128)S(1)}, f32[2,1,32,128]{3,2,1,0:T(8,128)S(1)}, u32[]{:S(2)}, u32[]{:S(2)}) collective-permute-start(f32[2,1,32,128]{3,2,1,0:T(8,128)S(1)} %get-tuple-element.58), channel_id=1, source_target_pairs={{0,2},{2,4},{4,6},{6,8},{8,10},{10,12},{12,14},{14,16},{16,18},{18... | collective-permute-start | bytes 98312 | tf_op jit(solution)/shard_map/ppermute | solution.py:24
  101.0 5.2 %collective-permute-start.15 = (f32[2,1,32,128]{3,2,1,0:T(8,128)S(1)}, f32[2,1,32,128]{3,2,1,0:T(8,128)S(1)}, u32[]{:S(2)}, u32[]{:S(2)}) collective-permute-start(f32[2,1,32,128]{3,2,1,0:T(8,128)S(1)} %get-tuple-element.59), channel_id=1, source_target_pairs={{2,0},{4,2},{6,4},{8,6},{10,8},{12,10},{14,12},{16,14},{18,16},{20... | collective-permute-start | bytes 98312 | tf_op jit(solution)/shard_map/ppermute | solution.py:26
  106.9 8.7 %copy-start.9 = (f32[2,16,32,128]{3,2,1,0:T(8,128)}, f32[2,16,32,128]{3,2,1,0:T(8,128)S(1)}, u32[]{:S(2)}) copy-start(f32[2,16,32,128]{3,2,1,0:T(8,128)S(1)} %get-tuple-element.16) | copy-start | bytes 1572868
  106.9 4.3 %collective-permute-start.16 = (f32[2,1,32,128]{3,2,1,0:T(8,128)S(1)}, f32[2,1,32,128]{3,2,1,0:T(8,128)S(1)}, u32[]{:S(2)}, u32[]{:S(2)}) collective-permute-start(f32[2,1,32,128]{3,2,1,0:T(8,128)S(1)} %get-tuple-element.56), channel_id=1, source_target_pairs={{0,2},{2,4},{4,6},{6,8},{8,10},{10,12},{12,14},{14,16},{16,18},{18... | collective-permute-start | bytes 98312 | tf_op jit(solution)/shard_map/ppermute | solution.py:24
  108.8 5.4 %collective-permute-start.17 = (f32[2,1,32,128]{3,2,1,0:T(8,128)S(1)}, f32[2,1,32,128]{3,2,1,0:T(8,128)S(1)}, u32[]{:S(2)}, u32[]{:S(2)}) collective-permute-start(f32[2,1,32,128]{3,2,1,0:T(8,128)S(1)} %get-tuple-element.57), channel_id=1, source_target_pairs={{2,0},{4,2},{6,4},{8,6},{10,8},{12,10},{14,12},{16,14},{18,16},{20... | collective-permute-start | bytes 98312 | tf_op jit(solution)/shard_map/ppermute | solution.py:26
  115.6 0.8 copy-start.11
  116.4 4.4 %collective-permute-start.18 = (f32[2,1,32,128]{3,2,1,0:T(8,128)S(1)}, f32[2,1,32,128]{3,2,1,0:T(8,128)S(1)}, u32[]{:S(2)}, u32[]{:S(2)}) collective-permute-start(f32[2,1,32,128]{3,2,1,0:T(8,128)S(1)} %get-tuple-element.54), channel_id=1, source_target_pairs={{0,2},{2,4},{4,6},{6,8},{8,10},{10,12},{12,14},{14,16},{16,18},{18... | collective-permute-start | bytes 98312 | tf_op jit(solution)/shard_map/ppermute | solution.py:24
  118.3 6.1 %collective-permute-start.19 = (f32[2,1,32,128]{3,2,1,0:T(8,128)S(1)}, f32[2,1,32,128]{3,2,1,0:T(8,128)S(1)}, u32[]{:S(2)}, u32[]{:S(2)}) collective-permute-start(f32[2,1,32,128]{3,2,1,0:T(8,128)S(1)} %get-tuple-element.55), channel_id=1, source_target_pairs={{2,0},{4,2},{6,4},{8,6},{10,8},{12,10},{14,12},{16,14},{18,16},{20... | collective-permute-start | bytes 98312 | tf_op jit(solution)/shard_map/ppermute | solution.py:26
  120.7 4.9 %copy-start.12 = (f32[2,16,32,128]{3,2,1,0:T(8,128)S(1)}, f32[2,16,32,128]{3,2,1,0:T(8,128)}, u32[]{:S(2)}) copy-start(f32[2,16,32,128]{3,2,1,0:T(8,128)} %copy-done.11) | copy-start | bytes 1572868
  120.7 4.9 %copy-start.16 = (f32[2,16,32,128]{3,2,1,0:T(8,128)S(1)}, f32[2,16,32,128]{3,2,1,0:T(8,128)}, u32[]{:S(2)}) copy-start(f32[2,16,32,128]{3,2,1,0:T(8,128)} %get-tuple-element.15) | copy-start | bytes 1572868
  126.1 4.6 %collective-permute-start.20 = (f32[2,1,32,128]{3,2,1,0:T(8,128)S(1)}, f32[2,1,32,128]{3,2,1,0:T(8,128)S(1)}, u32[]{:S(2)}, u32[]{:S(2)}) collective-permute-start(f32[2,1,32,128]{3,2,1,0:T(8,128)S(1)} %get-tuple-element.52), channel_id=1, source_target_pairs={{0,2},{2,4},{4,6},{6,8},{8,10},{10,12},{12,14},{14,16},{16,18},{18... | collective-permute-start | bytes 98312 | tf_op jit(solution)/shard_map/ppermute | solution.py:24
  128.0 6.1 %collective-permute-start.21 = (f32[2,1,32,128]{3,2,1,0:T(8,128)S(1)}, f32[2,1,32,128]{3,2,1,0:T(8,128)S(1)}, u32[]{:S(2)}, u32[]{:S(2)}) collective-permute-start(f32[2,1,32,128]{3,2,1,0:T(8,128)S(1)} %get-tuple-element.53), channel_id=1, source_target_pairs={{2,0},{4,2},{6,4},{8,6},{10,8},{12,10},{14,12},{16,14},{18,16},{20... | collective-permute-start | bytes 98312 | tf_op jit(solution)/shard_map/ppermute | solution.py:26
  134.3 1.0 copy-start.8
  134.3 1.2 copy-start.10
  134.3 1.3 copy-start.15
  140.7 1.9 copy-start.1
  146.3 4.3 %collective-permute-start.23 = (f32[2,1,32,256]{3,1,2,0:T(1,128)S(1)}, f32[2,1,32,256]{3,1,2,0:T(1,128)S(1)}, u32[]{:S(2)}, u32[]{:S(2)}) collective-permute-start(f32[2,1,32,256]{3,1,2,0:T(1,128)S(1)} %get-tuple-element.40), channel_id=1, source_target_pairs={{0,2},{2,4},{4,6},{6,8},{8,10},{10,12},{12,14},{14,16},{16,18},{18... | collective-permute-start | bytes 196616 | tf_op jit(solution)/shard_map/ppermute | solution.py:24
  148.2 6.5 %collective-permute-start.22 = (f32[2,1,32,256]{3,1,2,0:T(1,128)S(1)}, f32[2,1,32,256]{3,1,2,0:T(1,128)S(1)}, u32[]{:S(2)}, u32[]{:S(2)}) collective-permute-start(f32[2,1,32,256]{3,1,2,0:T(1,128)S(1)} %get-tuple-element.41), channel_id=1, source_target_pairs={{2,0},{4,2},{6,4},{8,6},{10,8},{12,10},{14,12},{16,14},{18,16},{20... | collective-permute-start | bytes 196616 | tf_op jit(solution)/shard_map/ppermute | solution.py:26
  154.7 3.6 %collective-permute-start.24 = (f32[2,34,1,256]{3,1,2,0:T(8,128)S(1)}, f32[2,34,1,256]{3,1,2,0:T(8,128)S(1)}, u32[]{:S(2)}, u32[]{:S(2)}) collective-permute-start(f32[2,34,1,256]{3,1,2,0:T(8,128)S(1)} %get-tuple-element.28), channel_id=1, source_target_pairs={{1,0},{3,2},{5,4},{7,6},{9,8},{11,10},{13,12},{15,14},{17,16},{19,... | collective-permute-start | bytes 208904 | tf_op jit(solution)/shard_map/ppermute | solution.py:26
  156.3 5.8 %collective-permute-start.25 = (f32[2,34,1,256]{3,1,2,0:T(8,128)S(1)}, f32[2,34,1,256]{3,1,2,0:T(8,128)S(1)}, u32[]{:S(2)}, u32[]{:S(2)}) collective-permute-start(f32[2,34,1,256]{3,1,2,0:T(8,128)S(1)} %get-tuple-element.29), channel_id=1, source_target_pairs={{0,1},{2,3},{4,5},{6,7},{8,9},{10,11},{12,13},{14,15},{16,17},{18,... | collective-permute-start | bytes 208904 | tf_op jit(solution)/shard_map/ppermute | solution.py:24
  166.4 15.1 %copy-start.5 = (f32[32,32,256]{2,0,1:T(8,128)S(1)}, f32[32,32,256]{2,0,1:T(8,128)}, u32[]{:S(2)}) copy-start(f32[32,32,256]{2,0,1:T(8,128)} %copy-done.4) | copy-start | bytes 3145732
  166.5 5.0 %collective-permute-start.27 = (f32[2,1,32,256]{3,1,2,0:T(1,128)S(1)}, f32[2,1,32,256]{3,1,2,0:T(1,128)S(1)}, u32[]{:S(2)}, u32[]{:S(2)}) collective-permute-start(f32[2,1,32,256]{3,1,2,0:T(1,128)S(1)} %get-tuple-element.38), channel_id=1, source_target_pairs={{0,2},{2,4},{4,6},{6,8},{8,10},{10,12},{12,14},{14,16},{16,18},{18... | collective-permute-start | bytes 196616 | tf_op jit(solution)/shard_map/ppermute | solution.py:24
  169.4 5.6 %collective-permute-start.26 = (f32[2,1,32,256]{3,1,2,0:T(1,128)S(1)}, f32[2,1,32,256]{3,1,2,0:T(1,128)S(1)}, u32[]{:S(2)}, u32[]{:S(2)}) collective-permute-start(f32[2,1,32,256]{3,1,2,0:T(1,128)S(1)} %get-tuple-element.39), channel_id=1, source_target_pairs={{2,0},{4,2},{6,4},{8,6},{10,8},{12,10},{14,12},{16,14},{18,16},{20... | collective-permute-start | bytes 196616 | tf_op jit(solution)/shard_map/ppermute | solution.py:26
  175.0 2.8 %collective-permute-start.28 = (f32[2,34,1,256]{3,1,2,0:T(8,128)S(1)}, f32[2,34,1,256]{3,1,2,0:T(8,128)S(1)}, u32[]{:S(2)}, u32[]{:S(2)}) collective-permute-start(f32[2,34,1,256]{3,1,2,0:T(8,128)S(1)} %get-tuple-element.26), channel_id=1, source_target_pairs={{1,0},{3,2},{5,4},{7,6},{9,8},{11,10},{13,12},{15,14},{17,16},{19,... | collective-permute-start | bytes 208904 | tf_op jit(solution)/shard_map/ppermute | solution.py:26
  176.3 5.2 %collective-permute-start.29 = (f32[2,34,1,256]{3,1,2,0:T(8,128)S(1)}, f32[2,34,1,256]{3,1,2,0:T(8,128)S(1)}, u32[]{:S(2)}, u32[]{:S(2)}) collective-permute-start(f32[2,34,1,256]{3,1,2,0:T(8,128)S(1)} %get-tuple-element.27), channel_id=1, source_target_pairs={{0,1},{2,3},{4,5},{6,7},{8,9},{10,11},{12,13},{14,15},{16,17},{18,... | collective-permute-start | bytes 208904 | tf_op jit(solution)/shard_map/ppermute | solution.py:24
  184.5 6.2 %collective-permute-start.31 = (f32[2,1,32,256]{3,1,2,0:T(1,128)S(1)}, f32[2,1,32,256]{3,1,2,0:T(1,128)S(1)}, u32[]{:S(2)}, u32[]{:S(2)}) collective-permute-start(f32[2,1,32,256]{3,1,2,0:T(1,128)S(1)} %get-tuple-element.36), channel_id=1, source_target_pairs={{0,2},{2,4},{4,6},{6,8},{8,10},{10,12},{12,14},{14,16},{16,18},{18... | collective-permute-start | bytes 196616 | tf_op jit(solution)/shard_map/ppermute | solution.py:24
  187.8 6.0 %collective-permute-start.30 = (f32[2,1,32,256]{3,1,2,0:T(1,128)S(1)}, f32[2,1,32,256]{3,1,2,0:T(1,128)S(1)}, u32[]{:S(2)}, u32[]{:S(2)}) collective-permute-start(f32[2,1,32,256]{3,1,2,0:T(1,128)S(1)} %get-tuple-element.37), channel_id=1, source_target_pairs={{2,0},{4,2},{6,4},{8,6},{10,8},{12,10},{14,12},{16,14},{18,16},{20... | collective-permute-start | bytes 196616 | tf_op jit(solution)/shard_map/ppermute | solution.py:26
  193.9 3.0 %collective-permute-start.32 = (f32[2,34,1,256]{3,1,2,0:T(8,128)S(1)}, f32[2,34,1,256]{3,1,2,0:T(8,128)S(1)}, u32[]{:S(2)}, u32[]{:S(2)}) collective-permute-start(f32[2,34,1,256]{3,1,2,0:T(8,128)S(1)} %get-tuple-element.24), channel_id=1, source_target_pairs={{1,0},{3,2},{5,4},{7,6},{9,8},{11,10},{13,12},{15,14},{17,16},{19,... | collective-permute-start | bytes 208904 | tf_op jit(solution)/shard_map/ppermute | solution.py:26
  195.5 5.2 %collective-permute-start.33 = (f32[2,34,1,256]{3,1,2,0:T(8,128)S(1)}, f32[2,34,1,256]{3,1,2,0:T(8,128)S(1)}, u32[]{:S(2)}, u32[]{:S(2)}) collective-permute-start(f32[2,34,1,256]{3,1,2,0:T(8,128)S(1)} %get-tuple-element.25), channel_id=1, source_target_pairs={{0,1},{2,3},{4,5},{6,7},{8,9},{10,11},{12,13},{14,15},{16,17},{18,... | collective-permute-start | bytes 208904 | tf_op jit(solution)/shard_map/ppermute | solution.py:24
where the time goes:
time: 210 us; the launch traced here: 206 us
  starting transfers between devices  80.2 us (38%)
  waiting for transfers between devices  51.7 us (25%)
  other arithmetic  43.6 us (21%)
  local copies, waits for them, and re-layouts  15.3 us (7%)
  blocking collectives  7.3 us (3%)
  matrix products  5.16 us (2%)
  between operations  3.25 us (2%)
    ppermute x17, starting transfers between devices, with_halo(): lax.ppermute(tail, axis, [(i, (i + 1) % count) for i in range(ends)])  44.2 us
    ppermute x17, starting transfers between devices, with_halo(): lax.ppermute(head, axis, [((i + 1) % count, i) for i in range(ends)])  36 us
    ppermute x17, waiting for transfers between devices, with_halo(): lax.ppermute(head, axis, [((i + 1) % count, i) for i in range(ends)])  30.9 us
    ppermute x17, waiting for transfers between devices, with_halo(): lax.ppermute(tail, axis, [(i, (i + 1) % count) for i in range(ends)])  20.8 us
    add x3, other arithmetic, on_device(): update = scale_old * update + scale_res * residual  13 us
    all_gather x1, blocking collectives, on_device(): slab = lax.all_gather(coarse_stack, 'gy', axis=2, tiled=True)  7.3 us
    mul x2, other arithmetic, on_device(): update = scale_old * update + scale_res * residual  7.27 us
    dot_general x3, matrix products, pair_along_depth(): jnp.dot(field, pairing, precision=lax.Precision.HIGHEST, preferred_elemen...  5.16 us
  transfers between devices with their start and end apart: 34, of which 20 were waited for; matrix products, arithmetic and copies ran while one was open for 4% of the time, Pallas kernels for 0%

commit v1 on v0

v1 whole, which is shorter than its diff:
```python
import functools

import jax
import jax.numpy as jnp
from jax import lax
from jax.experimental import pallas as pl
from jax.experimental.pallas import tpu as pltpu
from jax.sharding import PartitionSpec as P

DEGREE = 3
COARSE_DEG = 6


FINE_LOWER = 3.0
FINE_UPPER = 12.4
COARSE_LOWER = 0.5
COARSE_UPPER = 13.4

LANES = 128
REACH = 7
F32 = jnp.float32


def cheb_pairs(lower, upper, count):
    middle = (upper + lower) / 2.0
    halfwidth = (upper - lower) / 2.0
    ratio_mid = middle / halfwidth
    rho_old = 1.0 / ratio_mid
    result = [(0.0, 1.0 / middle)]
    for repeat in range(count - 1):
        rho_new = 1.0 / (2.0 * ratio_mid - rho_old)
        result.append((rho_new * rho_old, 2.0 * rho_new / halfwidth))
        rho_old = rho_new
    return result


FINE = cheb_pairs(FINE_LOWER, FINE_UPPER, DEGREE)
COARSE = cheb_pairs(COARSE_LOWER, COARSE_UPPER, COARSE_DEG)


class Sizes:
    def __init__(self, nx, ny, nz, n_gy):
        assert nz == 2 * LANES and n_gy >= 2 and ny % 16 == 0 and nx % 4 == 0
        self.nx, self.ny, self.nz = nx, ny, nz
        self.two = n_gy == 2
        self.sides = 1 if self.two else 2
        self.wy = ny + 8 * self.sides
        self.cx, self.cy = nx // 2, ny // 2
        self.wc = self.cy + 8 * self.sides
        self.xmsg = 3 * REACH * self.cy + 8 * ny
        self.ymsg = 3 * self.cx * 8 + 8 * nx
        self.cmsg = 3 * REACH * 8 + 8


S_PAR, S_YOFF, S_HASL, S_HASR, S_LINKL, S_LINKR, S_RLO, S_RHI, S_HI0, S_HI1 = range(10)


def rows(start, size):
    return pl.ds(pl.multiple_of(start, 8), size)


def lane_masks(height):
    lane = lax.broadcasted_iota(jnp.int32, (height, LANES), 1)
    return lane == 0, lane == LANES - 1


def y_sum(v):
    return pltpu.roll(v, 1, 0) + pltpu.roll(v, v.shape[0] - 1, 0)


def z_sum(v0, v1, masks):
    first, last = masks
    l0, l1 = pltpu.roll(v0, 1, 1), pltpu.roll(v1, 1, 1)
    r0, r1 = pltpu.roll(v0, LANES - 1, 1), pltpu.roll(v1, LANES - 1, 1)
    return (
        jnp.where(first, 0.0, l0) + jnp.where(last, r1, r0),
        jnp.where(first, l0, l1) + jnp.where(last, 0.0, r1),
    )


def row_mask(height, low, high):
    row = lax.broadcasted_iota(jnp.int32, (height, LANES), 0)
    return (row >= low) & (row < high)


def fine_operator(ref, probe, plane, diag, wy, masks):
    v = [ref[probe, h, rows(plane * wy, wy), :] for h in range(2)]
    z = z_sum(v[0], v[1], masks)
    res = []
    for h in range(2):
        x = ref[probe, h, rows((plane - 1) * wy, wy), :] + ref[probe, h, rows((plane + 1) * wy, wy), :]
        res.append(diag[h] * v[h] - ((x + y_sum(v[h])) + z[h]))
    return v, res


def edge(high, size, count):
    return jnp.where(high, size - count, 0)


def pre_kernel(sz, *refs):
    n = sz.sides
    sc, rhs, diag, xa, xb = refs[:5]
    ys = refs[5 : 5 + n]
    cas = refs[5 + n : 5 + 2 * n]
    cbs = refs[5 + 2 * n : 5 + 3 * n]
    r_out, sol_out, dw, coarse, m_a, m_b = refs[5 + 3 * n : 11 + 3 * n]
    m_ys = refs[11 + 3 * n : 11 + 4 * n]
    m_cas = refs[11 + 4 * n : 11 + 5 * n]
    m_cbs = refs[11 + 5 * n : 11 + 6 * n]
    bw, r1, u2, u3, xs, ysm = refs[11 + 6 * n :]
    nx, ny, wy, cx, cy = sz.nx, sz.ny, sz.wy, sz.cx, sz.cy
    par_even = sc[S_PAR] == 0
    yoff = pl.multiple_of(sc[S_YOFF], 8)
    has_l, has_r = sc[S_HASL] == 1, sc[S_HASR] == 1
    his = [sc[S_HI0], sc[S_HI1]]
    half = [slice(0, LANES), slice(LANES, 2 * LANES)]
    masks = lane_masks(wy)

    zero8 = jnp.zeros((8, LANES), F32)
    zero_at = [jnp.where(sc[S_YOFF] == 0, ny, 0)] if sz.two else [0, ny + 8]

    def own(p, _):
        for h in range(2):
            for probe in range(2):
                bw[probe, h, rows((p + 3) * wy + yoff, ny), :] = rhs[probe, p, :, half[h]]
                for z in zero_at:
                    bw[probe, h, rows((p + 3) * wy + z, 8), :] = zero8
            dw[h, rows((p + 2) * wy + yoff, ny), :] = 6.0 + diag[p, :, half[h]]
            for z in zero_at:
                dw[h, rows((p + 2) * wy + z, 8), :] = zero8
        return 0

    lax.fori_loop(0, nx, own, 0)
    for msg, corners, to_right in ((xa, cas, par_even), (xb, cbs, jnp.logical_not(par_even))):
        b0 = jnp.where(to_right, nx + 3, 0)
        d0 = jnp.where(to_right, nx + 2, 0)
        for h in range(2):
            for k in range(3):
                for probe in range(2):
                    bw[probe, h, rows((b0 + k) * wy + yoff, ny), :] = msg[probe * 3 + k, :, half[h]]
                    for z in zero_at:
                        bw[probe, h, rows((b0 + k) * wy + z, 8), :] = zero8
            for k in range(2):
                dw[h, rows((d0 + k) * wy + yoff, ny), :] = 6.0 + msg[6 + k, :, half[h]]
                for z in zero_at:
                    dw[h, rows((d0 + k) * wy + z, 8), :] = zero8
        for s in range(n):
            bp = jnp.where(to_right, nx + 3, 1)
            dp = jnp.where(to_right, nx + 2, 1)
            br = jnp.where(his[s] == 1, ny, -2) + yoff
            dr = jnp.where(his[s] == 1, ny, -1) + yoff
            for h in range(2):
                for probe in range(2):
                    for k in range(2):
                        for r in range(2):
                            i = probe * 4 + k * 2 + r
                            bw[probe, h, pl.ds((bp + k) * wy + br + r, 1), :] = corners[s][i : i + 1, half[h]]
                dw[h, pl.ds(dp * wy + dr, 1), :] = 6.0 + corners[s][8:9, half[h]]
    for s in range(n):
        br = jnp.where(his[s] == 1, ny, -3) + yoff
        dr = jnp.where(his[s] == 1, ny, -2) + yoff
        for h in range(2):
            for k in range(3):
                for probe in range(2):
                    bw[probe, h, pl.ds(3 * wy + br + k, nx, stride=wy), :] = ys[s][probe * 3 + k, :, half[h]]
            for k in range(2):
                dw[h, pl.ds(2 * wy + dr + k, nx, stride=wy), :] = 6.0 + ys[s][6 + k, :, half[h]]
    zero = jnp.zeros((wy, LANES), F32)
    for probe in range(2):
        for h in range(2):
            for i in (1, nx + 2):
                u2[probe, h, rows(i * wy, wy), :] = zero
                u3[probe, h, rows(i * wy, wy), :] = zero

    inside = row_mask(wy, sc[S_RLO], sc[S_RHI])
    c0, (a1, c1), (a2, c2) = FINE[0][1], FINE[1], FINE[2]
    c1 = jnp.where(inside, c1, 0.0)
    c2 = jnp.where(inside, c2, 0.0)

    def step1(p):
        at = rows((p + 2) * wy, wy)
        d = [dw[h, at, :] for h in range(2)]
        for probe in range(2):
            v, av = fine_operator(bw, probe, p + 3, d, wy, masks)
            for h in range(2):
                res = v[h] - c0 * av[h]
                r1[probe, h, at, :] = res
                u2[probe, h, at, :] = (a1 * c0) * v[h] + c1 * res

    def step2(p):
        at = rows((p + 2) * wy, wy)
        d = [dw[h, at, :] for h in range(2)]
        for probe in range(2):
            v, av = fine_operator(u2, probe, p + 2, d, wy, masks)
            for h in range(2):
                res = r1[probe, h, at, :] - av[h]
                r1[probe, h, at, :] = res
                u3[probe, h, at, :] = a2 * v[h] + c2 * res

    mine = row_mask(wy, sc[S_YOFF], sc[S_YOFF] + ny)

    def step3(p):
        at = rows((p + 2) * wy, wy)
        to = rows(p * wy, wy)
        d = [dw[h, at, :] for h in range(2)]
        res = []
        for probe in range(2):
            v, av = fine_operator(u3, probe, p + 2, d, wy, masks)
            for h in range(2):
                out = jnp.where(mine, r1[probe, h, at, :] - av[h], 0.0)
                r_out[probe, h, to, :] = out
                sol_out[probe, h, to, :] = (
                    c0 * bw[probe, h, rows((p + 3) * wy, wy), :] + u2[probe, h, at, :] + v[h]
                )
                res.append(out)
        return res, d

    def pair(step):
        def body(i, _):
            step(2 * i)
            step(2 * i + 1)
            return 0

        lax.fori_loop(0, nx // 2, body, 0)

    def pair3(i, _):
        (low, d_low), (high, d_high) = step3(2 * i), step3(2 * i + 1)
        for k, value in enumerate([a + b for a, b in zip(low + d_low, high + d_high)]):
            xs[k] = value
        for k in range(6):
            even = xs[k, pl.ds(yoff, cy, stride=2), :]
            odd = xs[k, pl.ds(yoff + 1, cy, stride=2), :]
            ysm[k // 2, rows(i * cy, cy), half[k % 2]] = even + odd
        return 0

    @pl.when(has_l)
    def _():
        step1(-2)
        step1(-1)

    @pl.when(has_r)
    def _():
        step1(nx)
        step1(nx + 1)

    pair(step1)

    @pl.when(has_l)
    def _():
        step2(-1)

    @pl.when(has_r)
    def _():
        step2(nx)

    pair(step2)
    lax.fori_loop(0, nx // 2, pair3, 0)

    pairing = (
        lax.broadcasted_iota(jnp.int32, (2 * LANES, LANES), 0) // 2
        == lax.broadcasted_iota(jnp.int32, (2 * LANES, LANES), 1)
    ).astype(jnp.bfloat16)
    for f in range(3):
        v = ysm[f]
        total = None
        for _ in range(3):
            part = v.astype(jnp.bfloat16)
            v = v - part.astype(F32)
            dot = jnp.dot(part, pairing, preferred_element_type=F32)
            total = dot if total is None else total + dot
        coarse[f] = 0.5 * total - (18.0 if f == 2 else 0.0)

    send_hi = [hi == (1 if sz.two else 0) for hi in his]
    for msg, corners, right in ((m_a, m_cas, par_even), (m_b, m_cbs, jnp.logical_not(par_even))):
        c_at = edge(right, cx, REACH)
        r_at = edge(right, nx, 2)
        for f in range(3):
            msg[pl.ds(f * REACH * cy, REACH * cy), :] = coarse[f, rows(c_at * cy, REACH * cy), :]
            for s in range(n):
                row = edge(send_hi[s], cy, 8)
                for k in range(REACH):
                    corners[s][pl.ds((f * REACH + k) * 8, 8), :] = coarse[f, rows((c_at + k) * cy + row, 8), :]
        base = 3 * REACH * cy
        for probe in range(2):
            for h in range(2):
                for k in range(2):
                    i = (probe * 2 + h) * 2 + k
                    msg[pl.ds(base + i * ny, ny), :] = r_out[probe, h, rows((r_at + k) * wy + yoff, ny), :]
        for s in range(n):
            row = edge(send_hi[s], ny, 1)
            for probe in range(2):
                for h in range(2):
                    i = probe * 2 + h
                    value = r_out[probe, h, pl.ds(edge(right, nx, 1) * wy + yoff + row, 1), :]
                    corners[s][pl.ds(3 * REACH * 8 + i, 1), :] = value
            corners[s][pl.ds(3 * REACH * 8 + 4, 4), :] = jnp.zeros((4, LANES), F32)
    for s in range(n):
        row = edge(send_hi[s], cy, 8)
        for f in range(3):
            for x in range(cx):
                m_ys[s][pl.ds((f * cx + x) * 8, 8), :] = coarse[f, rows(x * cy + row, 8), :]
        row = edge(send_hi[s], ny, 2)
        for probe in range(2):
            for h in range(2):
                for k in range(2):
                    i = (probe * 2 + h) * 2 + k
                    m_ys[s][pl.ds(3 * cx * 8 + i * nx, nx), :] = r_out[
                        probe, h, pl.ds(yoff + row + k, nx, stride=wy), :
                    ]


def post_kernel(sz, *refs):
    n = sz.sides
    sc, r_in, sol_in, dw, coarse, x_a, x_b = refs[:7]
    ys = refs[7 : 7 + n]
    cas = refs[7 + n : 7 + 2 * n]
    cbs = refs[7 + 2 * n : 7 + 3 * n]
    out = refs[7 + 3 * n]
    cw, cu, cc, uz, wz, st_g, st_u, rh, re, r1, u2, ow, sem = refs[8 + 3 * n :]
    nx, ny, wy, cx, cy, wc = sz.nx, sz.ny, sz.wy, sz.cx, sz.cy, sz.wc
    par_even = sc[S_PAR] == 0
    yoff = pl.multiple_of(sc[S_YOFF], 8)
    has_l, has_r = sc[S_HASL] == 1, sc[S_HASR] == 1
    his = [sc[S_HI0], sc[S_HI1]]
    half = [slice(0, LANES), slice(LANES, 2 * LANES)]
    masks = lane_masks(wy)
    planes = cx + 2 * REACH

    y_at = [jnp.where(his[s] == 1, yoff + cy, yoff - 8) for s in range(n)]
    for f in range(3):
        for x in range(cx):
            cw[f, rows((x + REACH) * wc + yoff, cy), :] = coarse[f, rows(x * cy, cy), :]
            for s in range(n):
                cw[f, rows((x + REACH) * wc + y_at[s], 8), :] = ys[s][rows((f * cx + x) * 8, 8), :]
        for msg, corners, to_right in ((x_a, cas, par_even), (x_b, cbs, jnp.logical_not(par_even))):
            at = jnp.where(to_right, REACH + cx, 0)
            for k in range(REACH):
                cw[f, rows((at + k) * wc + yoff, cy), :] = msg[rows((f * REACH + k) * cy, cy), :]
                for s in range(n):
                    cw[f, rows((at + k) * wc + y_at[s], 8), :] = corners[s][rows((f * REACH + k) * 8, 8), :]

    first, last = lane_masks(wc)
    if sz.two:
        low = jnp.where(sc[S_YOFF] == 0, 0, 1)
        high = jnp.where(sc[S_YOFF] == 0, wc - 1, wc)
    else:
        low = jnp.where(sc[S_RLO] > 1, 8, 1)
        high = jnp.where(sc[S_RHI] < wy - 1, wc - 8, wc - 1)
    inside = row_mask(wc, low, high)
    link_l = sc[S_LINKL].astype(F32)
    link_r = sc[S_LINKR].astype(F32)
    for p in range(planes):
        at = pl.ds(p * wc, wc)
        for probe in range(2):
            u = jnp.where(inside, COARSE[0][1], 0.0) * cw[probe, at, :]
            cu[0, probe, at, :] = u
            cc[probe, at, :] = u
    for k in range(COARSE_DEG - 1):
        a, c = COARSE[k + 1]
        c = jnp.where(inside, c, 0.0)
        old, new = k % 2, 1 - k % 2
        for p in range(1 + k, planes - 1 - k):
            at = pl.ds(p * wc, wc)
            for probe in range(2):
                u = cu[old, probe, at, :]
                before = cu[old, probe, pl.ds((p - 1) * wc, wc), :]
                after = cu[old, probe, pl.ds((p + 1) * wc, wc), :]
                if p == REACH:
                    before = before * link_l
                if p == REACH - 1:
                    after = after * link_l
                if p == REACH + cx:
                    before = before * link_r
                if p == REACH + cx - 1:
                    after = after * link_r
                z = jnp.where(first, 0.0, pltpu.roll(u, 1, 1)) + jnp.where(last, 0.0, pltpu.roll(u, LANES - 1, 1))
                near = ((before + after) + y_sum(u)) + z
                res = cw[probe, at, :] - (cw[2, at, :] * u - near)
                if k + 2 < COARSE_DEG:
                    cw[probe, at, :] = res
                u = a * u + c * res
                if k + 2 < COARSE_DEG:
                    cu[new, probe, at, :] = u
                cc[probe, at, :] = cc[probe, at, :] + u

    depth = lax.broadcasted_iota(jnp.int32, (2 * LANES, 2 * LANES), 0) % LANES
    child = lax.broadcasted_iota(jnp.int32, (2 * LANES, 2 * LANES), 1)
    up = (child // 2 == depth).astype(jnp.bfloat16)
    aside = ((child == 2 * depth + 2) | (child == 2 * depth - 1)).astype(jnp.bfloat16)
    span = (cx + 4) * wc
    for probe in range(2):
        v = cc[probe, pl.ds((REACH - 2) * wc, span), :]
        hi = v.astype(jnp.bfloat16)
        lo = (v - hi.astype(F32)).astype(jnp.bfloat16)
        both = jnp.concatenate([hi, lo], axis=1)
        wide = jnp.dot(both, up, preferred_element_type=F32)
        beside = jnp.dot(both, aside, preferred_element_type=F32)
        for h in range(2):
            uz[probe, h] = wide[:, half[h]]
            wz[probe, h] = beside[:, half[h]]

    zero8 = jnp.zeros((8, LANES), F32)
    base = 3 * REACH * cy
    for msg, corners, to_right in ((x_a, cas, par_even), (x_b, cbs, jnp.logical_not(par_even))):
        at = jnp.where(to_right, 2, 0)
        for probe in range(2):
            for h in range(2):
                for k in range(2):
                    i = (probe * 2 + h) * 2 + k
                    rh[probe, h, rows((at + k) * wy + yoff, ny), :] = msg[pl.ds(base + i * ny, ny), :]
                    for s in range(n):
                        zero_at = jnp.where(his[s] == 1, yoff + ny, yoff - 8)
                        rh[probe, h, rows((at + k) * wy + zero_at, 8), :] = zero8
                for s in range(n):
                    row = jnp.where(his[s] == 1, yoff + ny, yoff - 1)
                    i = probe * 2 + h
                    rh[probe, h, pl.ds(jnp.where(to_right, 2, 1) * wy + row, 1), :] = corners[s][
                        pl.ds(3 * REACH * 8 + i, 1), :
                    ]

    c0, (a1, c1), (a2, c2) = FINE[0][1], FINE[1], FINE[2]
    if sz.two:
        low = jnp.where(sc[S_YOFF] == 0, 0, 6)
        high = jnp.where(sc[S_YOFF] == 0, ny + 2, wy)
    else:
        low = jnp.where(sc[S_RLO] > 1, 8, 6)
        high = jnp.where(sc[S_RHI] < wy - 1, ny + 8, ny + 10)
    valid = row_mask(wy, low, high)

    def spread(q, r_ref, r_plane, own):
        at = rows((q + 2) * wc, wc)
        for probe in range(2):
            for h in range(2):
                u = uz[probe, h, at, :]
                g = 3.0 * u + wz[probe, h, at, :]
                before, after = pltpu.roll(u, 1, 0), pltpu.roll(u, wc - 1, 0)
                for k in range(2):
                    gx = g + uz[probe, h, rows((q + 1 + 2 * k) * wc, wc), :]
                    st_g[probe, h, k, pl.ds(0, wc, stride=2), :] = gx + before
                    st_g[probe, h, k, pl.ds(1, wc, stride=2), :] = gx + after
                st_u[probe, h, pl.ds(0, wc, stride=2), :] = u
                st_u[probe, h, pl.ds(1, wc, stride=2), :] = u
        for k in range(2):
            to = rows((2 * q + k + 2) * wy, wy)
            for h in range(2):
                d = dw[h, to, :]
                for probe in range(2):
                    u = st_u[probe, h, rows(yoff, wy), :]
                    old = r_ref[probe, h, rows((r_plane + k) * wy, wy), :]
                    res = (old - d * u) + st_g[probe, h, k, rows(yoff, wy), :]
                    res = jnp.where(valid, res, 0.0)
                    re[probe, h, to, :] = res
                    if own:
                        ow[probe, 2 * q + k, :, half[h]] = (
                            sol_in[probe, h, rows((2 * q + k) * wy, wy), :] + u
                        )

    def own_planes(q, _):
        spread(q, r_in, 2 * q, True)
        return 0

    lax.fori_loop(0, cx, own_planes, 0)
    zero = jnp.zeros((wy, LANES), F32)
    for has, q, at in ((has_l, -1, 0), (has_r, cx, 2)):

        @pl.when(has)
        def _():
            spread(q, rh, at, False)

        @pl.when(jnp.logical_not(has))
        def _():
            for probe in range(2):
                for h in range(2):
                    for k in range(2):
                        re[probe, h, rows((2 * q + 2 + k) * wy, wy), :] = zero
                        u2[probe, h, rows((2 * q + 2 + k) * wy, wy), :] = zero

    for s in range(n):
        row = jnp.where(his[s] == 1, yoff + ny, yoff - 2)
        for probe in range(2):
            for h in range(2):
                for k in range(2):
                    i = (probe * 2 + h) * 2 + k
                    at = pl.ds(2 * wy + row + k, nx, stride=wy)
                    re[probe, h, at, :] = re[probe, h, at, :] + ys[s][pl.ds(3 * cx * 8 + i * nx, nx), :]

    c1 = jnp.where(row_mask(wy, sc[S_RLO], sc[S_RHI]), c1, 0.0)

    def step1(p):
        at = rows((p + 2) * wy, wy)
        d = [dw[h, at, :] for h in range(2)]
        for probe in range(2):
            v, av = fine_operator(re, probe, p + 2, d, wy, masks)
            for h in range(2):
                res = v[h] - c0 * av[h]
                r1[probe, h, at, :] = res
                u2[probe, h, at, :] = (a1 * c0) * v[h] + c1 * res

    def step2(p):
        at = rows((p + 2) * wy, wy)
        d = [dw[h, at, :] for h in range(2)]
        for probe in range(2):
            v, av = fine_operator(u2, probe, p + 2, d, wy, masks)
            for h in range(2):
                res = r1[probe, h, at, :] - av[h]
                last_two = (1.0 + a2) * v[h] + c2 * res
                ow[probe, p, :, half[h]] = (ow[probe, p, :, half[h]] + c0 * re[probe, h, at, :]) + last_two

    def body1(i, _):
        step1(2 * i)
        step1(2 * i + 1)
        return 0

    def body2(i, _):
        step2(2 * i)
        step2(2 * i + 1)
        return 0

    @pl.when(has_l)
    def _():
        step1(-1)

    @pl.when(has_r)
    def _():
        step1(nx)

    lax.fori_loop(0, nx // 2, body1, 0)
    pieces = 4
    size = nx // pieces
    copies = []
    for i in range(pieces):
        lax.fori_loop(i * size // 2, (i + 1) * size // 2, body2, 0)
        copy = pltpu.make_async_copy(
            ow.at[:, pl.ds(i * size, size), rows(yoff, ny), :], out.at[:, pl.ds(i * size, size)], sem.at[i]
        )
        copy.start()
        copies.append(copy)
    for copy in copies:
        copy.wait()


def pick_entry(table, where):
    places = jnp.arange(table.shape[0], dtype=jnp.int32)
    return jnp.sum(jnp.where(places == where, table, 0))


def on_device(n_gx, n_gy, right_side, diagonal, aggregates):
    nx, ny, nz = right_side.shape[1:]
    sz = Sizes(nx, ny, nz, n_gy)
    n, wy, wc, cx, cy = sz.sides, sz.wy, sz.wc, sz.cx, sz.cy
    i, j = lax.axis_index("gx"), lax.axis_index("gy")
    even = i % 2 == 0

    pairs_a = [(k, k ^ 1) for k in range(n_gx)]
    pairs_b = [(k, k + 1) for k in range(1, n_gx - 1, 2)] + [(k + 1, k) for k in range(1, n_gx - 1, 2)]
    along = [[(0, 1), (1, 0)]] if sz.two else [
        [(k, k - 1) for k in range(1, n_gy)],
        [(k, k + 1) for k in range(n_gy - 1)],
    ]

    def both(pairs, perm):
        return [(a * n_gy + c, b * n_gy + d) for a, b in pairs for c, d in perm]

    if sz.two:
        highs = [(j == 0).astype(jnp.int32)] * 2
        sends = [j == 0]
    else:
        highs = [jnp.int32(1), jnp.int32(0)]
        sends = [jnp.bool_(False), jnp.bool_(True)]

    def exchange(m_a, m_b, m_ys, m_cas, m_cbs):
        m_a, m_b, m_ys, m_cas, m_cbs = lax.optimization_barrier((m_a, m_b, m_ys, m_cas, m_cbs))
        got = (
            lax.ppermute(m_a, "gx", pairs_a),
            lax.ppermute(m_b, "gx", pairs_b),
            [lax.ppermute(m_ys[s], "gy", along[s]) for s in range(n)],
            [lax.ppermute(m_cas[s], ("gx", "gy"), both(pairs_a, along[s])) for s in range(n)],
            [lax.ppermute(m_cbs[s], ("gx", "gy"), both(pairs_b, along[s])) for s in range(n)],
        )
        return lax.optimization_barrier(got)

    def ends(field, axis, high, count):
        return lax.dynamic_slice_in_dim(field, edge(high, field.shape[axis], count), count, axis)

    def x_message(right):
        return jnp.concatenate(
            [ends(right_side, 1, right, 3).reshape(6, ny, nz), ends(diagonal, 0, right, 2)], 0
        )

    def y_message(high):
        b = ends(right_side, 2, high, 3).transpose(0, 2, 1, 3).reshape(6, nx, nz)
        return jnp.concatenate([b, ends(diagonal, 1, high, 2).transpose(1, 0, 2)], 0)

    def corner_message(right, high):
        b = ends(ends(right_side, 1, right, 2), 2, high, 2).reshape(8, nz)
        d = ends(ends(diagonal, 0, right, 1), 1, high, 1).reshape(1, nz)
        return jnp.concatenate([b, jnp.broadcast_to(d, (8, nz))], 0)

    odd = jnp.logical_not(even)
    x_a, x_b, ys, cas, cbs = exchange(
        x_message(even),
        x_message(odd),
        [y_message(h) for h in sends],
        [corner_message(even, h) for h in sends],
        [corner_message(odd, h) for h in sends],
    )

    here = pick_entry(aggregates, i)
    link_l = (i > 0) & (pick_entry(aggregates, i - 1) == here)
    link_r = (i < n_gx - 1) & (pick_entry(aggregates, i + 1) == here)
    yoff = 8 * j if sz.two else jnp.int32(8)
    if sz.two:
        r_lo, r_hi = j, wy - 1 + j
    else:
        r_lo = jnp.where(j == 0, 8, 1)
        r_hi = jnp.where(j == n_gy - 1, ny + 8, wy - 1)
    scalars = jnp.stack(
        [i % 2, yoff, i > 0, i < n_gx - 1, link_l, link_r, r_lo, r_hi, highs[0], highs[1]]
    ).astype(jnp.int32)

    smem = pl.BlockSpec(memory_space=pltpu.SMEM)
    vmem = pl.BlockSpec(memory_space=pltpu.VMEM)

    def shape(*dims):
        return jax.ShapeDtypeStruct(dims, F32)

    results = pl.pallas_call(
        functools.partial(pre_kernel, sz),
        in_specs=[smem] + [vmem] * (4 + 3 * n),
        out_specs=[vmem] * (6 + 3 * n),
        out_shape=[
            shape(2, 2, nx * wy, LANES),
            shape(2, 2, nx * wy, LANES),
            shape(2, (nx + 4) * wy, LANES),
            shape(3, cx * cy, LANES),
            shape(sz.xmsg, LANES),
            shape(sz.xmsg, LANES),
        ]
        + [shape(sz.ymsg, LANES)] * n
        + [shape(sz.cmsg, LANES)] * (2 * n),
        scratch_shapes=[
            pltpu.VMEM((2, 2, (nx + 6) * wy, LANES), F32),
            pltpu.VMEM((2, 2, (nx + 4) * wy, LANES), F32),
            pltpu.VMEM((2, 2, (nx + 4) * wy, LANES), F32),
            pltpu.VMEM((2, 2, (nx + 4) * wy, LANES), F32),
            pltpu.VMEM((6, wy, LANES), F32),
            pltpu.VMEM((3, cx * cy, 2 * LANES), F32),
        ],
        compiler_params=pltpu.CompilerParams(vmem_limit_bytes=48 << 20),
        name="pre_smooth",
    )(scalars, right_side, diagonal, x_a, x_b, *ys, *cas, *cbs)
    r_own, sol, dw, coarse = results[:4]
    x_a, x_b, ys, cas, cbs = exchange(
        results[4],
        results[5],
        list(results[6 : 6 + n]),
        list(results[6 + n : 6 + 2 * n]),
        list(results[6 + 2 * n :]),
    )
    planes = cx + 2 * REACH
    return pl.pallas_call(
        functools.partial(post_kernel, sz),
        in_specs=[smem] + [vmem] * (6 + 3 * n),
        out_specs=pl.BlockSpec(memory_space=pl.ANY),
        out_shape=shape(2, nx, ny, nz),
        scratch_shapes=[
            pltpu.VMEM((3, planes * wc, LANES), F32),
            pltpu.VMEM((2, 2, planes * wc, LANES), F32),
            pltpu.VMEM((2, planes * wc, LANES), F32),
            pltpu.VMEM((2, 2, (cx + 4) * wc, LANES), F32),
            pltpu.VMEM((2, 2, (cx + 4) * wc, LANES), F32),
            pltpu.VMEM((2, 2, 2, 2 * wc, LANES), F32),
            pltpu.VMEM((2, 2, 2 * wc, LANES), F32),
            pltpu.VMEM((2, 2, 4 * wy, LANES), F32),
            pltpu.VMEM((2, 2, (nx + 4) * wy, LANES), F32),
            pltpu.VMEM((2, 2, (nx + 4) * wy, LANES), F32),
            pltpu.VMEM((2, 2, (nx + 4) * wy, LANES), F32),
            pltpu.VMEM((2, nx, wy, nz), F32),
            pltpu.SemaphoreType.DMA((4,)),
        ],
        compiler_params=pltpu.CompilerParams(vmem_limit_bytes=48 << 20),
        name="correct_and_smooth",
    )(scalars, r_own, sol, dw, coarse, x_a, x_b, *ys, *cas, *cbs)


def solution(mesh):
    return jax.shard_map(
        functools.partial(on_device, mesh.shape["gx"], mesh.shape["gy"]),
        mesh=mesh,
        in_specs=(P(None, "gx", "gy", None), P("gx", "gy", None), P()),
        out_specs=P(None, "gx", "gy", None),
        check_vma=False,
    )
```

time: 210 us -> 61.8 us (0.29); the launches traced: 206 us -> 61.2 us
  starting transfers between devices: 80.2 us -> 16.9 us
  waiting for transfers between devices: 51.7 us -> 7.58 us
  other arithmetic: 43.6 us -> 0.77 us
  Pallas kernels: 0 us -> 26.3 us
  local copies, waits for them, and re-layouts: 15.3 us -> 6.94 us
  blocking collectives: 7.3 us -> 0 us
  matrix products: 5.16 us -> 0 us
    ppermute x34 -> x10, starting transfers between devices: 80.2 us -> 16.9 us  [the longest x2 6.54 us: exchange(): lax.ppermute(m_b, 'gx', pairs_b)]
    ppermute x34 -> x10, waiting for transfers between devices: 51.7 us -> 7.58 us  [the longest x2 3.79 us: exchange(): lax.ppermute(m_cas[s], ('gx', 'gy'), both(pairs_a, along[s]))]
    pallas_call x0 -> x2, Pallas kernels: none -> 26.3 us  [the longest x1 14 us: on_device(): pl.pallas_call(functools.partial(pre_kernel, sz), in_specs=[smem] + [vmem...]
    add x12 -> x0, other arithmetic: 24.3 us -> none  [the longest x3 13 us: on_device(): update = scale_old * update + scale_res * residual]
    mul x11 -> x0, other arithmetic: 8.94 us -> none  [the longest x2 7.27 us: on_device(): update = scale_old * update + scale_res * residual]
    all_gather x1 -> x0, blocking collectives: 7.3 us -> none  [on_device(): slab = lax.all_gather(coarse_stack, 'gy', axis=2, tiled=True)]
    dot_general x3 -> x0, matrix products: 5.16 us -> none  [pair_along_depth(): jnp.dot(field, pairing, precision=lax.Precision.HIGHEST, preferred_elemen...]
    add x2 -> x0, local copies, waits for them, and re-layouts: 4.52 us -> none  [the longest x1 2.54 us: on_device(): solution = solution + update]
  transfers between devices with their start and end apart: 34 -> 10, of which waited for: 20 -> 3; matrix products, arithmetic and copies ran while one was open for 4% -> 1% of each run, Pallas kernels for 0% -> 0%
where the time goes in v1:
time: 61.8 us; the launch traced here: 61.2 us
  Pallas kernels  26.3 us (43%)
  starting transfers between devices  16.9 us (27%)
  waiting for transfers between devices  7.58 us (12%)
  local copies, waits for them, and re-layouts  6.94 us (11%)
  between operations  2.7 us (4%)
  other arithmetic  0.77 us (1%)
    pallas_call x1, Pallas kernels, on_device(): pl.pallas_call(functools.partial(pre_kernel, sz), in_specs=[smem] + [vmem...  14 us
    pallas_call x1, Pallas kernels, on_device(): pl.pallas_call(functools.partial(post_kernel, sz), in_specs=[smem] + [vme...  12.4 us
    ppermute x2, starting transfers between devices, exchange(): lax.ppermute(m_b, 'gx', pairs_b)  6.54 us
    ppermute x2, starting transfers between devices, exchange(): lax.ppermute(m_cbs[s], ('gx', 'gy'), both(pairs_b, along[s]))  5.43 us
    dynamic_slice x5, local copies, waits for them, and re-layouts, ends(): lax.dynamic_slice_in_dim(field, edge(high, field.shape[axis], count), cou...  3.94 us
    ppermute x2, waiting for transfers between devices, exchange(): lax.ppermute(m_cas[s], ('gx', 'gy'), both(pairs_a, along[s]))  3.79 us
    ppermute x2, waiting for transfers between devices, exchange(): lax.ppermute(m_cbs[s], ('gx', 'gy'), both(pairs_b, along[s]))  3.77 us
    ppermute x2, starting transfers between devices, exchange(): lax.ppermute(m_cas[s], ('gx', 'gy'), both(pairs_a, along[s]))  3.36 us
  transfers between devices with their start and end apart: 10, of which 3 were waited for; matrix products, arithmetic and copies ran while one was open for 1% of the time, Pallas kernels for 0%

profile of v1, /device:TPU:21, one launch (start us, length us, event | category | flops | bytes accessed | tf_op | source)
XLA Modules:
  0.0 61.2 jit_solution(5607657653000244825)
XLA Ops:
  0.0 0.0 copy-start.1
  0.0 0.0 copy-start.2
  0.0 1.1 %constant_dynamic-slice_fusion.4 = f32[32,2,256]{2,1,0:T(2,128)S(1)} fusion(f32[32,32,256]{2,1,0:T(8,128)} %refs_2_.1, s32[]{:T(128)S(6)} %select_n.87), kind=kLoop, calls=%fused_computation.11 | loop fusion | bytes 131076 | tf_op jit(solution)/shard_map/dynamic_slice | solution.py:583
  1.1 0.9 %constant_dynamic-slice_fusion.5 = (f32[2,32,256]{2,1,0:T(8,128)S(1)}, f32[2,32,256]{2,1,0:T(8,128)S(1)}) fusion(f32[32,32,256]{2,1,0:T(8,128)} %refs_2_.1, s32[]{:T(128)S(6)} %select_n.85, s32[]{:T(128)S(6)} %select_n.83), kind=kLoop, calls=%fused_computation.12 | loop fusion | bytes 262152 | tf_op jit(solution)/shard_map/dynamic_slice | solution.py:583
  2.0 0.9 %constant_dynamic-slice_fusion.1 = (f32[2,2,2,256]{3,2,1,0:T(2,128)S(1)}, f32[2,2,2,256]{3,2,1,0:T(2,128)S(1)}) fusion(f32[2,32,32,256]{3,2,1,0:T(8,128)} %refs_1_.1, s32[]{:T(128)S(6)} %select_n.94, s32[]{:T(128)S(6)} %select_n.89, s32[]{:T(128)S(6)} %select_n.88), kind=kLoop, calls=%fused_computation.8 | loop fusion | bytes 32780 | tf_op jit(solution)/shard_map/dynamic_slice | solution.py:583
  2.9 1.1 %dynamic-slice_bitcast_fusion = f32[2,3,32,256]{3,1,2,0:T(4,128)S(1)} fusion(f32[2,32,32,256]{3,2,1,0:T(8,128)} %refs_1_.1, s32[]{:T(128)S(6)} %select_n.86), kind=kLoop, calls=%fused_computation.3 | loop fusion | bytes 393220 | tf_op jit(solution)/shard_map/transpose | solution.py:591
  4.1 1.1 %constant_dynamic-slice_fusion.6 = (f32[2,3,32,256]{3,2,1,0:T(8,128)S(1)}, f32[2,3,32,256]{3,2,1,0:T(8,128)S(1)}) fusion(f32[2,32,32,256]{3,2,1,0:T(8,128)} %refs_1_.1, s32[]{:T(128)S(6)} %select_n.84, s32[]{:T(128)S(6)} %select_n.82), kind=kLoop, calls=%fused_computation.13 | loop fusion | bytes 786440 | tf_op jit(solution)/shard_map/dynamic_slice | solution.py:583
  5.2 0.0 copy-done.1
  5.3 0.7 %collective-permute-start = (f32[8,32,256]{2,1,0:T(8,128)S(1)}, f32[8,32,256]{2,1,0:T(8,128)S(1)}, u32[]{:S(2)}, u32[]{:S(2)}) collective-permute-start(f32[8,32,256]{2,1,0:T(8,128)S(1)} %get-tuple-element.34), channel_id=1, source_target_pairs={{0,2},{2,0},{4,6},{6,4},{8,10},{10,8},{12,14},{14,12},{16,18},{18,... | collective-permute-start | bytes 786440 | tf_op jit(solution)/shard_map/ppermute | solution.py:574
  6.0 3.0 %collective-permute-start.1 = (f32[8,32,256]{2,1,0:T(8,128)S(1)}, f32[8,32,256]{2,1,0:T(8,128)S(1)}, u32[]{:S(2)}, u32[]{:S(2)}) collective-permute-start(f32[8,32,256]{2,1,0:T(8,128)S(1)} %get-tuple-element.35), channel_id=1, source_target_pairs={{2,4},{6,8},{10,12},{14,16},{18,20},{22,24},{26,28},{4,2},{8,6},{1... | collective-permute-start | bytes 786440 | tf_op jit(solution)/shard_map/ppermute | solution.py:575
  9.1 0.2 collective-permute-start.2
  9.3 1.9 %collective-permute-start.3 = (f32[16,256]{1,0:T(8,128)S(1)}, f32[16,256]{1,0:T(8,128)S(1)}, u32[]{:S(2)}, u32[]{:S(2)}) collective-permute-start(f32[16,256]{1,0:T(8,128)S(1)} %get-tuple-element.37), channel_id=1, source_target_pairs={{0,3},{1,2},{2,1},{3,0},{4,7},{5,6},{6,5},{7,4},{8,11},{9,10},{10,... | collective-permute-start | bytes 49160 | tf_op jit(solution)/shard_map/ppermute | solution.py:577
  11.1 2.8 %collective-permute-start.4 = (f32[16,256]{1,0:T(8,128)S(1)}, f32[16,256]{1,0:T(8,128)S(1)}, u32[]{:S(2)}, u32[]{:S(2)}) collective-permute-start(f32[16,256]{1,0:T(8,128)S(1)} %get-tuple-element.38), channel_id=1, source_target_pairs={{2,5},{3,4},{6,9},{7,8},{10,13},{11,12},{14,17},{15,16},{18,21},{1... | collective-permute-start | bytes 49160 | tf_op jit(solution)/shard_map/ppermute | solution.py:578
  13.9 0.0 copy-done.2
  13.9 0.7 %fusion.2 = (s32[]{:T(128)}, s32[]{:T(128)}, s32[]{:T(128)}) fusion(s32[16]{0:T(128)S(1)} %copy-done.2, s32[]{:T(128)S(6)} %add.38, s32[]{:T(128)S(6)} %sub.3, s32[]{:T(128)S(6)} %axis_index.23), kind=kLoop, calls=%fused_computation.21 | loop fusion | flops 141 | bytes 88 | tf_op jit(solution)/shard_map/reduce_sum | solution.py:544
  17.1 0.1 stack.60.refs_0_
  17.2 0.8 %collective-permute-done.3.refs_6_ = f32[16,256]{1,0:T(8,128)S(1)} collective-permute-done((f32[16,256]{1,0:T(8,128)S(1)}, f32[16,256]{1,0:T(8,128)S(1)}, u32[]{:S(2)}, u32[]{:S(2)}) %collective-permute-start.3) | collective-permute-done | bytes 16416 | tf_op jit(solution)/shard_map/ppermute | solution.py:577
  18.0 0.0 collective-permute-done.4.refs_7_
  18.0 0.0 collective-permute-done.refs_3_
  18.0 0.0 collective-permute-done.1.refs_4_
  18.0 0.0 collective-permute-done.2.refs_5_
  18.0 14.0 %pre_smooth.1 = (f32[2,2,1280,128]{3,2,1,0:T(8,128)}, f32[2,2,1280,128]{3,2,1,0:T(8,128)}, f32[2,1440,128]{2,1,0:T(8,128)S(1)}, f32[3,256,128]{2,1,0:T(8,128)S(1...) custom-call(s32[10]{0:T(128)S(1)} %stack.60.refs_0_, ...), custom_call_target="tpu_custom_call" | custom-call | tf_op jit(solution)/shard_map/pre_smooth/pallas_call | solution.py:627
  32.0 0.6 %collective-permute-start.7 = (f32[640,128]{1,0:T(8,128)S(1)}, f32[640,128]{1,0:T(8,128)S(1)}, u32[]{:S(2)}, u32[]{:S(2)}) collective-permute-start(f32[640,128]{1,0:T(8,128)S(1)} %get-tuple-element.55), channel_id=1, source_target_pairs={{0,1},{1,0},{2,3},{3,2},{4,5},{5,4},{6,7},{7,6},{8,9},{9,8},{10,11... | collective-permute-start | bytes 983048 | tf_op jit(solution)/shard_map/ppermute | solution.py:576
  32.6 0.0 collective-permute-start.5
  32.6 3.5 %collective-permute-start.6 = (f32[592,128]{1,0:T(8,128)S(1)}, f32[592,128]{1,0:T(8,128)S(1)}, u32[]{:S(2)}, u32[]{:S(2)}) collective-permute-start(f32[592,128]{1,0:T(8,128)S(1)} %get-tuple-element.54), channel_id=1, source_target_pairs={{2,4},{6,8},{10,12},{14,16},{18,20},{22,24},{26,28},{4,2},{8,6},{1... | collective-permute-start | bytes 909320 | tf_op jit(solution)/shard_map/ppermute | solution.py:575
  36.1 1.5 %collective-permute-start.8 = (f32[176,128]{1,0:T(8,128)S(1)}, f32[176,128]{1,0:T(8,128)S(1)}, u32[]{:S(2)}, u32[]{:S(2)}) collective-permute-start(f32[176,128]{1,0:T(8,128)S(1)} %get-tuple-element.56), channel_id=1, source_target_pairs={{0,3},{1,2},{2,1},{3,0},{4,7},{5,6},{6,5},{7,4},{8,11},{9,10},{10,... | collective-permute-start | bytes 270344 | tf_op jit(solution)/shard_map/ppermute | solution.py:577
  37.6 2.7 %collective-permute-start.9 = (f32[176,128]{1,0:T(8,128)S(1)}, f32[176,128]{1,0:T(8,128)S(1)}, u32[]{:S(2)}, u32[]{:S(2)}) collective-permute-start(f32[176,128]{1,0:T(8,128)S(1)} %get-tuple-element.57), channel_id=1, source_target_pairs={{2,5},{3,4},{6,9},{7,8},{10,13},{11,12},{14,17},{15,16},{18,21},{1... | collective-permute-start | bytes 270344 | tf_op jit(solution)/shard_map/ppermute | solution.py:578
  40.3 3.0 %collective-permute-done.8.refs_8_ = f32[176,128]{1,0:T(8,128)S(1)} collective-permute-done((f32[176,128]{1,0:T(8,128)S(1)}, f32[176,128]{1,0:T(8,128)S(1)}, u32[]{:S(2)}, u32[]{:S(2)}) %collective-permute-start.8) | collective-permute-done | bytes 90144 | tf_op jit(solution)/shard_map/ppermute | solution.py:577
  43.3 3.8 %collective-permute-done.9.refs_9_ = f32[176,128]{1,0:T(8,128)S(1)} collective-permute-done((f32[176,128]{1,0:T(8,128)S(1)}, f32[176,128]{1,0:T(8,128)S(1)}, u32[]{:S(2)}, u32[]{:S(2)}) %collective-permute-start.9) | collective-permute-done | bytes 90144 | tf_op jit(solution)/shard_map/ppermute | solution.py:578
  47.1 0.0 collective-permute-done.5.refs_5_
  47.1 0.0 collective-permute-done.6.refs_6_
  47.1 0.0 collective-permute-done.7.refs_7_
  47.1 0.0 copy-start
  47.1 1.7 %copy-done = f32[2,2,1280,128]{3,2,1,0:T(8,128)S(1)} copy-done((f32[2,2,1280,128]{3,2,1,0:T(8,128)S(1)}, f32[2,2,1280,128]{3,2,1,0:T(8,128)}, u32[]{:S(2)}) %copy-start) | copy-done | bytes 2621464
  48.9 12.4 %correct_and_smooth.1 = f32[2,32,32,256]{3,2,1,0:T(8,128)} custom-call(s32[10]{0:T(128)S(1)} %stack.60.refs_0_, f32[2,2,1280,128]{3,2,1,0:T(8,128)S(1)} %copy-done, f32[2,2,1280,128]{3,2,1,0:T(8,128)} %get-tuple-element.45.refs_2_, f32[2,1440,128]{2,1,0:T(8,128)S(1)} %get-tuple-element.46.refs_3_, f32[3,256,128]{2,1,0:T(8,128)S(1)} %get-tuple-element.47.refs_4_, ...), custom_call_target="tpu_custom_call" | custom-call | tf_op jit(solution)/shard_map/correct_and_smooth/pallas_call | solution.py:661
  (10 shorter events, 0.2 us)
Async XLA Ops:
  0.0 5.2 %copy-start.1 = (f32[32,32,256]{2,1,0:T(8,128)S(1)}, f32[32,32,256]{2,1,0:T(8,128)}, u32[]{:S(2)}) copy-start(f32[32,32,256]{2,1,0:T(8,128)} %refs_2_.1) | copy-start | bytes 3145732
  0.0 13.9 %copy-start.2 = (s32[16]{0:T(128)S(1)}, s32[16]{0:T(128)}, u32[]{:S(2)}) copy-start(s32[16]{0:T(128)} %param.5) | copy-start | bytes 196
  5.3 12.7 %collective-permute-start = (f32[8,32,256]{2,1,0:T(8,128)S(1)}, f32[8,32,256]{2,1,0:T(8,128)S(1)}, u32[]{:S(2)}, u32[]{:S(2)}) collective-permute-start(f32[8,32,256]{2,1,0:T(8,128)S(1)} %get-tuple-element.34), channel_id=1, source_target_pairs={{0,2},{2,0},{4,6},{6,4},{8,10},{10,8},{12,14},{14,12},{16,18},{18,... | collective-permute-start | bytes 786440 | tf_op jit(solution)/shard_map/ppermute | solution.py:574
  6.0 12.0 %collective-permute-start.1 = (f32[8,32,256]{2,1,0:T(8,128)S(1)}, f32[8,32,256]{2,1,0:T(8,128)S(1)}, u32[]{:S(2)}, u32[]{:S(2)}) collective-permute-start(f32[8,32,256]{2,1,0:T(8,128)S(1)} %get-tuple-element.35), channel_id=1, source_target_pairs={{2,4},{6,8},{10,12},{14,16},{18,20},{22,24},{26,28},{4,2},{8,6},{1... | collective-permute-start | bytes 786440 | tf_op jit(solution)/shard_map/ppermute | solution.py:575
  9.1 8.9 %collective-permute-start.2 = (f32[8,32,256]{2,1,0:T(8,128)S(1)}, f32[8,32,256]{2,1,0:T(8,128)S(1)}, u32[]{:S(2)}, u32[]{:S(2)}) collective-permute-start(f32[8,32,256]{2,1,0:T(8,128)S(1)} %pad_maximum_fusion.2), channel_id=1, source_target_pairs={{0,1},{1,0},{2,3},{3,2},{4,5},{5,4},{6,7},{7,6},{8,9},{9,8},{10,11... | collective-permute-start | bytes 786440 | tf_op jit(solution)/shard_map/ppermute | solution.py:576
  9.3 8.7 %collective-permute-start.3 = (f32[16,256]{1,0:T(8,128)S(1)}, f32[16,256]{1,0:T(8,128)S(1)}, u32[]{:S(2)}, u32[]{:S(2)}) collective-permute-start(f32[16,256]{1,0:T(8,128)S(1)} %get-tuple-element.37), channel_id=1, source_target_pairs={{0,3},{1,2},{2,1},{3,0},{4,7},{5,6},{6,5},{7,4},{8,11},{9,10},{10,... | collective-permute-start | bytes 49160 | tf_op jit(solution)/shard_map/ppermute | solution.py:577
  11.1 6.9 %collective-permute-start.4 = (f32[16,256]{1,0:T(8,128)S(1)}, f32[16,256]{1,0:T(8,128)S(1)}, u32[]{:S(2)}, u32[]{:S(2)}) collective-permute-start(f32[16,256]{1,0:T(8,128)S(1)} %get-tuple-element.38), channel_id=1, source_target_pairs={{2,5},{3,4},{6,9},{7,8},{10,13},{11,12},{14,17},{15,16},{18,21},{1... | collective-permute-start | bytes 49160 | tf_op jit(solution)/shard_map/ppermute | solution.py:578
  32.0 15.1 %collective-permute-start.7 = (f32[640,128]{1,0:T(8,128)S(1)}, f32[640,128]{1,0:T(8,128)S(1)}, u32[]{:S(2)}, u32[]{:S(2)}) collective-permute-start(f32[640,128]{1,0:T(8,128)S(1)} %get-tuple-element.55), channel_id=1, source_target_pairs={{0,1},{1,0},{2,3},{3,2},{4,5},{5,4},{6,7},{7,6},{8,9},{9,8},{10,11... | collective-permute-start | bytes 983048 | tf_op jit(solution)/shard_map/ppermute | solution.py:576
  32.6 14.5 %collective-permute-start.5 = (f32[592,128]{1,0:T(8,128)S(1)}, f32[592,128]{1,0:T(8,128)S(1)}, u32[]{:S(2)}, u32[]{:S(2)}) collective-permute-start(f32[592,128]{1,0:T(8,128)S(1)} %get-tuple-element.53), channel_id=1, source_target_pairs={{0,2},{2,0},{4,6},{6,4},{8,10},{10,8},{12,14},{14,12},{16,18},{18,... | collective-permute-start | bytes 909320 | tf_op jit(solution)/shard_map/ppermute | solution.py:574
  32.6 14.5 %collective-permute-start.6 = (f32[592,128]{1,0:T(8,128)S(1)}, f32[592,128]{1,0:T(8,128)S(1)}, u32[]{:S(2)}, u32[]{:S(2)}) collective-permute-start(f32[592,128]{1,0:T(8,128)S(1)} %get-tuple-element.54), channel_id=1, source_target_pairs={{2,4},{6,8},{10,12},{14,16},{18,20},{22,24},{26,28},{4,2},{8,6},{1... | collective-permute-start | bytes 909320 | tf_op jit(solution)/shard_map/ppermute | solution.py:575
  36.1 7.2 %collective-permute-start.8 = (f32[176,128]{1,0:T(8,128)S(1)}, f32[176,128]{1,0:T(8,128)S(1)}, u32[]{:S(2)}, u32[]{:S(2)}) collective-permute-start(f32[176,128]{1,0:T(8,128)S(1)} %get-tuple-element.56), channel_id=1, source_target_pairs={{0,3},{1,2},{2,1},{3,0},{4,7},{5,6},{6,5},{7,4},{8,11},{9,10},{10,... | collective-permute-start | bytes 270344 | tf_op jit(solution)/shard_map/ppermute | solution.py:577
  37.6 9.5 %collective-permute-start.9 = (f32[176,128]{1,0:T(8,128)S(1)}, f32[176,128]{1,0:T(8,128)S(1)}, u32[]{:S(2)}, u32[]{:S(2)}) collective-permute-start(f32[176,128]{1,0:T(8,128)S(1)} %get-tuple-element.57), channel_id=1, source_target_pairs={{2,5},{3,4},{6,9},{7,8},{10,13},{11,12},{14,17},{15,16},{18,21},{1... | collective-permute-start | bytes 270344 | tf_op jit(solution)/shard_map/ppermute | solution.py:578
  47.1 1.7 %copy-start = (f32[2,2,1280,128]{3,2,1,0:T(8,128)S(1)}, f32[2,2,1280,128]{3,2,1,0:T(8,128)}, u32[]{:S(2)}) copy-start(f32[2,2,1280,128]{3,2,1,0:T(8,128)} %get-tuple-element.44.refs_1_) | copy-start | bytes 7864324

commit v2 on v0

v2 whole, which is shorter than its diff:
```python
import functools

import jax
import jax.numpy as jnp
from jax import lax
from jax.experimental import pallas as pl
from jax.experimental.pallas import tpu as pltpu
from jax.sharding import PartitionSpec as P

DEGREE = 3
COARSE_DEG = 6


FINE_LOWER = 3.0
FINE_UPPER = 12.4
COARSE_LOWER = 0.5
COARSE_UPPER = 13.4

LANES = 128
REACH = 7
F32 = jnp.float32


def cheb_pairs(lower, upper, count):
    middle = (upper + lower) / 2.0
    halfwidth = (upper - lower) / 2.0
    ratio_mid = middle / halfwidth
    rho_old = 1.0 / ratio_mid
    result = [(0.0, 1.0 / middle)]
    for repeat in range(count - 1):
        rho_new = 1.0 / (2.0 * ratio_mid - rho_old)
        result.append((rho_new * rho_old, 2.0 * rho_new / halfwidth))
        rho_old = rho_new
    return result


FINE = cheb_pairs(FINE_LOWER, FINE_UPPER, DEGREE)
COARSE = cheb_pairs(COARSE_LOWER, COARSE_UPPER, COARSE_DEG)


class Sizes:
    def __init__(self, nx, ny, nz, n_gx, n_gy):
        assert nz == 2 * LANES and n_gy >= 2 and ny % 16 == 0 and nx % 4 == 0
        self.nx, self.ny, self.nz = nx, ny, nz
        self.n_gx, self.n_gy = n_gx, n_gy
        self.two = n_gy == 2
        self.sides = 1 if self.two else 2
        self.wy = ny + 8 * self.sides
        self.cx, self.cy = nx // 2, ny // 2
        self.wc = self.cy + 8 * self.sides
        self.bw = (2, 2, (nx + 6) * self.wy, LANES)
        self.dw = (2, (nx + 4) * self.wy, LANES)
        self.brick = (2, 2, nx * self.wy, LANES)
        self.coarse = self.cx * self.cy
        self.x1 = 8 * 2 * ny
        self.y1 = 8 * 2 * nx
        self.c1 = 16
        self.x2_base = (3 * REACH - 1) * self.cy
        self.x2 = self.x2_base + 8 * ny
        self.y2_base = (3 * REACH - 1) * self.cx
        self.y2 = self.y2_base + 8 * nx
        self.c2 = 64


class Place:
    def __init__(self, sz):
        i, j = lax.axis_index("gx"), lax.axis_index("gy")
        self.i = i
        self.even = i % 2 == 0
        self.odd = i % 2 != 0
        self.has_l, self.has_r = i > 0, i < sz.n_gx - 1
        if sz.two:
            self.yoff = pl.multiple_of(8 * j, 8)
            self.high_in = [j == 0]
            self.high_out = [j == 0]
            self.fine = (j, sz.wy - 1 + j)
            self.crs = (j, sz.wc - 1 + j)
            self.valid = (6 * j, sz.ny + 2 + 6 * j)
        else:
            first, last = j == 0, j == sz.n_gy - 1
            self.yoff = 8
            self.high_in = [True, False]
            self.high_out = [False, True]
            self.fine = (jnp.where(first, 8, 1), jnp.where(last, sz.ny + 8, sz.wy - 1))
            self.crs = (jnp.where(first, 8, 1), jnp.where(last, sz.cy + 8, sz.wc - 1))
            self.valid = (jnp.where(first, 8, 6), jnp.where(last, sz.ny + 8, sz.ny + 10))


def pick(condition, yes, no):
    if isinstance(condition, bool):
        return yes if condition else no
    return jnp.where(condition, yes, no)


def edge(high, size, count):
    return pick(high, size - count, 0)


def rows(start, size):
    return pl.ds(pl.multiple_of(start, 8), size)


def lane_masks(height):
    lane = lax.broadcasted_iota(jnp.int32, (height, LANES), 1)
    return lane == 0, lane == LANES - 1


def row_mask(height, span):
    row = lax.broadcasted_iota(jnp.int32, (height, LANES), 0)
    return (row >= span[0]) & (row < span[1])


def y_sum(v):
    return pltpu.roll(v, 1, 0) + pltpu.roll(v, v.shape[0] - 1, 0)


def below(v, masks):
    return jnp.where(masks[0], 0.0, pltpu.roll(v, 1, 1))


def above(v, masks):
    return jnp.where(masks[1], 0.0, pltpu.roll(v, LANES - 1, 1))


def z_sum(even, odd, masks):
    return odd + below(odd, masks), even + above(even, masks)


def parity_matrix(transposed):
    row = lax.broadcasted_iota(jnp.int32, (2 * LANES, 2 * LANES), 0)
    col = lax.broadcasted_iota(jnp.int32, (2 * LANES, 2 * LANES), 1)
    if transposed:
        row, col = col, row
    return (row == 2 * (col % LANES) + col // LANES).astype(jnp.bfloat16)


def permute_lanes(v, matrix, terms):
    total = None
    for k in range(terms):
        part = v.astype(jnp.bfloat16)
        if k + 1 < terms:
            v = v - part.astype(F32)
        dot = jnp.dot(part, matrix, preferred_element_type=F32)
        total = dot if total is None else total + dot
    return total


def fine_operator(ref, probe, plane, diag, wy, masks):
    v = [ref[probe, h, rows(plane * wy, wy), :] for h in range(2)]
    z = z_sum(v[0], v[1], masks)
    res = []
    for h in range(2):
        x = ref[probe, h, rows((plane - 1) * wy, wy), :] + ref[probe, h, rows((plane + 1) * wy, wy), :]
        res.append(diag[h] * v[h] - ((x + y_sum(v[h])) + z[h]))
    return v, res


def looped(step, count, width=4):
    def body(i, _):
        for k in range(width):
            step(width * i + k)
        return 0

    lax.fori_loop(0, count // width, body, 0)


HALF = [slice(0, LANES), slice(LANES, 2 * LANES)]
CORNER1 = [(0, 0), (0, 1), (1, 0)]
CORNER2 = [(f, p, q) for f in range(3) for p in range(6) for q in range(6 - p - f // 2)]


def pack_kernel(sz, *refs):
    n = sz.sides
    rhs, diag, m_a, m_b = refs[:4]
    m_ys, m_cas, m_cbs = refs[4 : 4 + n], refs[4 + n : 4 + 2 * n], refs[4 + 2 * n : 4 + 3 * n]
    xr, xd, yr, yd, tr, td, sem = refs[4 + 3 * n :]
    nx, ny = sz.nx, sz.ny
    at = Place(sz)
    copies = []

    def fetch(src, dst):
        copy = pltpu.make_async_copy(src, dst, sem.at[len(copies)])
        copy.start()
        copies.append(copy)

    for s in range(n):
        slab = rows(edge(at.high_out[s], ny, 8), 8)
        fetch(rhs.at[:, :, slab, :], yr.at[s])
        fetch(diag.at[:, slab, :], yd.at[s])
    for e, right in enumerate((at.even, at.odd)):
        fetch(rhs.at[:, pl.ds(edge(right, nx, 3), 3)], xr.at[e])
        fetch(diag.at[pl.ds(edge(right, nx, 2), 2)], xd.at[e])
    split = parity_matrix(False)
    for copy in copies[: 2 * n]:
        copy.wait()
    for s in range(n):
        v = permute_lanes(yr[s].reshape(2 * nx * 8, 2 * LANES), split, 3)
        d = permute_lanes(yd[s].reshape(nx * 8, 2 * LANES), split, 3)
        for h in range(2):
            tr[s, h] = v[:, HALF[h]]
            td[s, h] = d[:, HALF[h]]
        high = at.high_out[s]
        for h in range(2):
            for k in range(3):
                for probe in range(2):
                    i = (probe * 3 + k) * 2 + h
                    row = edge(high, 8, 3) + k + probe * nx * 8
                    m_ys[s][pl.ds(i * nx, nx), :] = tr[s, h, pl.ds(row, nx, stride=8), :]
            for k in range(2):
                row = edge(high, 8, 2) + k
                m_ys[s][pl.ds((12 + 2 * k + h) * nx, nx), :] = td[s, h, pl.ds(row, nx, stride=8), :]
            for msgs, right in ((m_cas, at.even), (m_cbs, at.odd)):
                for m, (p, q) in enumerate(CORNER1):
                    row = pick(high, 7 - q, q) + pick(right, nx - 1 - p, p) * 8
                    for probe in range(2):
                        msgs[s][pl.ds((m * 2 + probe) * 2 + h, 1), :] = tr[s, h, pl.ds(row + probe * nx * 8, 1), :]
                row = pick(high, 7, 0) + pick(right, nx - 1, 0) * 8
                msgs[s][pl.ds(12 + h, 1), :] = td[s, h, pl.ds(row, 1), :]
                msgs[s][pl.ds(14 + h, 1), :] = td[s, h, pl.ds(row, 1), :]
    for copy in copies[2 * n :]:
        copy.wait()
    for e, msg in enumerate((m_a, m_b)):
        v = permute_lanes(xr[e].reshape(6 * ny, 2 * LANES), split, 3)
        d = permute_lanes(xd[e].reshape(2 * ny, 2 * LANES), split, 3)
        for k in range(6):
            for h in range(2):
                msg[pl.ds((2 * k + h) * ny, ny), :] = v[k * ny : (k + 1) * ny, HALF[h]]
        for k in range(2):
            for h in range(2):
                msg[pl.ds((12 + 2 * k + h) * ny, ny), :] = d[k * ny : (k + 1) * ny, HALF[h]]


def open_kernel(sz, first, rhs, diag, bw, dw, cd, rb, db, xs, sem):
    del first
    nx, ny, wy, cy = sz.nx, sz.ny, sz.wy, sz.cy
    at = Place(sz)
    split = parity_matrix(False)
    zero8 = jnp.zeros((8, LANES), F32)
    zero_at = [pick(at.high_in[s], at.yoff + ny, at.yoff - 8) for s in range(sz.sides)]
    width = 4
    pieces = 4
    size = nx // pieces
    copies = []
    for i in range(pieces):
        part = pl.ds(i * size, size)
        copies.append(
            (
                pltpu.make_async_copy(rhs.at[:, part], rb.at[:, part], sem.at[i, 0]),
                pltpu.make_async_copy(diag.at[part], db.at[part], sem.at[i, 1]),
            )
        )
        for copy in copies[-1]:
            copy.start()

    def body(i, _):
        for f in range(3):
            src = db[pl.ds(width * i, width)] if f == 2 else rb[f, pl.ds(width * i, width)]
            v = permute_lanes(src.reshape(width * ny, 2 * LANES), split, 3)
            if f == 2:
                v = v + 6.0
            for k in range(width):
                for h in range(2):
                    if f == 2:
                        ref, base = dw.at[h], (width * i + k + 2) * wy
                    else:
                        ref, base = bw.at[f, h], (width * i + k + 3) * wy
                    ref[rows(base + at.yoff, ny), :] = v[k * ny : (k + 1) * ny, HALF[h]]
                    for z in zero_at:
                        ref[rows(base + z, 8), :] = zero8
            if f == 2:
                for k in range(width // 2):
                    low, high = v[2 * k * ny : (2 * k + 1) * ny], v[(2 * k + 1) * ny : (2 * k + 2) * ny]
                    total = low + high
                    xs[k] = total[:, HALF[0]] + total[:, HALF[1]]
                    pair = xs[k, pl.ds(0, cy, stride=2), :] + xs[k, pl.ds(1, cy, stride=2), :]
                    cd[rows((i * (width // 2) + k) * cy, cy), :] = 0.5 * pair - 18.0
        return 0

    for i in range(pieces):
        for copy in copies[i]:
            copy.wait()
        lax.fori_loop(i * size // width, (i + 1) * size // width, body, 0)


def pre_kernel(sz, *refs):
    n = sz.sides
    cd, xa, xb = refs[2:5]
    ys, cas, cbs = refs[5 : 5 + n], refs[5 + n : 5 + 2 * n], refs[5 + 2 * n : 5 + 3 * n]
    outs = refs[5 + 3 * n :]
    bw, dw, r_out, sol_out, coarse, m_a, m_b = outs[:7]
    m_ys, m_cas, m_cbs = outs[7 : 7 + n], outs[7 + n : 7 + 2 * n], outs[7 + 2 * n : 7 + 3 * n]
    r1, u2, u3, xs = outs[7 + 3 * n :]
    nx, ny, wy, cx, cy = sz.nx, sz.ny, sz.wy, sz.cx, sz.cy
    at = Place(sz)
    yoff = at.yoff
    masks = lane_masks(wy)

    zero8 = jnp.zeros((8, LANES), F32)
    zero_at = [pick(at.high_in[s], yoff + ny, yoff - 8) for s in range(n)]
    for msg, corners, to_right in ((xa, cas, at.even), (xb, cbs, at.odd)):
        b0 = jnp.where(to_right, nx + 3, 0)
        d0 = jnp.where(to_right, nx + 2, 0)
        for h in range(2):
            for k in range(3):
                for probe in range(2):
                    i = (probe * 3 + k) * 2 + h
                    bw[probe, h, rows((b0 + k) * wy + yoff, ny), :] = msg[pl.ds(i * ny, ny), :]
                    for z in zero_at:
                        bw[probe, h, rows((b0 + k) * wy + z, 8), :] = zero8
            for k in range(2):
                dw[h, rows((d0 + k) * wy + yoff, ny), :] = 6.0 + msg[pl.ds((12 + 2 * k + h) * ny, ny), :]
                for z in zero_at:
                    dw[h, rows((d0 + k) * wy + z, 8), :] = zero8
            for s in range(n):
                for m, (p, q) in enumerate(CORNER1):
                    row = pick(at.high_in[s], yoff + ny + q, yoff - 1 - q)
                    row = row + jnp.where(to_right, nx + 3 + p, 2 - p) * wy
                    for probe in range(2):
                        bw[probe, h, pl.ds(row, 1), :] = corners[s][pl.ds((m * 2 + probe) * 2 + h, 1), :]
                row = pick(at.high_in[s], yoff + ny, yoff - 1) + jnp.where(to_right, nx + 2, 1) * wy
                dw[h, pl.ds(row, 1), :] = 6.0 + corners[s][pl.ds(12 + h, 1), :]
    for s in range(n):
        br = pick(at.high_in[s], ny, -3) + yoff
        dr = pick(at.high_in[s], ny, -2) + yoff
        for h in range(2):
            for k in range(3):
                for probe in range(2):
                    i = (probe * 3 + k) * 2 + h
                    bw[probe, h, pl.ds(3 * wy + br + k, nx, stride=wy), :] = ys[s][pl.ds(i * nx, nx), :]
            for k in range(2):
                i = 12 + 2 * k + h
                dw[h, pl.ds(2 * wy + dr + k, nx, stride=wy), :] = 6.0 + ys[s][pl.ds(i * nx, nx), :]
    zero = jnp.zeros((wy, LANES), F32)
    for probe in range(2):
        for h in range(2):
            for i in (1, nx + 2):
                u2[probe, h, rows(i * wy, wy), :] = zero
                u3[probe, h, rows(i * wy, wy), :] = zero

    inside = row_mask(wy, at.fine)
    c0, (a1, c1), (a2, c2) = FINE[0][1], FINE[1], FINE[2]
    c1 = jnp.where(inside, c1, 0.0)
    c2 = jnp.where(inside, c2, 0.0)

    def step1(p):
        to = rows((p + 2) * wy, wy)
        d = [dw[h, to, :] for h in range(2)]
        for probe in range(2):
            v, av = fine_operator(bw, probe, p + 3, d, wy, masks)
            for h in range(2):
                res = v[h] - c0 * av[h]
                r1[probe, h, to, :] = res
                u2[probe, h, to, :] = (a1 * c0) * v[h] + c1 * res

    def step2(p):
        to = rows((p + 2) * wy, wy)
        d = [dw[h, to, :] for h in range(2)]
        for probe in range(2):
            v, av = fine_operator(u2, probe, p + 2, d, wy, masks)
            for h in range(2):
                res = r1[probe, h, to, :] - av[h]
                r1[probe, h, to, :] = res
                u3[probe, h, to, :] = a2 * v[h] + c2 * res

    mine = row_mask(wy, (yoff, yoff + ny))

    def step3(p):
        src = rows((p + 2) * wy, wy)
        to = rows(p * wy, wy)
        d = [dw[h, src, :] for h in range(2)]
        sums = []
        for probe in range(2):
            v, av = fine_operator(u3, probe, p + 2, d, wy, masks)
            total = None
            for h in range(2):
                out = jnp.where(mine, r1[probe, h, src, :] - av[h], 0.0)
                r_out[probe, h, to, :] = out
                sol_out[probe, h, to, :] = (
                    c0 * bw[probe, h, rows((p + 3) * wy, wy), :] + u2[probe, h, src, :] + v[h]
                )
                total = out if total is None else total + out
            sums.append(total)
        return sums

    def steps3(i, _):
        for k in range(2):
            low, high = step3(4 * i + 2 * k), step3(4 * i + 2 * k + 1)
            for probe in range(2):
                xs[k, probe] = low[probe] + high[probe]
        for k in range(2):
            for probe in range(2):
                pair = (
                    xs[k, probe, pl.ds(yoff, cy, stride=2), :] + xs[k, probe, pl.ds(yoff + 1, cy, stride=2), :]
                )
                coarse[probe, rows((2 * i + k) * cy, cy), :] = 0.5 * pair
        return 0

    @pl.when(at.has_l)
    def _():
        step1(-2)
        step1(-1)

    @pl.when(at.has_r)
    def _():
        step1(nx)
        step1(nx + 1)

    looped(step1, nx)

    @pl.when(at.has_l)
    def _():
        step2(-1)

    @pl.when(at.has_r)
    def _():
        step2(nx)

    looped(step2, nx)
    lax.fori_loop(0, nx // 4, steps3, 0)

    field = [coarse.at[0], coarse.at[1], cd]
    depth = [REACH, REACH, REACH - 1]
    for msg, corners, right in ((m_a, m_cas, at.even), (m_b, m_cbs, at.odd)):
        for f in range(3):
            size = depth[f] * cy
            msg[pl.ds(f * REACH * cy, size), :] = field[f][rows(edge(right, cx, depth[f]) * cy, size), :]
        for s in range(n):
            for m, (f, p, q) in enumerate(CORNER2):
                row = pick(at.high_out[s], cy - 1 - q, q) + pick(right, cx - 1 - p, p) * cy
                corners[s][pl.ds(m, 1), :] = field[f][pl.ds(row, 1), :]
            row = pick(at.high_out[s], yoff + ny - 1, yoff) + pick(right, nx - 1, 0) * wy
            for probe in range(2):
                for h in range(2):
                    i = len(CORNER2) + probe * 2 + h
                    corners[s][pl.ds(i, 1), :] = r_out[probe, h, pl.ds(row, 1), :]
            corners[s][pl.ds(sz.c2 - 3, 3), :] = jnp.zeros((3, LANES), F32)
        for probe in range(2):
            for h in range(2):
                for k in range(2):
                    i = (probe * 2 + h) * 2 + k
                    row = (edge(right, nx, 2) + k) * wy + yoff
                    msg[pl.ds(sz.x2_base + i * ny, ny), :] = r_out[probe, h, rows(row, ny), :]
    for s in range(n):
        for f in range(3):
            for k in range(depth[f]):
                row = edge(at.high_out[s], cy, depth[f]) + k
                m_ys[s][pl.ds((f * REACH + k) * cx, cx), :] = field[f][pl.ds(row, cx, stride=cy), :]
        row = edge(at.high_out[s], ny, 2) + yoff
        for probe in range(2):
            for h in range(2):
                for k in range(2):
                    i = (probe * 2 + h) * 2 + k
                    m_ys[s][pl.ds(sz.y2_base + i * nx, nx), :] = r_out[probe, h, pl.ds(row + k, nx, stride=wy), :]


def post_kernel(sz, *refs):
    n = sz.sides
    agg, r_in, sol_in, dw, coarse, cd, x_a, x_b = refs[:8]
    ys, cas, cbs = refs[8 : 8 + n], refs[8 + n : 8 + 2 * n], refs[8 + 2 * n : 8 + 3 * n]
    out = refs[8 + 3 * n]
    cw, cu, cc, st_g, st_u, rh, re, r1, u2, acc, ow, sem = refs[9 + 3 * n :]
    nx, ny, wy, cx, cy, wc = sz.nx, sz.ny, sz.wy, sz.cx, sz.cy, sz.wc
    at = Place(sz)
    yoff = at.yoff
    masks = lane_masks(wy)
    planes = cx + 2 * REACH

    zero8 = jnp.zeros((8, LANES), F32)
    zero_at = [pick(at.high_in[s], yoff + cy, yoff - 8) for s in range(n)]
    field = [coarse.at[0], coarse.at[1], cd]
    depth = [REACH, REACH, REACH - 1]
    for f in range(3):
        for p in range(planes):
            for z in zero_at:
                cw[f, rows(p * wc + z, 8), :] = zero8
        for x in range(cx):
            cw[f, rows((x + REACH) * wc + yoff, cy), :] = field[f][rows(x * cy, cy), :]
        for s in range(n):
            for k in range(depth[f]):
                row = pick(at.high_in[s], yoff + cy, yoff - depth[f]) + k
                cw[f, pl.ds(REACH * wc + row, cx, stride=wc), :] = ys[s][rows((f * REACH + k) * cx, cx), :]
        for msg, to_right in ((x_a, at.even), (x_b, at.odd)):
            first = jnp.where(to_right, REACH + cx, REACH - depth[f])
            for k in range(depth[f]):
                cw[f, rows((first + k) * wc + yoff, cy), :] = msg[rows((f * REACH + k) * cy, cy), :]
    for corners, to_right in ((cas, at.even), (cbs, at.odd)):
        for s in range(n):
            for m, (f, p, q) in enumerate(CORNER2):
                row = pick(at.high_in[s], yoff + cy + q, yoff - 1 - q)
                row = row + jnp.where(to_right, REACH + cx + p, REACH - 1 - p) * wc
                cw[f, pl.ds(row, 1), :] = corners[s][pl.ds(m, 1), :]

    cmasks = lane_masks(wc)
    inside = row_mask(wc, at.crs)
    i = at.i
    here = agg[i]
    link_l = (at.has_l & (agg[jnp.maximum(i - 1, 0)] == here)).astype(F32)
    link_r = (at.has_r & (agg[jnp.minimum(i + 1, sz.n_gx - 1)] == here)).astype(F32)
    for p in range(planes):
        to = pl.ds(p * wc, wc)
        for probe in range(2):
            u = jnp.where(inside, COARSE[0][1], 0.0) * cw[probe, to, :]
            cu[0, probe, to, :] = u
            cc[probe, to, :] = u
    for k in range(COARSE_DEG - 1):
        a, c = COARSE[k + 1]
        c = jnp.where(inside, c, 0.0)
        old, new = k % 2, 1 - k % 2
        for p in range(1 + k, planes - 1 - k):
            to = pl.ds(p * wc, wc)
            for probe in range(2):
                u = cu[old, probe, to, :]
                before = cu[old, probe, pl.ds((p - 1) * wc, wc), :]
                after = cu[old, probe, pl.ds((p + 1) * wc, wc), :]
                if p == REACH:
                    before = before * link_l
                if p == REACH - 1:
                    after = after * link_l
                if p == REACH + cx:
                    before = before * link_r
                if p == REACH + cx - 1:
                    after = after * link_r
                near = ((before + after) + y_sum(u)) + (below(u, cmasks) + above(u, cmasks))
                res = cw[probe, to, :] - (cw[2, to, :] * u - near)
                u = a * u + c * res
                if k + 2 < COARSE_DEG:
                    cw[probe, to, :] = res
                    cu[new, probe, to, :] = u
                cc[probe, to, :] = cc[probe, to, :] + u

    for msg, corners, to_right in ((x_a, cas, at.even), (x_b, cbs, at.odd)):
        for probe in range(2):
            for h in range(2):
                for k in range(2):
                    i = (probe * 2 + h) * 2 + k
                    base = (jnp.where(to_right, 2, 0) + k) * wy
                    rh[probe, h, rows(base + yoff, ny), :] = msg[pl.ds(sz.x2_base + i * ny, ny), :]
                    for s in range(n):
                        zero_row = pick(at.high_in[s], yoff + ny, yoff - 8)
                        rh[probe, h, rows(base + zero_row, 8), :] = zero8
                for s in range(n):
                    row = pick(at.high_in[s], yoff + ny, yoff - 1) + jnp.where(to_right, 2, 1) * wy
                    i = len(CORNER2) + probe * 2 + h
                    rh[probe, h, pl.ds(row, 1), :] = corners[s][pl.ds(i, 1), :]

    c0, (a1, c1), (a2, c2) = FINE[0][1], FINE[1], FINE[2]
    valid = row_mask(wy, at.valid)

    def spread(q, r_ref, r_plane, own):
        for probe in range(2):
            u = cc[probe, rows((q + REACH) * wc, wc), :]
            sides = [cc[probe, rows((q + REACH - 1 + 2 * k) * wc, wc), :] for k in range(2)]
            u3 = 3.0 * u
            shifted = [pltpu.roll(u, 1, 0), pltpu.roll(u, wc - 1, 0)]
            for row in range(2):
                st_u[probe, pl.ds(row, wc, stride=2), :] = u
            for h in range(2):
                g = u3 + (above(u, cmasks) if h else below(u, cmasks))
                for k in range(2):
                    for row in range(2):
                        st_g[probe, h, k, pl.ds(row, wc, stride=2), :] = (g + sides[k]) + shifted[row]
        for k in range(2):
            to = rows((2 * q + k + 2) * wy, wy)
            for h in range(2):
                d = dw[h, to, :]
                for probe in range(2):
                    u = st_u[probe, rows(yoff, wy), :]
                    old = r_ref[probe, h, rows((r_plane + k) * wy, wy), :]
                    res = (old - d * u) + st_g[probe, h, k, rows(yoff, wy), :]
                    res = jnp.where(valid, res, 0.0)
                    re[probe, h, to, :] = res
                    if own:
                        mine = rows((2 * q + k) * wy, wy)
                        acc[probe, h, mine, :] = (sol_in[probe, h, mine, :] + u) + c0 * res

    def own_planes(q):
        spread(q, r_in, 2 * q, True)

    looped(own_planes, cx, 2)
    zero = jnp.zeros((wy, LANES), F32)
    for has, q, first in ((at.has_l, -1, 0), (at.has_r, cx, 2)):

        @pl.when(has)
        def _():
            spread(q, rh, first, False)

        @pl.when(jnp.logical_not(has))
        def _():
            for probe in range(2):
                for h in range(2):
                    for k in range(2):
                        re[probe, h, rows((2 * q + 2 + k) * wy, wy), :] = zero
                        u2[probe, h, rows((2 * q + 2 + k) * wy, wy), :] = zero

    for s in range(n):
        row = pick(at.high_in[s], yoff + ny, yoff - 2)
        for probe in range(2):
            for h in range(2):
                for k in range(2):
                    i = (probe * 2 + h) * 2 + k
                    to = pl.ds(2 * wy + row + k, nx, stride=wy)
                    re[probe, h, to, :] = re[probe, h, to, :] + ys[s][pl.ds(sz.y2_base + i * nx, nx), :]

    c1 = jnp.where(row_mask(wy, at.fine), c1, 0.0)

    def step1(p):
        to = rows((p + 2) * wy, wy)
        d = [dw[h, to, :] for h in range(2)]
        for probe in range(2):
            v, av = fine_operator(re, probe, p + 2, d, wy, masks)
            for h in range(2):
                res = v[h] - c0 * av[h]
                r1[probe, h, to, :] = res
                u2[probe, h, to, :] = (a1 * c0) * v[h] + c1 * res

    join = parity_matrix(True)

    def steps2(i, _):
        width = 4
        for probe in range(2):
            done = []
            for k in range(width):
                p = width * i + k
                to = rows((p + 2) * wy, wy)
                d = [dw[h, to, :] for h in range(2)]
                v, av = fine_operator(u2, probe, p + 2, d, wy, masks)
                parts = []
                for h in range(2):
                    res = r1[probe, h, to, :] - av[h]
                    parts.append(acc[probe, h, rows(p * wy, wy), :] + ((1.0 + a2) * v[h] + c2 * res))
                done.append(jnp.concatenate(parts, axis=1))
            joined = permute_lanes(jnp.concatenate(done, axis=0), join, 2)
            for k in range(width):
                ow[probe, width * i + k] = joined[k * wy : (k + 1) * wy]
        return 0

    @pl.when(at.has_l)
    def _():
        step1(-1)

    @pl.when(at.has_r)
    def _():
        step1(nx)

    looped(step1, nx)
    pieces = 4
    size = nx // pieces
    copies = []
    for i in range(pieces):
        lax.fori_loop(i * size // 4, (i + 1) * size // 4, steps2, 0)
        copy = pltpu.make_async_copy(
            ow.at[:, pl.ds(i * size, size), rows(yoff, ny), :], out.at[:, pl.ds(i * size, size)], sem.at[i]
        )
        copy.start()
        copies.append(copy)
    for copy in copies:
        copy.wait()


def on_device(n_gx, n_gy, right_side, diagonal, aggregates):
    nx, ny, nz = right_side.shape[1:]
    sz = Sizes(nx, ny, nz, n_gx, n_gy)
    n, wy, wc, cx = sz.sides, sz.wy, sz.wc, sz.cx

    pairs_a = [(k, k ^ 1) for k in range(n_gx)]
    pairs_b = [(k, k + 1) for k in range(1, n_gx - 1, 2)] + [(k + 1, k) for k in range(1, n_gx - 1, 2)]
    along = [[(0, 1), (1, 0)]] if sz.two else [
        [(k, k - 1) for k in range(1, n_gy)],
        [(k, k + 1) for k in range(n_gy - 1)],
    ]

    def both(pairs, perm):
        return [(a * n_gy + c, b * n_gy + d) for a, b in pairs for c, d in perm]

    def exchange(messages):
        m_a, m_b, rest = messages[0], messages[1], messages[2:]
        got = [lax.ppermute(m_a, "gx", pairs_a), lax.ppermute(m_b, "gx", pairs_b)]
        got += [lax.ppermute(rest[s], "gy", along[s]) for s in range(n)]
        got += [lax.ppermute(rest[n + s], ("gx", "gy"), both(pairs_a, along[s])) for s in range(n)]
        got += [lax.ppermute(rest[2 * n + s], ("gx", "gy"), both(pairs_b, along[s])) for s in range(n)]
        return got

    smem = pl.BlockSpec(memory_space=pltpu.SMEM)
    vmem = pl.BlockSpec(memory_space=pltpu.VMEM)
    hbm = pl.BlockSpec(memory_space=pltpu.HBM)
    params = pltpu.CompilerParams(vmem_limit_bytes=24 << 20)

    def shape(*dims):
        return jax.ShapeDtypeStruct(dims, F32)

    def messages(x, y, c):
        return [shape(x, LANES)] * 2 + [shape(y, LANES)] * n + [shape(c, LANES)] * (2 * n)

    packed = pl.pallas_call(
        functools.partial(pack_kernel, sz),
        in_specs=[hbm] * 2,
        out_specs=[vmem] * (2 + 3 * n),
        out_shape=messages(sz.x1, sz.y1, sz.c1),
        scratch_shapes=[
            pltpu.VMEM((2, 2, 3, ny, nz), F32),
            pltpu.VMEM((2, 2, ny, nz), F32),
            pltpu.VMEM((n, 2, nx, 8, nz), F32),
            pltpu.VMEM((n, nx, 8, nz), F32),
            pltpu.VMEM((n, 2, 2 * nx * 8, LANES), F32),
            pltpu.VMEM((n, 2, nx * 8, LANES), F32),
            pltpu.SemaphoreType.DMA((2 * n + 4,)),
        ],
        compiler_params=pltpu.CompilerParams(vmem_limit_bytes=120 << 19),
        name="pack_kernel",
    )(right_side, diagonal)
    halos = exchange(packed)
    bw, dw, cd = pl.pallas_call(
        functools.partial(open_kernel, sz),
        in_specs=[pl.BlockSpec(memory_space=pl.ANY), hbm, hbm],
        out_specs=[vmem] * 3,
        out_shape=[shape(*sz.bw), shape(*sz.dw), shape(sz.coarse, LANES)],
        scratch_shapes=[
            pltpu.VMEM((2, nx, ny, nz), F32),
            pltpu.VMEM((nx, ny, nz), F32),
            pltpu.VMEM((2, ny, LANES), F32),
            pltpu.SemaphoreType.DMA((4, 2)),
        ],
        compiler_params=params,
        name="open_kernel",
    )(packed[-1], right_side, diagonal)
    results = pl.pallas_call(
        functools.partial(pre_kernel, sz),
        in_specs=[vmem] * (5 + 3 * n),
        out_specs=[vmem] * (7 + 3 * n),
        out_shape=[shape(*sz.bw), shape(*sz.dw), shape(*sz.brick), shape(*sz.brick), shape(2, sz.coarse, LANES)]
        + messages(sz.x2, sz.y2, sz.c2),
        scratch_shapes=[pltpu.VMEM((2, 2, (nx + 4) * wy, LANES), F32)] * 3 + [pltpu.VMEM((2, 2, wy, LANES), F32)],
        input_output_aliases={0: 0, 1: 1},
        compiler_params=params,
        name="pre_smooth",
    )(bw, dw, cd, *halos)
    dw, r_own, sol, coarse = results[1:5]
    halos = exchange(results[5:])
    planes = cx + 2 * REACH
    return pl.pallas_call(
        functools.partial(post_kernel, sz),
        in_specs=[smem] + [vmem] * (7 + 3 * n),
        out_specs=hbm,
        out_shape=shape(2, nx, ny, nz),
        scratch_shapes=[
            pltpu.VMEM((3, planes * wc, LANES), F32),
            pltpu.VMEM((2, 2, planes * wc, LANES), F32),
            pltpu.VMEM((2, planes * wc, LANES), F32),
            pltpu.VMEM((2, 2, 2, 2 * wc, LANES), F32),
            pltpu.VMEM((2, 2 * wc, LANES), F32),
            pltpu.VMEM((2, 2, 4 * wy, LANES), F32),
        ]
        + [pltpu.VMEM((2, 2, (nx + 4) * wy, LANES), F32)] * 3
        + [
            pltpu.VMEM(sz.brick, F32),
            pltpu.VMEM((2, nx, wy, nz), F32),
            pltpu.SemaphoreType.DMA((4,)),
        ],
        compiler_params=params,
        name="correct_and_smooth",
    )(aggregates, r_own, sol, dw, coarse, cd, *halos)


def solution(mesh):
    return jax.shard_map(
        functools.partial(on_device, mesh.shape["gx"], mesh.shape["gy"]),
        mesh=mesh,
        in_specs=(P(None, "gx", "gy", None), P("gx", "gy", None), P()),
        out_specs=P(None, "gx", "gy", None),
        check_vma=False,
    )
```

time: 210 us -> 47.6 us (0.23)
  the two profiles are of different devices: /device:TPU:21 before, /device:TPU:17 now
where the time goes in v2:
time: 47.6 us; the launch traced here: 47.4 us
  Pallas kernels  23 us (48%)
  starting transfers between devices  18.2 us (38%)
  waiting for transfers between devices  5.28 us (11%)
  local copies, waits for them, and re-layouts  0.73 us (2%)
    pallas_call x1, Pallas kernels, on_device(): pl.pallas_call(functools.partial(post_kernel, sz), in_specs=[smem] + [vme...  11 us
    ppermute x4, starting transfers between devices, exchange(): got = [lax.ppermute(m_a, 'gx', pairs_a), lax.ppermute(m_b, 'gx', pairs_b)]  7.29 us
    ppermute x2, starting transfers between devices, exchange(): lax.ppermute(rest[2 * n + s], ('gx', 'gy'), both(pairs_b, along[s]))  7.21 us
    pallas_call x1, Pallas kernels, on_device(): pl.pallas_call(functools.partial(pre_kernel, sz), in_specs=[vmem] * (5 +...  5.64 us
    ppermute x2, waiting for transfers between devices, exchange(): lax.ppermute(rest[n + s], ('gx', 'gy'), both(pairs_a, along[s]))  5.26 us
    pallas_call x1, Pallas kernels, on_device(): pl.pallas_call(functools.partial(pack_kernel, sz), in_specs=[hbm] * 2, ou...  3.22 us
    pallas_call x1, Pallas kernels, on_device(): pl.pallas_call(functools.partial(open_kernel, sz), in_specs=[pl.BlockSpec...  3.17 us
    ppermute x2, starting transfers between devices, exchange(): lax.ppermute(rest[n + s], ('gx', 'gy'), both(pairs_a, along[s]))  2 us
  transfers between devices with their start and end apart: 10, of which 1 were waited for; matrix products, arithmetic and copies ran while one was open for 0% of the time, Pallas kernels for 7%

profile of v2, /device:TPU:17, one launch (start us, length us, event | category | flops | bytes accessed | tf_op | source)
XLA Modules:
  0.0 47.4 jit_solution(8305399785915100039)
XLA Ops:
  0.0 0.0 copy-start.1
  0.0 0.0 copy-start
  0.0 3.2 %pack_kernel.1 = (f32[512,128]{1,0:T(8,128)}, f32[512,128]{1,0:T(8,128)}, f32[512,128]{1,0:T(8,128)}, f32[16,128]{1,0:T(8,128)}, f32[16,128]{1,0:T(8,128)}) custom-call(f32[2,32,32,256]{3,2,1,0:T(8,128)} %rhs.1, f32[32,32,256]{2,1,0:T(8,128)} %diag.1), custom_call_target="tpu_custom_call" | custom-call | tf_op jit(solution)/shard_map/pack_kernel/pallas_call | solution.py:694
  3.2 0.7 %collective-permute-start = (f32[512,128]{1,0:T(8,128)}, f32[512,128]{1,0:T(8,128)S(1)}, u32[]{:S(2)}, u32[]{:S(2)}) collective-permute-start(f32[512,128]{1,0:T(8,128)} %get-tuple-element.26), channel_id=1, source_target_pairs={{0,2},{2,0},{4,6},{6,4},{8,10},{10,8},{12,14},{14,12},{16,18},{18,... | collective-permute-start | bytes 786440 | tf_op jit(solution)/shard_map/ppermute | solution.py:677
  4.0 3.0 %collective-permute-start.1 = (f32[512,128]{1,0:T(8,128)}, f32[512,128]{1,0:T(8,128)S(1)}, u32[]{:S(2)}, u32[]{:S(2)}) collective-permute-start(f32[512,128]{1,0:T(8,128)} %get-tuple-element.27), channel_id=1, source_target_pairs={{2,4},{6,8},{10,12},{14,16},{18,20},{22,24},{26,28},{4,2},{8,6},{1... | collective-permute-start | bytes 786440 | tf_op jit(solution)/shard_map/ppermute | solution.py:677
  7.0 1.3 %collective-permute-start.2 = (f32[512,128]{1,0:T(8,128)}, f32[512,128]{1,0:T(8,128)S(1)}, u32[]{:S(2)}, u32[]{:S(2)}) collective-permute-start(f32[512,128]{1,0:T(8,128)} %get-tuple-element.28), channel_id=1, source_target_pairs={{0,1},{1,0},{2,3},{3,2},{4,5},{5,4},{6,7},{7,6},{8,9},{9,8},{10,11... | collective-permute-start | bytes 786440 | tf_op jit(solution)/shard_map/ppermute | solution.py:678
  8.3 0.8 %collective-permute-start.3 = (f32[16,128]{1,0:T(8,128)}, f32[16,128]{1,0:T(8,128)S(1)}, u32[]{:S(2)}, u32[]{:S(2)}) collective-permute-start(f32[16,128]{1,0:T(8,128)} %get-tuple-element.29), channel_id=1, source_target_pairs={{0,3},{1,2},{2,1},{3,0},{4,7},{5,6},{6,5},{7,4},{8,11},{9,10},{10,... | collective-permute-start | bytes 24584 | tf_op jit(solution)/shard_map/ppermute | solution.py:679
  9.1 3.9 %collective-permute-start.4 = (f32[16,128]{1,0:T(8,128)}, f32[16,128]{1,0:T(8,128)S(1)}, u32[]{:S(2)}, u32[]{:S(2)}) collective-permute-start(f32[16,128]{1,0:T(8,128)} %get-tuple-element.22.first), channel_id=1, source_target_pairs={{2,5},{3,4},{6,9},{7,8},{10,13},{11,12},{14,17},{15,16},{18,21},{1... | collective-permute-start | bytes 24584 | tf_op jit(solution)/shard_map/ppermute | solution.py:680
  12.9 0.0 copy-done.1
  12.9 0.0 copy-done
  13.0 0.0 copy-start.2
  13.0 0.7 %copy-done.2 = f32[16,128]{1,0:T(8,128)S(1)} copy-done((f32[16,128]{1,0:T(8,128)S(1)}, f32[16,128]{1,0:T(8,128)}, u32[]{:S(2)}) %copy-start.2) | copy-done | bytes 8216
  13.7 3.2 %open_kernel.1 = (f32[2,2,1520,128]{3,2,1,0:T(8,128)S(1)}, f32[2,1440,128]{2,1,0:T(8,128)S(1)}, f32[256,128]{1,0:T(8,128)S(1)}) custom-call(f32[16,128]{1,0:T(8,128)S(1)} %copy-done.2, f32[2,32,32,256]{3,2,1,0:T(8,128)S(1)} %copy-done, f32[32,32,256]{2,1,0:T(8,128)S(1)} %copy-done.1), custom_call_target="tpu_custom_call" | custom-call | tf_op jit(solution)/shard_map/open_kernel/pallas_call | solution.py:712
  16.9 0.0 collective-permute-done.3.refs_6_
  16.9 0.0 collective-permute-done.4.refs_7_
  16.9 0.0 collective-permute-done.refs_3_
  16.9 0.0 collective-permute-done.1.refs_4_
  16.9 0.0 collective-permute-done.2.refs_5_
  16.9 0.0 copy-start.3
  16.9 5.6 %pre_smooth.1 = (f32[2,2,1520,128]{3,2,1,0:T(8,128)S(1)}, f32[2,1440,128]{2,1,0:T(8,128)S(1)}, f32[2,2,1280,128]{3,2,1,0:T(8,128)S(1)}, f32[2,2,1280,128]{3,2,1,...) custom-call(f32[2,2,1520,128]{3,2,1,0:T(8,128)S(1)} %get-tuple-eleme, ...), custom_call_target="tpu_custom_call", output_to_operand_aliasing={{0}: (0, {}), {1}: (1, {})} | custom-call | tf_op jit(solution)/shard_map/pre_smooth/pallas_call | solution.py:726
  22.6 0.1 collective-permute-start.5
  22.7 3.5 %collective-permute-start.6 = (f32[576,128]{1,0:T(8,128)S(1)}, f32[576,128]{1,0:T(8,128)S(1)}, u32[]{:S(2)}, u32[]{:S(2)}) collective-permute-start(f32[576,128]{1,0:T(8,128)S(1)} %get-tuple-element.35), channel_id=1, source_target_pairs={{2,4},{6,8},{10,12},{14,16},{18,20},{22,24},{26,28},{4,2},{8,6},{1... | collective-permute-start | bytes 884744 | tf_op jit(solution)/shard_map/ppermute | solution.py:677
  26.1 0.4 collective-permute-start.7
  26.5 1.2 %collective-permute-start.8 = (f32[64,128]{1,0:T(8,128)S(1)}, f32[64,128]{1,0:T(8,128)S(1)}, u32[]{:S(2)}, u32[]{:S(2)}) collective-permute-start(f32[64,128]{1,0:T(8,128)S(1)} %get-tuple-element.37), channel_id=1, source_target_pairs={{0,3},{1,2},{2,1},{3,0},{4,7},{5,6},{6,5},{7,4},{8,11},{9,10},{10,... | collective-permute-start | bytes 98312 | tf_op jit(solution)/shard_map/ppermute | solution.py:679
  27.7 3.3 %collective-permute-start.9 = (f32[64,128]{1,0:T(8,128)S(1)}, f32[64,128]{1,0:T(8,128)S(1)}, u32[]{:S(2)}, u32[]{:S(2)}) collective-permute-start(f32[64,128]{1,0:T(8,128)S(1)} %get-tuple-element.38), channel_id=1, source_target_pairs={{2,5},{3,4},{6,9},{7,8},{10,13},{11,12},{14,17},{15,16},{18,21},{1... | collective-permute-start | bytes 98312 | tf_op jit(solution)/shard_map/ppermute | solution.py:680
  31.1 5.3 %collective-permute-done.8.refs_9_ = f32[64,128]{1,0:T(8,128)S(1)} collective-permute-done((f32[64,128]{1,0:T(8,128)S(1)}, f32[64,128]{1,0:T(8,128)S(1)}, u32[]{:S(2)}, u32[]{:S(2)}) %collective-permute-start.8) | collective-permute-done | bytes 32800 | tf_op jit(solution)/shard_map/ppermute | solution.py:679
  36.3 0.0 collective-permute-done.9.refs_10_
  36.3 0.0 collective-permute-done.5.refs_6_
  36.3 0.0 collective-permute-done.6.refs_7_
  36.4 0.0 collective-permute-done.7.refs_8_
  36.4 0.0 copy-done.3
  36.4 11.0 %correct_and_smooth.1 = f32[2,32,32,256]{3,2,1,0:T(8,128)} custom-call(s32[16]{0:T(128)S(1)} %copy-done.3, f32[2,2,1280,128]{3,2,1,0:T(8,128)S(1)} %get-tuple-element.30.refs_1_, f32[2,2,1280,128]{3,2,1,0:T(8,128)S(1)} %get-tuple-element.31.refs_2_, f32[2,1440,128]{2,1,0:T(8,128)S(1)} %get-tuple-element.32.refs_3_, ...), custom_call_target="tpu_custom_call" | custom-call | tf_op jit(solution)/shard_map/correct_and_smooth/pallas_call | solution.py:740
Async XLA Ops:
  0.0 12.9 %copy-start.1 = (f32[32,32,256]{2,1,0:T(8,128)S(1)}, f32[32,32,256]{2,1,0:T(8,128)}, u32[]{:S(2)}) copy-start(f32[32,32,256]{2,1,0:T(8,128)} %diag.1) | copy-start | bytes 3145732
  0.0 12.9 %copy-start = (f32[2,32,32,256]{3,2,1,0:T(8,128)S(1)}, f32[2,32,32,256]{3,2,1,0:T(8,128)}, u32[]{:S(2)}) copy-start(f32[2,32,32,256]{3,2,1,0:T(8,128)} %rhs.1) | copy-start | bytes 6291460
  3.2 13.6 %collective-permute-start = (f32[512,128]{1,0:T(8,128)}, f32[512,128]{1,0:T(8,128)S(1)}, u32[]{:S(2)}, u32[]{:S(2)}) collective-permute-start(f32[512,128]{1,0:T(8,128)} %get-tuple-element.26), channel_id=1, source_target_pairs={{0,2},{2,0},{4,6},{6,4},{8,10},{10,8},{12,14},{14,12},{16,18},{18,... | collective-permute-start | bytes 786440 | tf_op jit(solution)/shard_map/ppermute | solution.py:677
  4.0 12.9 %collective-permute-start.1 = (f32[512,128]{1,0:T(8,128)}, f32[512,128]{1,0:T(8,128)S(1)}, u32[]{:S(2)}, u32[]{:S(2)}) collective-permute-start(f32[512,128]{1,0:T(8,128)} %get-tuple-element.27), channel_id=1, source_target_pairs={{2,4},{6,8},{10,12},{14,16},{18,20},{22,24},{26,28},{4,2},{8,6},{1... | collective-permute-start | bytes 786440 | tf_op jit(solution)/shard_map/ppermute | solution.py:677
  7.0 9.9 %collective-permute-start.2 = (f32[512,128]{1,0:T(8,128)}, f32[512,128]{1,0:T(8,128)S(1)}, u32[]{:S(2)}, u32[]{:S(2)}) collective-permute-start(f32[512,128]{1,0:T(8,128)} %get-tuple-element.28), channel_id=1, source_target_pairs={{0,1},{1,0},{2,3},{3,2},{4,5},{5,4},{6,7},{7,6},{8,9},{9,8},{10,11... | collective-permute-start | bytes 786440 | tf_op jit(solution)/shard_map/ppermute | solution.py:678
  8.3 8.6 %collective-permute-start.3 = (f32[16,128]{1,0:T(8,128)}, f32[16,128]{1,0:T(8,128)S(1)}, u32[]{:S(2)}, u32[]{:S(2)}) collective-permute-start(f32[16,128]{1,0:T(8,128)} %get-tuple-element.29), channel_id=1, source_target_pairs={{0,3},{1,2},{2,1},{3,0},{4,7},{5,6},{6,5},{7,4},{8,11},{9,10},{10,... | collective-permute-start | bytes 24584 | tf_op jit(solution)/shard_map/ppermute | solution.py:679
  9.1 7.8 %collective-permute-start.4 = (f32[16,128]{1,0:T(8,128)}, f32[16,128]{1,0:T(8,128)S(1)}, u32[]{:S(2)}, u32[]{:S(2)}) collective-permute-start(f32[16,128]{1,0:T(8,128)} %get-tuple-element.22.first), channel_id=1, source_target_pairs={{2,5},{3,4},{6,9},{7,8},{10,13},{11,12},{14,17},{15,16},{18,21},{1... | collective-permute-start | bytes 24584 | tf_op jit(solution)/shard_map/ppermute | solution.py:680
  13.0 0.7 %copy-start.2 = (f32[16,128]{1,0:T(8,128)S(1)}, f32[16,128]{1,0:T(8,128)}, u32[]{:S(2)}) copy-start(f32[16,128]{1,0:T(8,128)} %get-tuple-element.22.first) | copy-start | bytes 24580
  16.9 19.5 %copy-start.3 = (s32[16]{0:T(128)S(1)}, s32[16]{0:T(128)}, u32[]{:S(2)}) copy-start(s32[16]{0:T(128)} %refs_0_.3) | copy-start | bytes 196
  22.6 13.8 %collective-permute-start.5 = (f32[576,128]{1,0:T(8,128)S(1)}, f32[576,128]{1,0:T(8,128)S(1)}, u32[]{:S(2)}, u32[]{:S(2)}) collective-permute-start(f32[576,128]{1,0:T(8,128)S(1)} %get-tuple-element.34), channel_id=1, source_target_pairs={{0,2},{2,0},{4,6},{6,4},{8,10},{10,8},{12,14},{14,12},{16,18},{18,... | collective-permute-start | bytes 884744 | tf_op jit(solution)/shard_map/ppermute | solution.py:677
  22.7 13.7 %collective-permute-start.6 = (f32[576,128]{1,0:T(8,128)S(1)}, f32[576,128]{1,0:T(8,128)S(1)}, u32[]{:S(2)}, u32[]{:S(2)}) collective-permute-start(f32[576,128]{1,0:T(8,128)S(1)} %get-tuple-element.35), channel_id=1, source_target_pairs={{2,4},{6,8},{10,12},{14,16},{18,20},{22,24},{26,28},{4,2},{8,6},{1... | collective-permute-start | bytes 884744 | tf_op jit(solution)/shard_map/ppermute | solution.py:677
  26.1 10.2 %collective-permute-start.7 = (f32[576,128]{1,0:T(8,128)S(1)}, f32[576,128]{1,0:T(8,128)S(1)}, u32[]{:S(2)}, u32[]{:S(2)}) collective-permute-start(f32[576,128]{1,0:T(8,128)S(1)} %get-tuple-element.36), channel_id=1, source_target_pairs={{0,1},{1,0},{2,3},{3,2},{4,5},{5,4},{6,7},{7,6},{8,9},{9,8},{10,11... | collective-permute-start | bytes 884744 | tf_op jit(solution)/shard_map/ppermute | solution.py:678
  26.5 9.8 %collective-permute-start.8 = (f32[64,128]{1,0:T(8,128)S(1)}, f32[64,128]{1,0:T(8,128)S(1)}, u32[]{:S(2)}, u32[]{:S(2)}) collective-permute-start(f32[64,128]{1,0:T(8,128)S(1)} %get-tuple-element.37), channel_id=1, source_target_pairs={{0,3},{1,2},{2,1},{3,0},{4,7},{5,6},{6,5},{7,4},{8,11},{9,10},{10,... | collective-permute-start | bytes 98312 | tf_op jit(solution)/shard_map/ppermute | solution.py:679
  27.7 8.6 %collective-permute-start.9 = (f32[64,128]{1,0:T(8,128)S(1)}, f32[64,128]{1,0:T(8,128)S(1)}, u32[]{:S(2)}, u32[]{:S(2)}) collective-permute-start(f32[64,128]{1,0:T(8,128)S(1)} %get-tuple-element.38), channel_id=1, source_target_pairs={{2,5},{3,4},{6,9},{7,8},{10,13},{11,12},{14,17},{15,16},{18,21},{1... | collective-permute-start | bytes 98312 | tf_op jit(solution)/shard_map/ppermute | solution.py:680

commit v3 on v2

--- a/solution.py
+++ b/solution.py
@@ -145,23 +145,46 @@
     return total
 
 
-def fine_operator(ref, probe, plane, diag, wy, masks):
-    v = [ref[probe, h, rows(plane * wy, wy), :] for h in range(2)]
-    z = z_sum(v[0], v[1], masks)
-    res = []
-    for h in range(2):
-        x = ref[probe, h, rows((plane - 1) * wy, wy), :] + ref[probe, h, rows((plane + 1) * wy, wy), :]
-        res.append(diag[h] * v[h] - ((x + y_sum(v[h])) + z[h]))
-    return v, res
+def sweep(ref, shift, dw, first, count, wy, masks, use):
+    for probe in range(2):
+
+        def load(plane):
+            return [ref[probe, h, rows((plane + shift) * wy, wy), :] for h in range(2)]
+
+        before, now = load(first - 1), load(first)
+        for k in range(count):
+            plane = first + k
+            at = plane + shift
+            after = load(plane + 1)
+            z = z_sum(now[0], now[1], masks)
+            res = []
+            for h in range(2):
+                y = pltpu.roll(now[h], 1, 0) + ref[probe, h, pl.ds(at * wy + 1, wy), :]
+                d = dw[h, rows((plane + 2) * wy, wy), :]
+                res.append(d * now[h] - (((before[h] + after[h]) + y) + z[h]))
+            use(probe, plane, now, res)
+            before, now = now, after
 
 
 def looped(step, count, width=4):
     def body(i, _):
-        for k in range(width):
-            step(width * i + k)
+        step(width * i, width)
         return 0
 
     lax.fori_loop(0, count // width, body, 0)
+
+
+ORDER1 = "aby"
+ORDER2 = "yba"
+
+
+def sorted_messages(sz, order, refs):
+    found, k = {}, 0
+    for name in order:
+        count = sz.sides if name == "y" else 1
+        found[name] = refs[k : k + count]
+        k += count
+    return found["y"], found["b"][0], found["a"][0]
 
 
 HALF = [slice(0, LANES), slice(LANES, 2 * LANES)]
@@ -171,8 +194,9 @@
 
 def pack_kernel(sz, *refs):
     n = sz.sides
-    rhs, diag, m_a, m_b = refs[:4]
-    m_ys, m_cas, m_cbs = refs[4 : 4 + n], refs[4 + n : 4 + 2 * n], refs[4 + 2 * n : 4 + 3 * n]
+    rhs, diag = refs[:2]
+    m_ys, m_b, m_a = sorted_messages(sz, ORDER1, refs[2 : 4 + n])
+    m_cas, m_cbs = refs[4 + n : 4 + 2 * n], refs[4 + 2 * n : 4 + 3 * n]
     xr, xd, yr, yd, tr, td, sem = refs[4 + 3 * n :]
     nx, ny = sz.nx, sz.ny
     at = Place(sz)
@@ -194,8 +218,8 @@
     for copy in copies[: 2 * n]:
         copy.wait()
     for s in range(n):
-        v = permute_lanes(yr[s].reshape(2 * nx * 8, 2 * LANES), split, 3)
-        d = permute_lanes(yd[s].reshape(nx * 8, 2 * LANES), split, 3)
+        v = permute_lanes(yr[s].reshape(2 * nx * 8, 2 * LANES), split, 2)
+        d = permute_lanes(yd[s].reshape(nx * 8, 2 * LANES), split, 2)
         for h in range(2):
             tr[s, h] = v[:, HALF[h]]
             td[s, h] = d[:, HALF[h]]
@@ -220,8 +244,8 @@
     for copy in copies[2 * n :]:
         copy.wait()
     for e, msg in enumerate((m_a, m_b)):
-        v = permute_lanes(xr[e].reshape(6 * ny, 2 * LANES), split, 3)
-        d = permute_lanes(xd[e].reshape(2 * ny, 2 * LANES), split, 3)
+        v = permute_lanes(xr[e].reshape(6 * ny, 2 * LANES), split, 2)
+        d = permute_lanes(xd[e].reshape(2 * ny, 2 * LANES), split, 2)
         for k in range(6):
             for h in range(2):
                 msg[pl.ds((2 * k + h) * ny, ny), :] = v[k * ny : (k + 1) * ny, HALF[h]]
@@ -230,32 +254,18 @@
                 msg[pl.ds((12 + 2 * k + h) * ny, ny), :] = d[k * ny : (k + 1) * ny, HALF[h]]
 
 
-def open_kernel(sz, first, rhs, diag, bw, dw, cd, rb, db, xs, sem):
-    del first
+def open_kernel(sz, rhs, diag, bw, dw, cd, xs):
     nx, ny, wy, cy = sz.nx, sz.ny, sz.wy, sz.cy
     at = Place(sz)
     split = parity_matrix(False)
     zero8 = jnp.zeros((8, LANES), F32)
     zero_at = [pick(at.high_in[s], at.yoff + ny, at.yoff - 8) for s in range(sz.sides)]
     width = 4
-    pieces = 4
-    size = nx // pieces
-    copies = []
-    for i in range(pieces):
-        part = pl.ds(i * size, size)
-        copies.append(
-            (
-                pltpu.make_async_copy(rhs.at[:, part], rb.at[:, part], sem.at[i, 0]),
-                pltpu.make_async_copy(diag.at[part], db.at[part], sem.at[i, 1]),
-            )
-        )
-        for copy in copies[-1]:
-            copy.start()
 
     def body(i, _):
         for f in range(3):
-            src = db[pl.ds(width * i, width)] if f == 2 else rb[f, pl.ds(width * i, width)]
-            v = permute_lanes(src.reshape(width * ny, 2 * LANES), split, 3)
+            src = diag[pl.ds(width * i, width)] if f == 2 else rhs[f, pl.ds(width * i, width)]
+            v = permute_lanes(src.reshape(width * ny, 2 * LANES), split, 2)
             if f == 2:
                 v = v + 6.0
             for k in range(width):
@@ -276,19 +286,18 @@
                     cd[rows((i * (width // 2) + k) * cy, cy), :] = 0.5 * pair - 18.0
         return 0
 
-    for i in range(pieces):
-        for copy in copies[i]:
-            copy.wait()
-        lax.fori_loop(i * size // width, (i + 1) * size // width, body, 0)
+    lax.fori_loop(0, nx // width, body, 0)
 
 
 def pre_kernel(sz, *refs):
     n = sz.sides
-    cd, xa, xb = refs[2:5]
-    ys, cas, cbs = refs[5 : 5 + n], refs[5 + n : 5 + 2 * n], refs[5 + 2 * n : 5 + 3 * n]
+    cd = refs[2]
+    ys, xb, xa = sorted_messages(sz, ORDER1, refs[3 : 5 + n])
+    cas, cbs = refs[5 + n : 5 + 2 * n], refs[5 + 2 * n : 5 + 3 * n]
     outs = refs[5 + 3 * n :]
-    bw, dw, r_out, sol_out, coarse, m_a, m_b = outs[:7]
-    m_ys, m_cas, m_cbs = outs[7 : 7 + n], outs[7 + n : 7 + 2 * n], outs[7 + 2 * n : 7 + 3 * n]
+    bw, dw, r_out, sol_out, coarse = outs[:5]
+    m_ys, m_b, m_a = sorted_messages(sz, ORDER2, outs[5 : 7 + n])
+    m_cas, m_cbs = outs[7 + n : 7 + 2 * n], outs[7 + 2 * n : 7 + 3 * n]
     r1, u2, u3, xs = outs[7 + 3 * n :]
     nx, ny, wy, cx, cy = sz.nx, sz.ny, sz.wy, sz.cx, sz.cy
     at = Place(sz)
@@ -342,35 +351,34 @@
     c1 = jnp.where(inside, c1, 0.0)
     c2 = jnp.where(inside, c2, 0.0)
 
-    def step1(p):
-        to = rows((p + 2) * wy, wy)
-        d = [dw[h, to, :] for h in range(2)]
-        for probe in range(2):
-            v, av = fine_operator(bw, probe, p + 3, d, wy, masks)
+    def step1(first, count):
+        def use(probe, p, v, av):
+            to = rows((p + 2) * wy, wy)
             for h in range(2):
                 res = v[h] - c0 * av[h]
                 r1[probe, h, to, :] = res
                 u2[probe, h, to, :] = (a1 * c0) * v[h] + c1 * res
 
-    def step2(p):
-        to = rows((p + 2) * wy, wy)
-        d = [dw[h, to, :] for h in range(2)]
-        for probe in range(2):
-            v, av = fine_operator(u2, probe, p + 2, d, wy, masks)
+        sweep(bw, 3, dw, first, count, wy, masks, use)
+
+    def step2(first, count):
+        def use(probe, p, v, av):
+            to = rows((p + 2) * wy, wy)
             for h in range(2):
                 res = r1[probe, h, to, :] - av[h]
                 r1[probe, h, to, :] = res
                 u3[probe, h, to, :] = a2 * v[h] + c2 * res
 
+        sweep(u2, 2, dw, first, count, wy, masks, use)
+
     mine = row_mask(wy, (yoff, yoff + ny))
 
-    def step3(p):
-        src = rows((p + 2) * wy, wy)
-        to = rows(p * wy, wy)
-        d = [dw[h, src, :] for h in range(2)]
-        sums = []
-        for probe in range(2):
-            v, av = fine_operator(u3, probe, p + 2, d, wy, masks)
+    def steps3(i, _):
+        totals = {}
+
+        def use(probe, p, v, av):
+            src = rows((p + 2) * wy, wy)
+            to = rows(p * wy, wy)
             total = None
             for h in range(2):
                 out = jnp.where(mine, r1[probe, h, src, :] - av[h], 0.0)
@@ -379,14 +387,12 @@
                     c0 * bw[probe, h, rows((p + 3) * wy, wy), :] + u2[probe, h, src, :] + v[h]
                 )
                 total = out if total is None else total + out
-            sums.append(total)
-        return sums
-
-    def steps3(i, _):
-        for k in range(2):
-            low, high = step3(4 * i + 2 * k), step3(4 * i + 2 * k + 1)
-            for probe in range(2):
-                xs[k, probe] = low[probe] + high[probe]
+            k = len(totals.setdefault(probe, []))
+            totals[probe].append(total)
+            if k % 2:
+                xs[k // 2, probe] = totals[probe][k - 1] + total
+
+        sweep(u3, 2, dw, 4 * i, 4, wy, masks, use)
         for k in range(2):
             for probe in range(2):
                 pair = (
@@ -397,23 +403,21 @@
 
     @pl.when(at.has_l)
     def _():
-        step1(-2)
-        step1(-1)
+        step1(-2, 2)
 
     @pl.when(at.has_r)
     def _():
-        step1(nx)
-        step1(nx + 1)
+        step1(nx, 2)
 
     looped(step1, nx)
 
     @pl.when(at.has_l)
     def _():
-        step2(-1)
+        step2(-1, 1)
 
     @pl.when(at.has_r)
     def _():
-        step2(nx)
+        step2(nx, 1)
 
     looped(step2, nx)
     lax.fori_loop(0, nx // 4, steps3, 0)
@@ -455,10 +459,11 @@
 
 def post_kernel(sz, *refs):
     n = sz.sides
-    agg, r_in, sol_in, dw, coarse, cd, x_a, x_b = refs[:8]
-    ys, cas, cbs = refs[8 : 8 + n], refs[8 + n : 8 + 2 * n], refs[8 + 2 * n : 8 + 3 * n]
+    agg, r_in, sol_in, dw, coarse, cd = refs[:6]
+    ys, x_b, x_a = sorted_messages(sz, ORDER2, refs[6 : 8 + n])
+    cas, cbs = refs[8 + n : 8 + 2 * n], refs[8 + 2 * n : 8 + 3 * n]
     out = refs[8 + 3 * n]
-    cw, cu, cc, st_g, st_u, rh, re, r1, u2, acc, ow, sem = refs[9 + 3 * n :]
+    cw, cu, cc, st_g, st_u, rh, re, r1, u2, acc, pj, ow, sem = refs[9 + 3 * n :]
     nx, ny, wy, cx, cy, wc = sz.nx, sz.ny, sz.wy, sz.cx, sz.cy, sz.wc
     at = Place(sz)
     yoff = at.yoff
@@ -546,37 +551,39 @@
     c0, (a1, c1), (a2, c2) = FINE[0][1], FINE[1], FINE[2]
     valid = row_mask(wy, at.valid)
 
-    def spread(q, r_ref, r_plane, own):
+    def spread(q, r_ref, r_plane, own, slot=0):
         for probe in range(2):
             u = cc[probe, rows((q + REACH) * wc, wc), :]
             sides = [cc[probe, rows((q + REACH - 1 + 2 * k) * wc, wc), :] for k in range(2)]
             u3 = 3.0 * u
             shifted = [pltpu.roll(u, 1, 0), pltpu.roll(u, wc - 1, 0)]
             for row in range(2):
-                st_u[probe, pl.ds(row, wc, stride=2), :] = u
+                st_u[slot, probe, pl.ds(row, wc, stride=2), :] = u
             for h in range(2):
                 g = u3 + (above(u, cmasks) if h else below(u, cmasks))
                 for k in range(2):
                     for row in range(2):
-                        st_g[probe, h, k, pl.ds(row, wc, stride=2), :] = (g + sides[k]) + shifted[row]
+                        st_g[slot, probe, h, k, pl.ds(row, wc, stride=2), :] = (g + sides[k]) + shifted[row]
         for k in range(2):
             to = rows((2 * q + k + 2) * wy, wy)
             for h in range(2):
                 d = dw[h, to, :]
                 for probe in range(2):
-                    u = st_u[probe, rows(yoff, wy), :]
+                    u = st_u[slot, probe, rows(yoff, wy), :]
                     old = r_ref[probe, h, rows((r_plane + k) * wy, wy), :]
-                    res = (old - d * u) + st_g[probe, h, k, rows(yoff, wy), :]
+                    res = (old - d * u) + st_g[slot, probe, h, k, rows(yoff, wy), :]
                     res = jnp.where(valid, res, 0.0)
                     re[probe, h, to, :] = res
                     if own:
                         mine = rows((2 * q + k) * wy, wy)
                         acc[probe, h, mine, :] = (sol_in[probe, h, mine, :] + u) + c0 * res
 
-    def own_planes(q):
-        spread(q, r_in, 2 * q, True)
-
-    looped(own_planes, cx, 2)
+    def own_planes(i, _):
+        for k in range(4):
+            spread(4 * i + k, r_in, 2 * (4 * i + k), True, k)
+        return 0
+
+    lax.fori_loop(0, cx // 4, own_planes, 0)
     zero = jnp.zeros((wy, LANES), F32)
     for has, q, first in ((at.has_l, -1, 0), (at.has_r, cx, 2)):
 
@@ -603,58 +610,68 @@
 
     c1 = jnp.where(row_mask(wy, at.fine), c1, 0.0)
 
-    def step1(p):
-        to = rows((p + 2) * wy, wy)
-        d = [dw[h, to, :] for h in range(2)]
-        for probe in range(2):
-            v, av = fine_operator(re, probe, p + 2, d, wy, masks)
+    def step1(first, count):
+        def use(probe, p, v, av):
+            to = rows((p + 2) * wy, wy)
             for h in range(2):
                 res = v[h] - c0 * av[h]
                 r1[probe, h, to, :] = res
                 u2[probe, h, to, :] = (a1 * c0) * v[h] + c1 * res
 
+        sweep(re, 2, dw, first, count, wy, masks, use)
+
     join = parity_matrix(True)
+    width = 4
+
+    def close(i):
+        slot = i % 2
+        planes = [(probe, k) for probe in range(2) for k in range(width)]
+        own = [
+            jnp.concatenate([pj[slot, probe, h, rows(k * wy + yoff, ny), :] for h in range(2)], axis=1)
+            for probe, k in planes
+        ]
+        joined = permute_lanes(jnp.concatenate(own, axis=0), join, 2)
+        for m, (probe, k) in enumerate(planes):
+            ow[probe, width * i + k] = joined[m * ny : (m + 1) * ny]
+
+    def send(i):
+        part = pl.ds(width * i, width)
+        return pltpu.make_async_copy(ow.at[:, part], out.at[:, part], sem.at[i])
+
+    def step2(i):
+        slot = i % 2
+
+        def use(probe, p, v, av):
+            to = rows((p + 2) * wy, wy)
+            for h in range(2):
+                res = r1[probe, h, to, :] - av[h]
+                pj[slot, probe, h, rows((p - width * i) * wy, wy), :] = acc[probe, h, rows(p * wy, wy), :] + (
+                    (1.0 + a2) * v[h] + c2 * res
+                )
+
+        sweep(u2, 2, dw, width * i, width, wy, masks, use)
 
     def steps2(i, _):
-        width = 4
-        for probe in range(2):
-            done = []
-            for k in range(width):
-                p = width * i + k
-                to = rows((p + 2) * wy, wy)
-                d = [dw[h, to, :] for h in range(2)]
-                v, av = fine_operator(u2, probe, p + 2, d, wy, masks)
-                parts = []
-                for h in range(2):
-                    res = r1[probe, h, to, :] - av[h]
-                    parts.append(acc[probe, h, rows(p * wy, wy), :] + ((1.0 + a2) * v[h] + c2 * res))
-                done.append(jnp.concatenate(parts, axis=1))
-            joined = permute_lanes(jnp.concatenate(done, axis=0), join, 2)
-            for k in range(width):
-                ow[probe, width * i + k] = joined[k * wy : (k + 1) * wy]
+        close(i - 1)
+        step2(i)
+        send(i - 1).start()
         return 0
 
     @pl.when(at.has_l)
     def _():
-        step1(-1)
+        step1(-1, 1)
 
     @pl.when(at.has_r)
     def _():
-        step1(nx)
+        step1(nx, 1)
 
     looped(step1, nx)
-    pieces = 4
-    size = nx // pieces
-    copies = []
-    for i in range(pieces):
-        lax.fori_loop(i * size // 4, (i + 1) * size // 4, steps2, 0)
-        copy = pltpu.make_async_copy(
-            ow.at[:, pl.ds(i * size, size), rows(yoff, ny), :], out.at[:, pl.ds(i * size, size)], sem.at[i]
-        )
-        copy.start()
-        copies.append(copy)
-    for copy in copies:
-        copy.wait()
+    step2(0)
+    lax.fori_loop(1, nx // width, steps2, 0)
+    close(nx // width - 1)
+    send(nx // width - 1).start()
+    for i in range(nx // width):
+        send(i).wait()
 
 
 def on_device(n_gx, n_gy, right_side, diagonal, aggregates):
@@ -672,13 +689,12 @@
     def both(pairs, perm):
         return [(a * n_gy + c, b * n_gy + d) for a, b in pairs for c, d in perm]
 
-    def exchange(messages):
-        m_a, m_b, rest = messages[0], messages[1], messages[2:]
-        got = [lax.ppermute(m_a, "gx", pairs_a), lax.ppermute(m_b, "gx", pairs_b)]
-        got += [lax.ppermute(rest[s], "gy", along[s]) for s in range(n)]
-        got += [lax.ppermute(rest[n + s], ("gx", "gy"), both(pairs_a, along[s])) for s in range(n)]
-        got += [lax.ppermute(rest[2 * n + s], ("gx", "gy"), both(pairs_b, along[s])) for s in range(n)]
-        return got
+    perms = {"a": [("gx", pairs_a)], "b": [("gx", pairs_b)], "y": [("gy", perm) for perm in along]}
+    corner_perms = [(("gx", "gy"), both(pairs, perm)) for pairs in (pairs_a, pairs_b) for perm in along]
+
+    def exchange(order, messages):
+        lines = [line for name in order for line in perms[name]] + corner_perms
+        return [lax.ppermute(m, *line) for m, line in zip(messages, lines)]
 
     smem = pl.BlockSpec(memory_space=pltpu.SMEM)
     vmem = pl.BlockSpec(memory_space=pltpu.VMEM)
@@ -688,14 +704,15 @@
     def shape(*dims):
         return jax.ShapeDtypeStruct(dims, F32)
 
-    def messages(x, y, c):
-        return [shape(x, LANES)] * 2 + [shape(y, LANES)] * n + [shape(c, LANES)] * (2 * n)
+    def messages(order, x, y, c):
+        sizes = [y if name == "y" else x for name in order for _ in perms[name]]
+        return [shape(size, LANES) for size in sizes + [c] * (2 * n)]
 
     packed = pl.pallas_call(
         functools.partial(pack_kernel, sz),
         in_specs=[hbm] * 2,
         out_specs=[vmem] * (2 + 3 * n),
-        out_shape=messages(sz.x1, sz.y1, sz.c1),
+        out_shape=messages(ORDER1, sz.x1, sz.y1, sz.c1),
         scratch_shapes=[
             pltpu.VMEM((2, 2, 3, ny, nz), F32),
             pltpu.VMEM((2, 2, ny, nz), F32),
@@ -708,34 +725,31 @@
         compiler_params=pltpu.CompilerParams(vmem_limit_bytes=120 << 19),
         name="pack_kernel",
     )(right_side, diagonal)
-    halos = exchange(packed)
+    halos = exchange(ORDER1, packed)
     bw, dw, cd = pl.pallas_call(
         functools.partial(open_kernel, sz),
-        in_specs=[pl.BlockSpec(memory_space=pl.ANY), hbm, hbm],
+        in_specs=[vmem] * 2,
         out_specs=[vmem] * 3,
         out_shape=[shape(*sz.bw), shape(*sz.dw), shape(sz.coarse, LANES)],
         scratch_shapes=[
-            pltpu.VMEM((2, nx, ny, nz), F32),
-            pltpu.VMEM((nx, ny, nz), F32),
             pltpu.VMEM((2, ny, LANES), F32),
-            pltpu.SemaphoreType.DMA((4, 2)),
         ],
         compiler_params=params,
         name="open_kernel",
-    )(packed[-1], right_side, diagonal)
+    )(right_side, diagonal)
     results = pl.pallas_call(
         functools.partial(pre_kernel, sz),
         in_specs=[vmem] * (5 + 3 * n),
         out_specs=[vmem] * (7 + 3 * n),
         out_shape=[shape(*sz.bw), shape(*sz.dw), shape(*sz.brick), shape(*sz.brick), shape(2, sz.coarse, LANES)]
-        + messages(sz.x2, sz.y2, sz.c2),
+        + messages(ORDER2, sz.x2, sz.y2, sz.c2),
         scratch_shapes=[pltpu.VMEM((2, 2, (nx + 4) * wy, LANES), F32)] * 3 + [pltpu.VMEM((2, 2, wy, LANES), F32)],
         input_output_aliases={0: 0, 1: 1},
         compiler_params=params,
         name="pre_smooth",
     )(bw, dw, cd, *halos)
     dw, r_own, sol, coarse = results[1:5]
-    halos = exchange(results[5:])
+    halos = exchange(ORDER2, results[5:])
     planes = cx + 2 * REACH
     return pl.pallas_call(
         functools.partial(post_kernel, sz),
@@ -746,15 +760,16 @@
             pltpu.VMEM((3, planes * wc, LANES), F32),
             pltpu.VMEM((2, 2, planes * wc, LANES), F32),
             pltpu.VMEM((2, planes * wc, LANES), F32),
-            pltpu.VMEM((2, 2, 2, 2 * wc, LANES), F32),
-            pltpu.VMEM((2, 2 * wc, LANES), F32),
+            pltpu.VMEM((4, 2, 2, 2, 2 * wc, LANES), F32),
+            pltpu.VMEM((4, 2, 2 * wc, LANES), F32),
             pltpu.VMEM((2, 2, 4 * wy, LANES), F32),
         ]
         + [pltpu.VMEM((2, 2, (nx + 4) * wy, LANES), F32)] * 3
         + [
             pltpu.VMEM(sz.brick, F32),
-            pltpu.VMEM((2, nx, wy, nz), F32),
-            pltpu.SemaphoreType.DMA((4,)),
+            pltpu.VMEM((2, 2, 2, 4 * wy, LANES), F32),
+            pltpu.VMEM((2, nx, ny, nz), F32),
+            pltpu.SemaphoreType.DMA((nx // 4,)),
         ],
         compiler_params=params,
         name="correct_and_smooth",

time: 47.6 us -> 44.2 us (0.929)
  the two profiles are of different devices: /device:TPU:17 before, /device:TPU:21 now
where the time goes in v3:
time: 44.2 us; the launch traced here: 44 us
  Pallas kernels  20.3 us (46%)
  starting transfers between devices  17.3 us (39%)
  waiting for transfers between devices  6.26 us (14%)
    ppermute x10, starting transfers between devices, exchange(): return [lax.ppermute(m, *line) for m, line in zip(messages, lines)]  17.3 us
    pallas_call x1, Pallas kernels, on_device(): pl.pallas_call(functools.partial(post_kernel, sz), in_specs=[smem] + [vme...  9.63 us
    ppermute x10, waiting for transfers between devices, exchange(): return [lax.ppermute(m, *line) for m, line in zip(messages, lines)]  6.26 us
    pallas_call x1, Pallas kernels, on_device(): pl.pallas_call(functools.partial(pre_kernel, sz), in_specs=[vmem] * (5 +...  5.37 us
    pallas_call x1, Pallas kernels, on_device(): pl.pallas_call(functools.partial(pack_kernel, sz), in_specs=[hbm] * 2, ou...  2.99 us
    pallas_call x1, Pallas kernels, on_device(): pl.pallas_call(functools.partial(open_kernel, sz), in_specs=[vmem] * 2, o...  2.32 us
  transfers between devices with their start and end apart: 10, of which 3 were waited for; matrix products, arithmetic and copies ran while one was open for 0% of the time, Pallas kernels for 5%

profile of v3, /device:TPU:21, one launch (start us, length us, event | category | flops | bytes accessed | tf_op | source)
XLA Modules:
  0.0 44.0 jit_solution(14601557414368776136)
XLA Ops:
  0.0 0.0 copy-start.1
  0.0 0.0 copy-start
  0.0 3.0 %pack_kernel.1 = (f32[512,128]{1,0:T(8,128)}, f32[512,128]{1,0:T(8,128)}, f32[512,128]{1,0:T(8,128)}, f32[16,128]{1,0:T(8,128)}, f32[16,128]{1,0:T(8,128)}) custom-call(f32[2,32,32,256]{3,2,1,0:T(8,128)} %refs_0_.2, f32[32,32,256]{2,1,0:T(8,128)} %refs_1_.1), custom_call_target="tpu_custom_call" | custom-call | tf_op jit(solution)/shard_map/pack_kernel/pallas_call | solution.py:711
  3.0 0.7 %collective-permute-start = (f32[512,128]{1,0:T(8,128)}, f32[512,128]{1,0:T(8,128)S(1)}, u32[]{:S(2)}, u32[]{:S(2)}) collective-permute-start(f32[512,128]{1,0:T(8,128)} %get-tuple-element.25), channel_id=1, source_target_pairs={{0,2},{2,0},{4,6},{6,4},{8,10},{10,8},{12,14},{14,12},{16,18},{18,... | collective-permute-start | bytes 786440 | tf_op jit(solution)/shard_map/ppermute | solution.py:697
  3.7 3.0 %collective-permute-start.1 = (f32[512,128]{1,0:T(8,128)}, f32[512,128]{1,0:T(8,128)S(1)}, u32[]{:S(2)}, u32[]{:S(2)}) collective-permute-start(f32[512,128]{1,0:T(8,128)} %get-tuple-element.26), channel_id=1, source_target_pairs={{2,4},{6,8},{10,12},{14,16},{18,20},{22,24},{26,28},{4,2},{8,6},{1... | collective-permute-start | bytes 786440 | tf_op jit(solution)/shard_map/ppermute | solution.py:697
  6.8 0.3 collective-permute-start.2
  7.1 1.8 %collective-permute-start.3 = (f32[16,128]{1,0:T(8,128)}, f32[16,128]{1,0:T(8,128)S(1)}, u32[]{:S(2)}, u32[]{:S(2)}) collective-permute-start(f32[16,128]{1,0:T(8,128)} %get-tuple-element.28), channel_id=1, source_target_pairs={{0,3},{1,2},{2,1},{3,0},{4,7},{5,6},{6,5},{7,4},{8,11},{9,10},{10,... | collective-permute-start | bytes 24584 | tf_op jit(solution)/shard_map/ppermute | solution.py:697
  8.9 2.8 %collective-permute-start.4 = (f32[16,128]{1,0:T(8,128)}, f32[16,128]{1,0:T(8,128)S(1)}, u32[]{:S(2)}, u32[]{:S(2)}) collective-permute-start(f32[16,128]{1,0:T(8,128)} %get-tuple-element.29), channel_id=1, source_target_pairs={{2,5},{3,4},{6,9},{7,8},{10,13},{11,12},{14,17},{15,16},{18,21},{1... | collective-permute-start | bytes 24584 | tf_op jit(solution)/shard_map/ppermute | solution.py:697
  11.7 0.0 copy-done.1
  11.7 0.0 copy-done
  11.7 2.3 %open_kernel.1 = (f32[2,2,1520,128]{3,2,1,0:T(8,128)S(1)}, f32[2,1440,128]{2,1,0:T(8,128)S(1)}, f32[256,128]{1,0:T(8,128)S(1)}) custom-call(f32[2,32,32,256]{3,2,1,0:T(8,128)S(1)} %copy-done, f32[32,32,256]{2,1,0:T(8,128)S(1)} %copy-done.1), custom_call_target="tpu_custom_call" | custom-call | tf_op jit(solution)/shard_map/open_kernel/pallas_call | solution.py:729
  14.0 1.6 %collective-permute-done.3.refs_6_ = f32[16,128]{1,0:T(8,128)S(1)} collective-permute-done((f32[16,128]{1,0:T(8,128)}, f32[16,128]{1,0:T(8,128)S(1)}, u32[]{:S(2)}, u32[]{:S(2)}) %collective-permute-start.3) | collective-permute-done | bytes 8224 | tf_op jit(solution)/shard_map/ppermute | solution.py:697
  15.6 0.0 collective-permute-done.4.refs_7_
  15.6 0.0 collective-permute-done.refs_3_
  15.6 0.0 collective-permute-done.1.refs_4_
  15.7 0.0 collective-permute-done.2.refs_5_
  15.7 0.0 copy-start.2
  15.7 5.4 %pre_smooth.1 = (f32[2,2,1520,128]{3,2,1,0:T(8,128)S(1)}, f32[2,1440,128]{2,1,0:T(8,128)S(1)}, f32[2,2,1280,128]{3,2,1,0:T(8,128)S(1)}, f32[2,2,1280,128]{3,2,1,...) custom-call(f32[2,2,1520,128]{3,2,1,0:T(8,128)S(1)} %get-tuple-eleme, ...), custom_call_target="tpu_custom_call", output_to_operand_aliasing={{0}: (0, {}), {1}: (1, {})} | custom-call | tf_op jit(solution)/shard_map/pre_smooth/pallas_call | solution.py:740
  21.1 0.2 collective-permute-start.5
  21.3 3.8 %collective-permute-start.6 = (f32[576,128]{1,0:T(8,128)S(1)}, f32[576,128]{1,0:T(8,128)S(1)}, u32[]{:S(2)}, u32[]{:S(2)}) collective-permute-start(f32[576,128]{1,0:T(8,128)S(1)} %get-tuple-element.35), channel_id=1, source_target_pairs={{2,4},{6,8},{10,12},{14,16},{18,20},{22,24},{26,28},{4,2},{8,6},{1... | collective-permute-start | bytes 884744 | tf_op jit(solution)/shard_map/ppermute | solution.py:697
  25.1 0.1 collective-permute-start.7
  25.2 1.6 %collective-permute-start.8 = (f32[64,128]{1,0:T(8,128)S(1)}, f32[64,128]{1,0:T(8,128)S(1)}, u32[]{:S(2)}, u32[]{:S(2)}) collective-permute-start(f32[64,128]{1,0:T(8,128)S(1)} %get-tuple-element.37), channel_id=1, source_target_pairs={{0,3},{1,2},{2,1},{3,0},{4,7},{5,6},{6,5},{7,4},{8,11},{9,10},{10,... | collective-permute-start | bytes 98312 | tf_op jit(solution)/shard_map/ppermute | solution.py:697
  26.8 2.9 %collective-permute-start.9 = (f32[64,128]{1,0:T(8,128)S(1)}, f32[64,128]{1,0:T(8,128)S(1)}, u32[]{:S(2)}, u32[]{:S(2)}) collective-permute-start(f32[64,128]{1,0:T(8,128)S(1)} %get-tuple-element.38), channel_id=1, source_target_pairs={{2,5},{3,4},{6,9},{7,8},{10,13},{11,12},{14,17},{15,16},{18,21},{1... | collective-permute-start | bytes 98312 | tf_op jit(solution)/shard_map/ppermute | solution.py:697
  29.7 0.9 %collective-permute-done.8.refs_9_ = f32[64,128]{1,0:T(8,128)S(1)} collective-permute-done((f32[64,128]{1,0:T(8,128)S(1)}, f32[64,128]{1,0:T(8,128)S(1)}, u32[]{:S(2)}, u32[]{:S(2)}) %collective-permute-start.8) | collective-permute-done | bytes 32800 | tf_op jit(solution)/shard_map/ppermute | solution.py:697
  30.6 3.8 %collective-permute-done.9.refs_10_ = f32[64,128]{1,0:T(8,128)S(1)} collective-permute-done((f32[64,128]{1,0:T(8,128)S(1)}, f32[64,128]{1,0:T(8,128)S(1)}, u32[]{:S(2)}, u32[]{:S(2)}) %collective-permute-start.9) | collective-permute-done | bytes 32800 | tf_op jit(solution)/shard_map/ppermute | solution.py:697
  34.3 0.0 collective-permute-done.5.refs_6_
  34.3 0.0 collective-permute-done.6.refs_7_
  34.3 0.0 collective-permute-done.7.refs_8_
  34.3 0.0 copy-done.2
  34.3 9.6 %correct_and_smooth.1 = f32[2,32,32,256]{3,2,1,0:T(8,128)} custom-call(s32[16]{0:T(128)S(1)} %copy-done.2, f32[2,2,1280,128]{3,2,1,0:T(8,128)S(1)} %get-tuple-element.30.refs_1_, f32[2,2,1280,128]{3,2,1,0:T(8,128)S(1)} %get-tuple-element.31.refs_2_, f32[2,1440,128]{2,1,0:T(8,128)S(1)} %get-tuple-element.32.refs_3_, ...), custom_call_target="tpu_custom_call" | custom-call | tf_op jit(solution)/shard_map/correct_and_smooth/pallas_call | solution.py:754
Async XLA Ops:
  0.0 11.7 %copy-start.1 = (f32[32,32,256]{2,1,0:T(8,128)S(1)}, f32[32,32,256]{2,1,0:T(8,128)}, u32[]{:S(2)}) copy-start(f32[32,32,256]{2,1,0:T(8,128)} %refs_1_.1) | copy-start | bytes 3145732
  0.0 11.7 %copy-start = (f32[2,32,32,256]{3,2,1,0:T(8,128)S(1)}, f32[2,32,32,256]{3,2,1,0:T(8,128)}, u32[]{:S(2)}) copy-start(f32[2,32,32,256]{3,2,1,0:T(8,128)} %refs_0_.2) | copy-start | bytes 6291460
  3.0 12.6 %collective-permute-start = (f32[512,128]{1,0:T(8,128)}, f32[512,128]{1,0:T(8,128)S(1)}, u32[]{:S(2)}, u32[]{:S(2)}) collective-permute-start(f32[512,128]{1,0:T(8,128)} %get-tuple-element.25), channel_id=1, source_target_pairs={{0,2},{2,0},{4,6},{6,4},{8,10},{10,8},{12,14},{14,12},{16,18},{18,... | collective-permute-start | bytes 786440 | tf_op jit(solution)/shard_map/ppermute | solution.py:697
  3.7 11.9 %collective-permute-start.1 = (f32[512,128]{1,0:T(8,128)}, f32[512,128]{1,0:T(8,128)S(1)}, u32[]{:S(2)}, u32[]{:S(2)}) collective-permute-start(f32[512,128]{1,0:T(8,128)} %get-tuple-element.26), channel_id=1, source_target_pairs={{2,4},{6,8},{10,12},{14,16},{18,20},{22,24},{26,28},{4,2},{8,6},{1... | collective-permute-start | bytes 786440 | tf_op jit(solution)/shard_map/ppermute | solution.py:697
  6.8 8.9 %collective-permute-start.2 = (f32[512,128]{1,0:T(8,128)}, f32[512,128]{1,0:T(8,128)S(1)}, u32[]{:S(2)}, u32[]{:S(2)}) collective-permute-start(f32[512,128]{1,0:T(8,128)} %get-tuple-element.27), channel_id=1, source_target_pairs={{0,1},{1,0},{2,3},{3,2},{4,5},{5,4},{6,7},{7,6},{8,9},{9,8},{10,11... | collective-permute-start | bytes 786440 | tf_op jit(solution)/shard_map/ppermute | solution.py:697
  7.1 8.6 %collective-permute-start.3 = (f32[16,128]{1,0:T(8,128)}, f32[16,128]{1,0:T(8,128)S(1)}, u32[]{:S(2)}, u32[]{:S(2)}) collective-permute-start(f32[16,128]{1,0:T(8,128)} %get-tuple-element.28), channel_id=1, source_target_pairs={{0,3},{1,2},{2,1},{3,0},{4,7},{5,6},{6,5},{7,4},{8,11},{9,10},{10,... | collective-permute-start | bytes 24584 | tf_op jit(solution)/shard_map/ppermute | solution.py:697
  8.9 6.8 %collective-permute-start.4 = (f32[16,128]{1,0:T(8,128)}, f32[16,128]{1,0:T(8,128)S(1)}, u32[]{:S(2)}, u32[]{:S(2)}) collective-permute-start(f32[16,128]{1,0:T(8,128)} %get-tuple-element.29), channel_id=1, source_target_pairs={{2,5},{3,4},{6,9},{7,8},{10,13},{11,12},{14,17},{15,16},{18,21},{1... | collective-permute-start | bytes 24584 | tf_op jit(solution)/shard_map/ppermute | solution.py:697
  15.7 18.7 %copy-start.2 = (s32[16]{0:T(128)S(1)}, s32[16]{0:T(128)}, u32[]{:S(2)}) copy-start(s32[16]{0:T(128)} %refs_0_.3) | copy-start | bytes 196
  21.1 13.3 %collective-permute-start.5 = (f32[576,128]{1,0:T(8,128)S(1)}, f32[576,128]{1,0:T(8,128)S(1)}, u32[]{:S(2)}, u32[]{:S(2)}) collective-permute-start(f32[576,128]{1,0:T(8,128)S(1)} %get-tuple-element.34), channel_id=1, source_target_pairs={{0,1},{1,0},{2,3},{3,2},{4,5},{5,4},{6,7},{7,6},{8,9},{9,8},{10,11... | collective-permute-start | bytes 884744 | tf_op jit(solution)/shard_map/ppermute | solution.py:697
  21.3 13.1 %collective-permute-start.6 = (f32[576,128]{1,0:T(8,128)S(1)}, f32[576,128]{1,0:T(8,128)S(1)}, u32[]{:S(2)}, u32[]{:S(2)}) collective-permute-start(f32[576,128]{1,0:T(8,128)S(1)} %get-tuple-element.35), channel_id=1, source_target_pairs={{2,4},{6,8},{10,12},{14,16},{18,20},{22,24},{26,28},{4,2},{8,6},{1... | collective-permute-start | bytes 884744 | tf_op jit(solution)/shard_map/ppermute | solution.py:697
  25.1 9.2 %collective-permute-start.7 = (f32[576,128]{1,0:T(8,128)S(1)}, f32[576,128]{1,0:T(8,128)S(1)}, u32[]{:S(2)}, u32[]{:S(2)}) collective-permute-start(f32[576,128]{1,0:T(8,128)S(1)} %get-tuple-element.36), channel_id=1, source_target_pairs={{0,2},{2,0},{4,6},{6,4},{8,10},{10,8},{12,14},{14,12},{16,18},{18,... | collective-permute-start | bytes 884744 | tf_op jit(solution)/shard_map/ppermute | solution.py:697
  25.2 5.4 %collective-permute-start.8 = (f32[64,128]{1,0:T(8,128)S(1)}, f32[64,128]{1,0:T(8,128)S(1)}, u32[]{:S(2)}, u32[]{:S(2)}) collective-permute-start(f32[64,128]{1,0:T(8,128)S(1)} %get-tuple-element.37), channel_id=1, source_target_pairs={{0,3},{1,2},{2,1},{3,0},{4,7},{5,6},{6,5},{7,4},{8,11},{9,10},{10,... | collective-permute-start | bytes 98312 | tf_op jit(solution)/shard_map/ppermute | solution.py:697
  26.8 7.5 %collective-permute-start.9 = (f32[64,128]{1,0:T(8,128)S(1)}, f32[64,128]{1,0:T(8,128)S(1)}, u32[]{:S(2)}, u32[]{:S(2)}) collective-permute-start(f32[64,128]{1,0:T(8,128)S(1)} %get-tuple-element.38), channel_id=1, source_target_pairs={{2,5},{3,4},{6,9},{7,8},{10,13},{11,12},{14,17},{15,16},{18,21},{1... | collective-permute-start | bytes 98312 | tf_op jit(solution)/shard_map/ppermute | solution.py:697

commit v4 on v3

--- a/solution.py
+++ b/solution.py
@@ -525,7 +525,9 @@
                     before = before * link_r
                 if p == REACH + cx - 1:
                     after = after * link_r
-                near = ((before + after) + y_sum(u)) + (below(u, cmasks) + above(u, cmasks))
+                row = p * wc
+                beside = cu[old, probe, pl.ds(row - 1, wc), :] + cu[old, probe, pl.ds(row + 1, wc), :]
+                near = ((before + after) + beside) + (below(u, cmasks) + above(u, cmasks))
                 res = cw[probe, to, :] - (cw[2, to, :] * u - near)
                 u = a * u + c * res
                 if k + 2 < COARSE_DEG:
@@ -722,7 +724,7 @@
             pltpu.VMEM((n, 2, nx * 8, LANES), F32),
             pltpu.SemaphoreType.DMA((2 * n + 4,)),
         ],
-        compiler_params=pltpu.CompilerParams(vmem_limit_bytes=120 << 19),
+        compiler_params=pltpu.CompilerParams(vmem_limit_bytes=105 << 19),
         name="pack_kernel",
     )(right_side, diagonal)
     halos = exchange(ORDER1, packed)

time: 44.2 us -> 43 us (0.973)
  Pallas kernels: 20.3 us -> 19.2 us
    pallas_call x1, Pallas kernels: 2.99 us -> 2.19 us  [on_device(): pl.pallas_call(functools.partial(pack_kernel, sz), in_specs=[hbm] * 2, ou...]
where the time goes in v4:
time: 43 us; the launch traced here: 42.7 us
  Pallas kernels  19.2 us (45%)
  starting transfers between devices  17.3 us (40%)
  waiting for transfers between devices  6.05 us (14%)
    ppermute x10, starting transfers between devices, exchange(): return [lax.ppermute(m, *line) for m, line in zip(messages, lines)]  17.3 us
    pallas_call x1, Pallas kernels, on_device(): pl.pallas_call(functools.partial(post_kernel, sz), in_specs=[smem] + [vme...  9.34 us
    ppermute x10, waiting for transfers between devices, exchange(): return [lax.ppermute(m, *line) for m, line in zip(messages, lines)]  6.05 us
    pallas_call x1, Pallas kernels, on_device(): pl.pallas_call(functools.partial(pre_kernel, sz), in_specs=[vmem] * (5 +...  5.37 us
    pallas_call x1, Pallas kernels, on_device(): pl.pallas_call(functools.partial(open_kernel, sz), in_specs=[vmem] * 2, o...  2.32 us
    pallas_call x1, Pallas kernels, on_device(): pl.pallas_call(functools.partial(pack_kernel, sz), in_specs=[hbm] * 2, ou...  2.19 us
  transfers between devices with their start and end apart: 10, of which 3 were waited for; matrix products, arithmetic and copies ran while one was open for 0% of the time, Pallas kernels for 5%

profile of v4, /device:TPU:21, one launch (start us, length us, event | category | flops | bytes accessed | tf_op | source)
XLA Modules:
  0.0 42.7 jit_solution(5958980737540726202)
XLA Ops:
  0.0 0.0 copy-start.1
  0.0 0.0 copy-start
  0.0 2.2 %pack_kernel.1 = (f32[512,128]{1,0:T(8,128)S(1)}, f32[512,128]{1,0:T(8,128)S(1)}, f32[512,128]{1,0:T(8,128)S(1)}, f32[16,128]{1,0:T(8,128)S(1)}, f32[16,128]{1,0:T(8,128)S(1)}) custom-call(f32[2,32,32,256]{3,2,1,0:T(8,128)} %refs_0_.2, f32[32,32,256]{2,1,0:T(8,128)} %refs_1_.1), custom_call_target="tpu_custom_call" | custom-call | tf_op jit(solution)/shard_map/pack_kernel/pallas_call | solution.py:713
  2.2 0.7 %collective-permute-start = (f32[512,128]{1,0:T(8,128)S(1)}, f32[512,128]{1,0:T(8,128)S(1)}, u32[]{:S(2)}, u32[]{:S(2)}) collective-permute-start(f32[512,128]{1,0:T(8,128)S(1)} %get-tuple-element.25), channel_id=1, source_target_pairs={{0,2},{2,0},{4,6},{6,4},{8,10},{10,8},{12,14},{14,12},{16,18},{18,... | collective-permute-start | bytes 786440 | tf_op jit(solution)/shard_map/ppermute | solution.py:699
  2.9 3.0 %collective-permute-start.1 = (f32[512,128]{1,0:T(8,128)S(1)}, f32[512,128]{1,0:T(8,128)S(1)}, u32[]{:S(2)}, u32[]{:S(2)}) collective-permute-start(f32[512,128]{1,0:T(8,128)S(1)} %get-tuple-element.26), channel_id=1, source_target_pairs={{2,4},{6,8},{10,12},{14,16},{18,20},{22,24},{26,28},{4,2},{8,6},{1... | collective-permute-start | bytes 786440 | tf_op jit(solution)/shard_map/ppermute | solution.py:699
  6.0 0.3 collective-permute-start.2
  6.3 1.8 %collective-permute-start.3 = (f32[16,128]{1,0:T(8,128)S(1)}, f32[16,128]{1,0:T(8,128)S(1)}, u32[]{:S(2)}, u32[]{:S(2)}) collective-permute-start(f32[16,128]{1,0:T(8,128)S(1)} %get-tuple-element.28), channel_id=1, source_target_pairs={{0,3},{1,2},{2,1},{3,0},{4,7},{5,6},{6,5},{7,4},{8,11},{9,10},{10,... | collective-permute-start | bytes 24584 | tf_op jit(solution)/shard_map/ppermute | solution.py:699
  8.1 2.8 %collective-permute-start.4 = (f32[16,128]{1,0:T(8,128)S(1)}, f32[16,128]{1,0:T(8,128)S(1)}, u32[]{:S(2)}, u32[]{:S(2)}) collective-permute-start(f32[16,128]{1,0:T(8,128)S(1)} %get-tuple-element.29), channel_id=1, source_target_pairs={{2,5},{3,4},{6,9},{7,8},{10,13},{11,12},{14,17},{15,16},{18,21},{1... | collective-permute-start | bytes 24584 | tf_op jit(solution)/shard_map/ppermute | solution.py:699
  10.9 0.0 copy-done.1
  10.9 0.0 copy-done
  10.9 2.3 %open_kernel.1 = (f32[2,2,1520,128]{3,2,1,0:T(8,128)S(1)}, f32[2,1440,128]{2,1,0:T(8,128)S(1)}, f32[256,128]{1,0:T(8,128)S(1)}) custom-call(f32[2,32,32,256]{3,2,1,0:T(8,128)S(1)} %copy-done, f32[32,32,256]{2,1,0:T(8,128)S(1)} %copy-done.1), custom_call_target="tpu_custom_call" | custom-call | tf_op jit(solution)/shard_map/open_kernel/pallas_call | solution.py:731
  13.2 1.4 %collective-permute-done.3.refs_6_ = f32[16,128]{1,0:T(8,128)S(1)} collective-permute-done((f32[16,128]{1,0:T(8,128)S(1)}, f32[16,128]{1,0:T(8,128)S(1)}, u32[]{:S(2)}, u32[]{:S(2)}) %collective-permute-start.3) | collective-permute-done | bytes 8224 | tf_op jit(solution)/shard_map/ppermute | solution.py:699
  14.6 0.0 collective-permute-done.4.refs_7_
  14.6 0.0 collective-permute-done.refs_3_
  14.6 0.0 collective-permute-done.1.refs_4_
  14.6 0.0 collective-permute-done.2.refs_5_
  14.7 0.0 copy-start.2
  14.7 5.4 %pre_smooth.1 = (f32[2,2,1520,128]{3,2,1,0:T(8,128)S(1)}, f32[2,1440,128]{2,1,0:T(8,128)S(1)}, f32[2,2,1280,128]{3,2,1,0:T(8,128)S(1)}, f32[2,2,1280,128]{3,2,1,...) custom-call(f32[2,2,1520,128]{3,2,1,0:T(8,128)S(1)} %get-tuple-eleme, ...), custom_call_target="tpu_custom_call", output_to_operand_aliasing={{0}: (0, {}), {1}: (1, {})} | custom-call | tf_op jit(solution)/shard_map/pre_smooth/pallas_call | solution.py:742
  20.0 0.2 collective-permute-start.5
  20.2 3.8 %collective-permute-start.6 = (f32[576,128]{1,0:T(8,128)S(1)}, f32[576,128]{1,0:T(8,128)S(1)}, u32[]{:S(2)}, u32[]{:S(2)}) collective-permute-start(f32[576,128]{1,0:T(8,128)S(1)} %get-tuple-element.35), channel_id=1, source_target_pairs={{2,4},{6,8},{10,12},{14,16},{18,20},{22,24},{26,28},{4,2},{8,6},{1... | collective-permute-start | bytes 884744 | tf_op jit(solution)/shard_map/ppermute | solution.py:699
  24.1 0.1 collective-permute-start.7
  24.2 1.6 %collective-permute-start.8 = (f32[64,128]{1,0:T(8,128)S(1)}, f32[64,128]{1,0:T(8,128)S(1)}, u32[]{:S(2)}, u32[]{:S(2)}) collective-permute-start(f32[64,128]{1,0:T(8,128)S(1)} %get-tuple-element.37), channel_id=1, source_target_pairs={{0,3},{1,2},{2,1},{3,0},{4,7},{5,6},{6,5},{7,4},{8,11},{9,10},{10,... | collective-permute-start | bytes 98312 | tf_op jit(solution)/shard_map/ppermute | solution.py:699
  25.8 2.9 %collective-permute-start.9 = (f32[64,128]{1,0:T(8,128)S(1)}, f32[64,128]{1,0:T(8,128)S(1)}, u32[]{:S(2)}, u32[]{:S(2)}) collective-permute-start(f32[64,128]{1,0:T(8,128)S(1)} %get-tuple-element.38), channel_id=1, source_target_pairs={{2,5},{3,4},{6,9},{7,8},{10,13},{11,12},{14,17},{15,16},{18,21},{1... | collective-permute-start | bytes 98312 | tf_op jit(solution)/shard_map/ppermute | solution.py:699
  28.7 0.9 %collective-permute-done.8.refs_9_ = f32[64,128]{1,0:T(8,128)S(1)} collective-permute-done((f32[64,128]{1,0:T(8,128)S(1)}, f32[64,128]{1,0:T(8,128)S(1)}, u32[]{:S(2)}, u32[]{:S(2)}) %collective-permute-start.8) | collective-permute-done | bytes 32800 | tf_op jit(solution)/shard_map/ppermute | solution.py:699
  29.5 3.8 %collective-permute-done.9.refs_10_ = f32[64,128]{1,0:T(8,128)S(1)} collective-permute-done((f32[64,128]{1,0:T(8,128)S(1)}, f32[64,128]{1,0:T(8,128)S(1)}, u32[]{:S(2)}, u32[]{:S(2)}) %collective-permute-start.9) | collective-permute-done | bytes 32800 | tf_op jit(solution)/shard_map/ppermute | solution.py:699
  33.3 0.0 collective-permute-done.5.refs_6_
  33.3 0.0 collective-permute-done.6.refs_7_
  33.3 0.0 collective-permute-done.7.refs_8_
  33.3 0.0 copy-done.2
  33.3 9.3 %correct_and_smooth.1 = f32[2,32,32,256]{3,2,1,0:T(8,128)} custom-call(s32[16]{0:T(128)S(1)} %copy-done.2, f32[2,2,1280,128]{3,2,1,0:T(8,128)S(1)} %get-tuple-element.30.refs_1_, f32[2,2,1280,128]{3,2,1,0:T(8,128)S(1)} %get-tuple-element.31.refs_2_, f32[2,1440,128]{2,1,0:T(8,128)S(1)} %get-tuple-element.32.refs_3_, ...), custom_call_target="tpu_custom_call" | custom-call | tf_op jit(solution)/shard_map/correct_and_smooth/pallas_call | solution.py:756
Async XLA Ops:
  0.0 10.9 %copy-start.1 = (f32[32,32,256]{2,1,0:T(8,128)S(1)}, f32[32,32,256]{2,1,0:T(8,128)}, u32[]{:S(2)}) copy-start(f32[32,32,256]{2,1,0:T(8,128)} %refs_1_.1) | copy-start | bytes 3145732
  0.0 10.9 %copy-start = (f32[2,32,32,256]{3,2,1,0:T(8,128)S(1)}, f32[2,32,32,256]{3,2,1,0:T(8,128)}, u32[]{:S(2)}) copy-start(f32[2,32,32,256]{3,2,1,0:T(8,128)} %refs_0_.2) | copy-start | bytes 6291460
  2.2 12.4 %collective-permute-start = (f32[512,128]{1,0:T(8,128)S(1)}, f32[512,128]{1,0:T(8,128)S(1)}, u32[]{:S(2)}, u32[]{:S(2)}) collective-permute-start(f32[512,128]{1,0:T(8,128)S(1)} %get-tuple-element.25), channel_id=1, source_target_pairs={{0,2},{2,0},{4,6},{6,4},{8,10},{10,8},{12,14},{14,12},{16,18},{18,... | collective-permute-start | bytes 786440 | tf_op jit(solution)/shard_map/ppermute | solution.py:699
  2.9 11.7 %collective-permute-start.1 = (f32[512,128]{1,0:T(8,128)S(1)}, f32[512,128]{1,0:T(8,128)S(1)}, u32[]{:S(2)}, u32[]{:S(2)}) collective-permute-start(f32[512,128]{1,0:T(8,128)S(1)} %get-tuple-element.26), channel_id=1, source_target_pairs={{2,4},{6,8},{10,12},{14,16},{18,20},{22,24},{26,28},{4,2},{8,6},{1... | collective-permute-start | bytes 786440 | tf_op jit(solution)/shard_map/ppermute | solution.py:699
  6.0 8.7 %collective-permute-start.2 = (f32[512,128]{1,0:T(8,128)S(1)}, f32[512,128]{1,0:T(8,128)S(1)}, u32[]{:S(2)}, u32[]{:S(2)}) collective-permute-start(f32[512,128]{1,0:T(8,128)S(1)} %get-tuple-element.27), channel_id=1, source_target_pairs={{0,1},{1,0},{2,3},{3,2},{4,5},{5,4},{6,7},{7,6},{8,9},{9,8},{10,11... | collective-permute-start | bytes 786440 | tf_op jit(solution)/shard_map/ppermute | solution.py:699
  6.3 8.4 %collective-permute-start.3 = (f32[16,128]{1,0:T(8,128)S(1)}, f32[16,128]{1,0:T(8,128)S(1)}, u32[]{:S(2)}, u32[]{:S(2)}) collective-permute-start(f32[16,128]{1,0:T(8,128)S(1)} %get-tuple-element.28), channel_id=1, source_target_pairs={{0,3},{1,2},{2,1},{3,0},{4,7},{5,6},{6,5},{7,4},{8,11},{9,10},{10,... | collective-permute-start | bytes 24584 | tf_op jit(solution)/shard_map/ppermute | solution.py:699
  8.1 6.6 %collective-permute-start.4 = (f32[16,128]{1,0:T(8,128)S(1)}, f32[16,128]{1,0:T(8,128)S(1)}, u32[]{:S(2)}, u32[]{:S(2)}) collective-permute-start(f32[16,128]{1,0:T(8,128)S(1)} %get-tuple-element.29), channel_id=1, source_target_pairs={{2,5},{3,4},{6,9},{7,8},{10,13},{11,12},{14,17},{15,16},{18,21},{1... | collective-permute-start | bytes 24584 | tf_op jit(solution)/shard_map/ppermute | solution.py:699
  14.7 18.7 %copy-start.2 = (s32[16]{0:T(128)S(1)}, s32[16]{0:T(128)}, u32[]{:S(2)}) copy-start(s32[16]{0:T(128)} %refs_0_.3) | copy-start | bytes 196
  20.0 13.3 %collective-permute-start.5 = (f32[576,128]{1,0:T(8,128)S(1)}, f32[576,128]{1,0:T(8,128)S(1)}, u32[]{:S(2)}, u32[]{:S(2)}) collective-permute-start(f32[576,128]{1,0:T(8,128)S(1)} %get-tuple-element.34), channel_id=1, source_target_pairs={{0,1},{1,0},{2,3},{3,2},{4,5},{5,4},{6,7},{7,6},{8,9},{9,8},{10,11... | collective-permute-start | bytes 884744 | tf_op jit(solution)/shard_map/ppermute | solution.py:699
  20.2 13.1 %collective-permute-start.6 = (f32[576,128]{1,0:T(8,128)S(1)}, f32[576,128]{1,0:T(8,128)S(1)}, u32[]{:S(2)}, u32[]{:S(2)}) collective-permute-start(f32[576,128]{1,0:T(8,128)S(1)} %get-tuple-element.35), channel_id=1, source_target_pairs={{2,4},{6,8},{10,12},{14,16},{18,20},{22,24},{26,28},{4,2},{8,6},{1... | collective-permute-start | bytes 884744 | tf_op jit(solution)/shard_map/ppermute | solution.py:699
  24.1 9.2 %collective-permute-start.7 = (f32[576,128]{1,0:T(8,128)S(1)}, f32[576,128]{1,0:T(8,128)S(1)}, u32[]{:S(2)}, u32[]{:S(2)}) collective-permute-start(f32[576,128]{1,0:T(8,128)S(1)} %get-tuple-element.36), channel_id=1, source_target_pairs={{0,2},{2,0},{4,6},{6,4},{8,10},{10,8},{12,14},{14,12},{16,18},{18,... | collective-permute-start | bytes 884744 | tf_op jit(solution)/shard_map/ppermute | solution.py:699
  24.2 5.4 %collective-permute-start.8 = (f32[64,128]{1,0:T(8,128)S(1)}, f32[64,128]{1,0:T(8,128)S(1)}, u32[]{:S(2)}, u32[]{:S(2)}) collective-permute-start(f32[64,128]{1,0:T(8,128)S(1)} %get-tuple-element.37), channel_id=1, source_target_pairs={{0,3},{1,2},{2,1},{3,0},{4,7},{5,6},{6,5},{7,4},{8,11},{9,10},{10,... | collective-permute-start | bytes 98312 | tf_op jit(solution)/shard_map/ppermute | solution.py:699
  25.8 7.5 %collective-permute-start.9 = (f32[64,128]{1,0:T(8,128)S(1)}, f32[64,128]{1,0:T(8,128)S(1)}, u32[]{:S(2)}, u32[]{:S(2)}) collective-permute-start(f32[64,128]{1,0:T(8,128)S(1)} %get-tuple-element.38), channel_id=1, source_target_pairs={{2,5},{3,4},{6,9},{7,8},{10,13},{11,12},{14,17},{15,16},{18,21},{1... | collective-permute-start | bytes 98312 | tf_op jit(solution)/shard_map/ppermute | solution.py:699

commit v5 on v4

--- a/solution.py
+++ b/solution.py
@@ -55,9 +55,9 @@
         self.x1 = 8 * 2 * ny
         self.y1 = 8 * 2 * nx
         self.c1 = 16
-        self.x2_base = (3 * REACH - 1) * self.cy
+        self.x2_base = (3 * REACH - 4) * self.cy
         self.x2 = self.x2_base + 8 * ny
-        self.y2_base = (3 * REACH - 1) * self.cx
+        self.y2_base = (3 * REACH - 4) * self.cx
         self.y2 = self.y2_base + 8 * nx
         self.c2 = 64
 
@@ -426,8 +426,9 @@
     depth = [REACH, REACH, REACH - 1]
     for msg, corners, right in ((m_a, m_cas, at.even), (m_b, m_cbs, at.odd)):
         for f in range(3):
-            size = depth[f] * cy
-            msg[pl.ds(f * REACH * cy, size), :] = field[f][rows(edge(right, cx, depth[f]) * cy, size), :]
+            size = (depth[f] - 1) * cy
+            first = pick(right, cx - depth[f], 1)
+            msg[pl.ds(f * (REACH - 1) * cy, size), :] = field[f][rows(first * cy, size), :]
         for s in range(n):
             for m, (f, p, q) in enumerate(CORNER2):
                 row = pick(at.high_out[s], cy - 1 - q, q) + pick(right, cx - 1 - p, p) * cy
@@ -446,9 +447,9 @@
                     msg[pl.ds(sz.x2_base + i * ny, ny), :] = r_out[probe, h, rows(row, ny), :]
     for s in range(n):
         for f in range(3):
-            for k in range(depth[f]):
-                row = edge(at.high_out[s], cy, depth[f]) + k
-                m_ys[s][pl.ds((f * REACH + k) * cx, cx), :] = field[f][pl.ds(row, cx, stride=cy), :]
+            for k in range(depth[f] - 1):
+                row = pick(at.high_out[s], cy - depth[f], 1) + k
+                m_ys[s][pl.ds((f * (REACH - 1) + k) * cx, cx), :] = field[f][pl.ds(row, cx, stride=cy), :]
         row = edge(at.high_out[s], ny, 2) + yoff
         for probe in range(2):
             for h in range(2):
@@ -463,7 +464,7 @@
     ys, x_b, x_a = sorted_messages(sz, ORDER2, refs[6 : 8 + n])
     cas, cbs = refs[8 + n : 8 + 2 * n], refs[8 + 2 * n : 8 + 3 * n]
     out = refs[8 + 3 * n]
-    cw, cu, cc, st_g, st_u, rh, re, r1, u2, acc, pj, ow, sem = refs[9 + 3 * n :]
+    cw, cu, cc, pt, st_g, st_u, rh, re, r1, u2, acc, pj, ow, sem = refs[9 + 3 * n :]
     nx, ny, wy, cx, cy, wc = sz.nx, sz.ny, sz.wy, sz.cx, sz.cy, sz.wc
     at = Place(sz)
     yoff = at.yoff
@@ -481,13 +482,41 @@
         for x in range(cx):
             cw[f, rows((x + REACH) * wc + yoff, cy), :] = field[f][rows(x * cy, cy), :]
         for s in range(n):
-            for k in range(depth[f]):
-                row = pick(at.high_in[s], yoff + cy, yoff - depth[f]) + k
-                cw[f, pl.ds(REACH * wc + row, cx, stride=wc), :] = ys[s][rows((f * REACH + k) * cx, cx), :]
-        for msg, to_right in ((x_a, at.even), (x_b, at.odd)):
-            first = jnp.where(to_right, REACH + cx, REACH - depth[f])
-            for k in range(depth[f]):
-                cw[f, rows((first + k) * wc + yoff, cy), :] = msg[rows((f * REACH + k) * cy, cy), :]
+            for k in range(depth[f] - 1):
+                row = pick(at.high_in[s], yoff + cy + 1, yoff - depth[f]) + k
+                cw[f, pl.ds(REACH * wc + row, cx, stride=wc), :] = ys[s][rows((f * (REACH - 1) + k) * cx, cx), :]
+            total = None
+            for h in range(2):
+                for k in range(2):
+                    if f == 2:
+                        row = pick(at.high_in[s], yoff + ny, yoff - 2) + k
+                        part = dw[h, pl.ds(2 * wy + row, nx, stride=wy), :]
+                    else:
+                        part = ys[s][pl.ds(sz.y2_base + ((f * 2 + h) * 2 + k) * nx, nx), :]
+                    total = part if total is None else total + part
+            slot = 6 + s * 3 + f
+            pt[slot, pl.ds(0, nx), :] = total
+            pair = pt[slot, pl.ds(0, cx, stride=2), :] + pt[slot, pl.ds(1, cx, stride=2), :]
+            row = pick(at.high_in[s], yoff + cy, yoff - 1)
+            cw[f, pl.ds(REACH * wc + row, cx, stride=wc), :] = 0.5 * pair - (18.0 if f == 2 else 0.0)
+        for side, (msg, to_right) in enumerate(((x_a, at.even), (x_b, at.odd))):
+            first = jnp.where(to_right, REACH + cx + 1, REACH - depth[f])
+            for k in range(depth[f] - 1):
+                cw[f, rows((first + k) * wc + yoff, cy), :] = msg[rows((f * (REACH - 1) + k) * cy, cy), :]
+            total = None
+            for h in range(2):
+                for k in range(2):
+                    if f == 2:
+                        plane = jnp.where(to_right, nx + 2, 0) + k
+                        part = dw[h, rows(plane * wy + yoff, ny), :]
+                    else:
+                        part = msg[pl.ds(sz.x2_base + ((f * 2 + h) * 2 + k) * ny, ny), :]
+                    total = part if total is None else total + part
+            slot = side * 3 + f
+            pt[slot, pl.ds(0, ny), :] = total
+            pair = pt[slot, pl.ds(0, cy, stride=2), :] + pt[slot, pl.ds(1, cy, stride=2), :]
+            plane = jnp.where(to_right, REACH + cx, REACH - 1)
+            cw[f, rows(plane * wc + yoff, cy), :] = 0.5 * pair - (18.0 if f == 2 else 0.0)
     for corners, to_right in ((cas, at.even), (cbs, at.odd)):
         for s in range(n):
             for m, (f, p, q) in enumerate(CORNER2):
@@ -762,6 +791,7 @@
             pltpu.VMEM((3, planes * wc, LANES), F32),
             pltpu.VMEM((2, 2, planes * wc, LANES), F32),
             pltpu.VMEM((2, planes * wc, LANES), F32),
+            pltpu.VMEM((6 + 3 * n, max(nx, ny), LANES), F32),
             pltpu.VMEM((4, 2, 2, 2, 2 * wc, LANES), F32),
             pltpu.VMEM((4, 2, 2 * wc, LANES), F32),
             pltpu.VMEM((2, 2, 4 * wy, LANES), F32),

time: 43 us -> 42.6 us (level)
  waiting for transfers between devices: 6.05 us -> 5.51 us
    ppermute x10, waiting for transfers between devices: 6.05 us -> 5.51 us  [exchange(): return [lax.ppermute(m, *line) for m, line in zip(messages, lines)]]
where the time goes in v5:
time: 42.6 us; the launch traced here: 42.4 us
  Pallas kernels  19.5 us (46%)
  starting transfers between devices  17.3 us (41%)
  waiting for transfers between devices  5.51 us (13%)
    ppermute x10, starting transfers between devices, exchange(): return [lax.ppermute(m, *line) for m, line in zip(messages, lines)]  17.3 us
    pallas_call x1, Pallas kernels, on_device(): pl.pallas_call(functools.partial(post_kernel, sz), in_specs=[smem] + [vme...  9.18 us
    pallas_call x1, Pallas kernels, on_device(): pl.pallas_call(functools.partial(pre_kernel, sz), in_specs=[vmem] * (5 +...  5.78 us
    ppermute x10, waiting for transfers between devices, exchange(): return [lax.ppermute(m, *line) for m, line in zip(messages, lines)]  5.51 us
    pallas_call x1, Pallas kernels, on_device(): pl.pallas_call(functools.partial(open_kernel, sz), in_specs=[vmem] * 2, o...  2.32 us
    pallas_call x1, Pallas kernels, on_device(): pl.pallas_call(functools.partial(pack_kernel, sz), in_specs=[hbm] * 2, ou...  2.19 us
  transfers between devices with their start and end apart: 10, of which 3 were waited for; matrix products, arithmetic and copies ran while one was open for 0% of the time, Pallas kernels for 5%

profile of v5, /device:TPU:21, one launch (start us, length us, event | category | flops | bytes accessed | tf_op | source)
XLA Modules:
  0.0 42.4 jit_solution(6770880881792275097)
XLA Ops:
  0.0 0.0 copy-start.1
  0.0 0.0 copy-start
  0.0 2.2 %pack_kernel.1 = (f32[512,128]{1,0:T(8,128)S(1)}, f32[512,128]{1,0:T(8,128)S(1)}, f32[512,128]{1,0:T(8,128)S(1)}, f32[16,128]{1,0:T(8,128)S(1)}, f32[16,128]{1,0:T(8,128)S(1)}) custom-call(f32[2,32,32,256]{3,2,1,0:T(8,128)} %refs_0_.2, f32[32,32,256]{2,1,0:T(8,128)} %refs_1_.1), custom_call_target="tpu_custom_call" | custom-call | tf_op jit(solution)/shard_map/pack_kernel/pallas_call | solution.py:742
  2.2 0.7 %collective-permute-start = (f32[512,128]{1,0:T(8,128)S(1)}, f32[512,128]{1,0:T(8,128)S(1)}, u32[]{:S(2)}, u32[]{:S(2)}) collective-permute-start(f32[512,128]{1,0:T(8,128)S(1)} %get-tuple-element.25), channel_id=1, source_target_pairs={{0,2},{2,0},{4,6},{6,4},{8,10},{10,8},{12,14},{14,12},{16,18},{18,... | collective-permute-start | bytes 786440 | tf_op jit(solution)/shard_map/ppermute | solution.py:728
  2.9 3.0 %collective-permute-start.1 = (f32[512,128]{1,0:T(8,128)S(1)}, f32[512,128]{1,0:T(8,128)S(1)}, u32[]{:S(2)}, u32[]{:S(2)}) collective-permute-start(f32[512,128]{1,0:T(8,128)S(1)} %get-tuple-element.26), channel_id=1, source_target_pairs={{2,4},{6,8},{10,12},{14,16},{18,20},{22,24},{26,28},{4,2},{8,6},{1... | collective-permute-start | bytes 786440 | tf_op jit(solution)/shard_map/ppermute | solution.py:728
  6.0 0.3 collective-permute-start.2
  6.3 1.8 %collective-permute-start.3 = (f32[16,128]{1,0:T(8,128)S(1)}, f32[16,128]{1,0:T(8,128)S(1)}, u32[]{:S(2)}, u32[]{:S(2)}) collective-permute-start(f32[16,128]{1,0:T(8,128)S(1)} %get-tuple-element.28), channel_id=1, source_target_pairs={{0,3},{1,2},{2,1},{3,0},{4,7},{5,6},{6,5},{7,4},{8,11},{9,10},{10,... | collective-permute-start | bytes 24584 | tf_op jit(solution)/shard_map/ppermute | solution.py:728
  8.1 2.8 %collective-permute-start.4 = (f32[16,128]{1,0:T(8,128)S(1)}, f32[16,128]{1,0:T(8,128)S(1)}, u32[]{:S(2)}, u32[]{:S(2)}) collective-permute-start(f32[16,128]{1,0:T(8,128)S(1)} %get-tuple-element.29), channel_id=1, source_target_pairs={{2,5},{3,4},{6,9},{7,8},{10,13},{11,12},{14,17},{15,16},{18,21},{1... | collective-permute-start | bytes 24584 | tf_op jit(solution)/shard_map/ppermute | solution.py:728
  10.9 0.0 copy-done.1
  10.9 0.0 copy-done
  10.9 2.3 %open_kernel.1 = (f32[2,2,1520,128]{3,2,1,0:T(8,128)S(1)}, f32[2,1440,128]{2,1,0:T(8,128)S(1)}, f32[256,128]{1,0:T(8,128)S(1)}) custom-call(f32[2,32,32,256]{3,2,1,0:T(8,128)S(1)} %copy-done, f32[32,32,256]{2,1,0:T(8,128)S(1)} %copy-done.1), custom_call_target="tpu_custom_call" | custom-call | tf_op jit(solution)/shard_map/open_kernel/pallas_call | solution.py:760
  13.2 1.4 %collective-permute-done.3.refs_6_ = f32[16,128]{1,0:T(8,128)S(1)} collective-permute-done((f32[16,128]{1,0:T(8,128)S(1)}, f32[16,128]{1,0:T(8,128)S(1)}, u32[]{:S(2)}, u32[]{:S(2)}) %collective-permute-start.3) | collective-permute-done | bytes 8224 | tf_op jit(solution)/shard_map/ppermute | solution.py:728
  14.6 0.0 collective-permute-done.4.refs_7_
  14.6 0.0 collective-permute-done.refs_3_
  14.6 0.0 collective-permute-done.1.refs_4_
  14.6 0.0 collective-permute-done.2.refs_5_
  14.7 0.0 copy-start.2
  14.7 5.8 %pre_smooth.1 = (f32[2,2,1520,128]{3,2,1,0:T(8,128)S(1)}, f32[2,1440,128]{2,1,0:T(8,128)S(1)}, f32[2,2,1280,128]{3,2,1,0:T(8,128)S(1)}, f32[2,2,1280,128]{3,2,1,...) custom-call(f32[2,2,1520,128]{3,2,1,0:T(8,128)S(1)} %get-tuple-eleme, ...), custom_call_target="tpu_custom_call", output_to_operand_aliasing={{0}: (0, {}), {1}: (1, {})} | custom-call | tf_op jit(solution)/shard_map/pre_smooth/pallas_call | solution.py:771
  20.4 0.2 collective-permute-start.5
  20.7 3.8 %collective-permute-start.6 = (f32[528,128]{1,0:T(8,128)S(1)}, f32[528,128]{1,0:T(8,128)S(1)}, u32[]{:S(2)}, u32[]{:S(2)}) collective-permute-start(f32[528,128]{1,0:T(8,128)S(1)} %get-tuple-element.35), channel_id=1, source_target_pairs={{2,4},{6,8},{10,12},{14,16},{18,20},{22,24},{26,28},{4,2},{8,6},{1... | collective-permute-start | bytes 811016 | tf_op jit(solution)/shard_map/ppermute | solution.py:728
  24.5 0.1 collective-permute-start.7
  24.6 1.6 %collective-permute-start.8 = (f32[64,128]{1,0:T(8,128)S(1)}, f32[64,128]{1,0:T(8,128)S(1)}, u32[]{:S(2)}, u32[]{:S(2)}) collective-permute-start(f32[64,128]{1,0:T(8,128)S(1)} %get-tuple-element.37), channel_id=1, source_target_pairs={{0,3},{1,2},{2,1},{3,0},{4,7},{5,6},{6,5},{7,4},{8,11},{9,10},{10,... | collective-permute-start | bytes 98312 | tf_op jit(solution)/shard_map/ppermute | solution.py:728
  26.2 2.9 %collective-permute-start.9 = (f32[64,128]{1,0:T(8,128)S(1)}, f32[64,128]{1,0:T(8,128)S(1)}, u32[]{:S(2)}, u32[]{:S(2)}) collective-permute-start(f32[64,128]{1,0:T(8,128)S(1)} %get-tuple-element.38), channel_id=1, source_target_pairs={{2,5},{3,4},{6,9},{7,8},{10,13},{11,12},{14,17},{15,16},{18,21},{1... | collective-permute-start | bytes 98312 | tf_op jit(solution)/shard_map/ppermute | solution.py:728
  29.1 0.5 %collective-permute-done.8.refs_9_ = f32[64,128]{1,0:T(8,128)S(1)} collective-permute-done((f32[64,128]{1,0:T(8,128)S(1)}, f32[64,128]{1,0:T(8,128)S(1)}, u32[]{:S(2)}, u32[]{:S(2)}) %collective-permute-start.8) | collective-permute-done | bytes 32800 | tf_op jit(solution)/shard_map/ppermute | solution.py:728
  29.6 3.6 %collective-permute-done.9.refs_10_ = f32[64,128]{1,0:T(8,128)S(1)} collective-permute-done((f32[64,128]{1,0:T(8,128)S(1)}, f32[64,128]{1,0:T(8,128)S(1)}, u32[]{:S(2)}, u32[]{:S(2)}) %collective-permute-start.9) | collective-permute-done | bytes 32800 | tf_op jit(solution)/shard_map/ppermute | solution.py:728
  33.2 0.0 collective-permute-done.5.refs_6_
  33.2 0.0 collective-permute-done.6.refs_7_
  33.2 0.0 collective-permute-done.7.refs_8_
  33.2 0.0 copy-done.2
  33.2 9.2 %correct_and_smooth.1 = f32[2,32,32,256]{3,2,1,0:T(8,128)} custom-call(s32[16]{0:T(128)S(1)} %copy-done.2, f32[2,2,1280,128]{3,2,1,0:T(8,128)S(1)} %get-tuple-element.30.refs_1_, f32[2,2,1280,128]{3,2,1,0:T(8,128)S(1)} %get-tuple-element.31.refs_2_, f32[2,1440,128]{2,1,0:T(8,128)S(1)} %get-tuple-element.32.refs_3_, ...), custom_call_target="tpu_custom_call" | custom-call | tf_op jit(solution)/shard_map/correct_and_smooth/pallas_call | solution.py:785
Async XLA Ops:
  0.0 10.9 %copy-start.1 = (f32[32,32,256]{2,1,0:T(8,128)S(1)}, f32[32,32,256]{2,1,0:T(8,128)}, u32[]{:S(2)}) copy-start(f32[32,32,256]{2,1,0:T(8,128)} %refs_1_.1) | copy-start | bytes 3145732
  0.0 10.9 %copy-start = (f32[2,32,32,256]{3,2,1,0:T(8,128)S(1)}, f32[2,32,32,256]{3,2,1,0:T(8,128)}, u32[]{:S(2)}) copy-start(f32[2,32,32,256]{3,2,1,0:T(8,128)} %refs_0_.2) | copy-start | bytes 6291460
  2.2 12.4 %collective-permute-start = (f32[512,128]{1,0:T(8,128)S(1)}, f32[512,128]{1,0:T(8,128)S(1)}, u32[]{:S(2)}, u32[]{:S(2)}) collective-permute-start(f32[512,128]{1,0:T(8,128)S(1)} %get-tuple-element.25), channel_id=1, source_target_pairs={{0,2},{2,0},{4,6},{6,4},{8,10},{10,8},{12,14},{14,12},{16,18},{18,... | collective-permute-start | bytes 786440 | tf_op jit(solution)/shard_map/ppermute | solution.py:728
  2.9 11.7 %collective-permute-start.1 = (f32[512,128]{1,0:T(8,128)S(1)}, f32[512,128]{1,0:T(8,128)S(1)}, u32[]{:S(2)}, u32[]{:S(2)}) collective-permute-start(f32[512,128]{1,0:T(8,128)S(1)} %get-tuple-element.26), channel_id=1, source_target_pairs={{2,4},{6,8},{10,12},{14,16},{18,20},{22,24},{26,28},{4,2},{8,6},{1... | collective-permute-start | bytes 786440 | tf_op jit(solution)/shard_map/ppermute | solution.py:728
  6.0 8.7 %collective-permute-start.2 = (f32[512,128]{1,0:T(8,128)S(1)}, f32[512,128]{1,0:T(8,128)S(1)}, u32[]{:S(2)}, u32[]{:S(2)}) collective-permute-start(f32[512,128]{1,0:T(8,128)S(1)} %get-tuple-element.27), channel_id=1, source_target_pairs={{0,1},{1,0},{2,3},{3,2},{4,5},{5,4},{6,7},{7,6},{8,9},{9,8},{10,11... | collective-permute-start | bytes 786440 | tf_op jit(solution)/shard_map/ppermute | solution.py:728
  6.3 8.4 %collective-permute-start.3 = (f32[16,128]{1,0:T(8,128)S(1)}, f32[16,128]{1,0:T(8,128)S(1)}, u32[]{:S(2)}, u32[]{:S(2)}) collective-permute-start(f32[16,128]{1,0:T(8,128)S(1)} %get-tuple-element.28), channel_id=1, source_target_pairs={{0,3},{1,2},{2,1},{3,0},{4,7},{5,6},{6,5},{7,4},{8,11},{9,10},{10,... | collective-permute-start | bytes 24584 | tf_op jit(solution)/shard_map/ppermute | solution.py:728
  8.1 6.6 %collective-permute-start.4 = (f32[16,128]{1,0:T(8,128)S(1)}, f32[16,128]{1,0:T(8,128)S(1)}, u32[]{:S(2)}, u32[]{:S(2)}) collective-permute-start(f32[16,128]{1,0:T(8,128)S(1)} %get-tuple-element.29), channel_id=1, source_target_pairs={{2,5},{3,4},{6,9},{7,8},{10,13},{11,12},{14,17},{15,16},{18,21},{1... | collective-permute-start | bytes 24584 | tf_op jit(solution)/shard_map/ppermute | solution.py:728
  14.7 18.5 %copy-start.2 = (s32[16]{0:T(128)S(1)}, s32[16]{0:T(128)}, u32[]{:S(2)}) copy-start(s32[16]{0:T(128)} %refs_0_.3) | copy-start | bytes 196
  20.4 12.7 %collective-permute-start.5 = (f32[528,128]{1,0:T(8,128)S(1)}, f32[528,128]{1,0:T(8,128)S(1)}, u32[]{:S(2)}, u32[]{:S(2)}) collective-permute-start(f32[528,128]{1,0:T(8,128)S(1)} %get-tuple-element.34), channel_id=1, source_target_pairs={{0,1},{1,0},{2,3},{3,2},{4,5},{5,4},{6,7},{7,6},{8,9},{9,8},{10,11... | collective-permute-start | bytes 811016 | tf_op jit(solution)/shard_map/ppermute | solution.py:728
  20.7 12.5 %collective-permute-start.6 = (f32[528,128]{1,0:T(8,128)S(1)}, f32[528,128]{1,0:T(8,128)S(1)}, u32[]{:S(2)}, u32[]{:S(2)}) collective-permute-start(f32[528,128]{1,0:T(8,128)S(1)} %get-tuple-element.35), channel_id=1, source_target_pairs={{2,4},{6,8},{10,12},{14,16},{18,20},{22,24},{26,28},{4,2},{8,6},{1... | collective-permute-start | bytes 811016 | tf_op jit(solution)/shard_map/ppermute | solution.py:728
  24.5 8.7 %collective-permute-start.7 = (f32[528,128]{1,0:T(8,128)S(1)}, f32[528,128]{1,0:T(8,128)S(1)}, u32[]{:S(2)}, u32[]{:S(2)}) collective-permute-start(f32[528,128]{1,0:T(8,128)S(1)} %get-tuple-element.36), channel_id=1, source_target_pairs={{0,2},{2,0},{4,6},{6,4},{8,10},{10,8},{12,14},{14,12},{16,18},{18,... | collective-permute-start | bytes 811016 | tf_op jit(solution)/shard_map/ppermute | solution.py:728
  24.6 5.0 %collective-permute-start.8 = (f32[64,128]{1,0:T(8,128)S(1)}, f32[64,128]{1,0:T(8,128)S(1)}, u32[]{:S(2)}, u32[]{:S(2)}) collective-permute-start(f32[64,128]{1,0:T(8,128)S(1)} %get-tuple-element.37), channel_id=1, source_target_pairs={{0,3},{1,2},{2,1},{3,0},{4,7},{5,6},{6,5},{7,4},{8,11},{9,10},{10,... | collective-permute-start | bytes 98312 | tf_op jit(solution)/shard_map/ppermute | solution.py:728
  26.2 7.0 %collective-permute-start.9 = (f32[64,128]{1,0:T(8,128)S(1)}, f32[64,128]{1,0:T(8,128)S(1)}, u32[]{:S(2)}, u32[]{:S(2)}) collective-permute-start(f32[64,128]{1,0:T(8,128)S(1)} %get-tuple-element.38), channel_id=1, source_target_pairs={{2,5},{3,4},{6,9},{7,8},{10,13},{11,12},{14,17},{15,16},{18,21},{1... | collective-permute-start | bytes 98312 | tf_op jit(solution)/shard_map/ppermute | solution.py:728

commit v6 on v5

--- a/solution.py
+++ b/solution.py
@@ -40,7 +40,7 @@
 
 class Sizes:
     def __init__(self, nx, ny, nz, n_gx, n_gy):
-        assert nz == 2 * LANES and n_gy >= 2 and ny % 16 == 0 and nx % 4 == 0
+        assert nz == 2 * LANES and n_gy >= 2 and ny % 16 == 0 and nx % 8 == 0
         self.nx, self.ny, self.nz = nx, ny, nz
         self.n_gx, self.n_gy = n_gx, n_gy
         self.two = n_gy == 2
@@ -166,7 +166,7 @@
             before, now = now, after
 
 
-def looped(step, count, width=4):
+def looped(step, count, width=8):
     def body(i, _):
         step(width * i, width)
         return 0

time: 42.6 us -> 42.2 us (level)
  no operation moved by 1% of the time
where the time goes in v6:
time: 42.2 us; the launch traced here: 42.1 us
  Pallas kernels  19.2 us (45%)
  starting transfers between devices  17.3 us (41%)
  waiting for transfers between devices  5.51 us (13%)
    ppermute x10, starting transfers between devices, exchange(): return [lax.ppermute(m, *line) for m, line in zip(messages, lines)]  17.3 us
    pallas_call x1, Pallas kernels, on_device(): pl.pallas_call(functools.partial(post_kernel, sz), in_specs=[smem] + [vme...  9.09 us
    pallas_call x1, Pallas kernels, on_device(): pl.pallas_call(functools.partial(pre_kernel, sz), in_specs=[vmem] * (5 +...  5.56 us
    ppermute x10, waiting for transfers between devices, exchange(): return [lax.ppermute(m, *line) for m, line in zip(messages, lines)]  5.51 us
    pallas_call x1, Pallas kernels, on_device(): pl.pallas_call(functools.partial(open_kernel, sz), in_specs=[vmem] * 2, o...  2.32 us
    pallas_call x1, Pallas kernels, on_device(): pl.pallas_call(functools.partial(pack_kernel, sz), in_specs=[hbm] * 2, ou...  2.19 us
  transfers between devices with their start and end apart: 10, of which 3 were waited for; matrix products, arithmetic and copies ran while one was open for 0% of the time, Pallas kernels for 5%

profile of v6, /device:TPU:21, one launch (start us, length us, event | category | flops | bytes accessed | tf_op | source)
XLA Modules:
  0.0 42.1 jit_solution(16575700155618592873)
XLA Ops:
  0.0 0.0 copy-start.1
  0.0 0.0 copy-start
  0.0 2.2 %pack_kernel.1 = (f32[512,128]{1,0:T(8,128)S(1)}, f32[512,128]{1,0:T(8,128)S(1)}, f32[512,128]{1,0:T(8,128)S(1)}, f32[16,128]{1,0:T(8,128)S(1)}, f32[16,128]{1,0:T(8,128)S(1)}) custom-call(f32[2,32,32,256]{3,2,1,0:T(8,128)} %refs_0_.2, f32[32,32,256]{2,1,0:T(8,128)} %refs_1_.1), custom_call_target="tpu_custom_call" | custom-call | tf_op jit(solution)/shard_map/pack_kernel/pallas_call | solution.py:742
  2.2 0.7 %collective-permute-start = (f32[512,128]{1,0:T(8,128)S(1)}, f32[512,128]{1,0:T(8,128)S(1)}, u32[]{:S(2)}, u32[]{:S(2)}) collective-permute-start(f32[512,128]{1,0:T(8,128)S(1)} %get-tuple-element.25), channel_id=1, source_target_pairs={{0,2},{2,0},{4,6},{6,4},{8,10},{10,8},{12,14},{14,12},{16,18},{18,... | collective-permute-start | bytes 786440 | tf_op jit(solution)/shard_map/ppermute | solution.py:728
  2.9 3.0 %collective-permute-start.1 = (f32[512,128]{1,0:T(8,128)S(1)}, f32[512,128]{1,0:T(8,128)S(1)}, u32[]{:S(2)}, u32[]{:S(2)}) collective-permute-start(f32[512,128]{1,0:T(8,128)S(1)} %get-tuple-element.26), channel_id=1, source_target_pairs={{2,4},{6,8},{10,12},{14,16},{18,20},{22,24},{26,28},{4,2},{8,6},{1... | collective-permute-start | bytes 786440 | tf_op jit(solution)/shard_map/ppermute | solution.py:728
  6.0 0.3 collective-permute-start.2
  6.3 1.8 %collective-permute-start.3 = (f32[16,128]{1,0:T(8,128)S(1)}, f32[16,128]{1,0:T(8,128)S(1)}, u32[]{:S(2)}, u32[]{:S(2)}) collective-permute-start(f32[16,128]{1,0:T(8,128)S(1)} %get-tuple-element.28), channel_id=1, source_target_pairs={{0,3},{1,2},{2,1},{3,0},{4,7},{5,6},{6,5},{7,4},{8,11},{9,10},{10,... | collective-permute-start | bytes 24584 | tf_op jit(solution)/shard_map/ppermute | solution.py:728
  8.1 2.8 %collective-permute-start.4 = (f32[16,128]{1,0:T(8,128)S(1)}, f32[16,128]{1,0:T(8,128)S(1)}, u32[]{:S(2)}, u32[]{:S(2)}) collective-permute-start(f32[16,128]{1,0:T(8,128)S(1)} %get-tuple-element.29), channel_id=1, source_target_pairs={{2,5},{3,4},{6,9},{7,8},{10,13},{11,12},{14,17},{15,16},{18,21},{1... | collective-permute-start | bytes 24584 | tf_op jit(solution)/shard_map/ppermute | solution.py:728
  10.9 0.0 copy-done.1
  10.9 0.0 copy-done
  10.9 2.3 %open_kernel.1 = (f32[2,2,1520,128]{3,2,1,0:T(8,128)S(1)}, f32[2,1440,128]{2,1,0:T(8,128)S(1)}, f32[256,128]{1,0:T(8,128)S(1)}) custom-call(f32[2,32,32,256]{3,2,1,0:T(8,128)S(1)} %copy-done, f32[32,32,256]{2,1,0:T(8,128)S(1)} %copy-done.1), custom_call_target="tpu_custom_call" | custom-call | tf_op jit(solution)/shard_map/open_kernel/pallas_call | solution.py:760
  13.2 1.4 %collective-permute-done.3.refs_6_ = f32[16,128]{1,0:T(8,128)S(1)} collective-permute-done((f32[16,128]{1,0:T(8,128)S(1)}, f32[16,128]{1,0:T(8,128)S(1)}, u32[]{:S(2)}, u32[]{:S(2)}) %collective-permute-start.3) | collective-permute-done | bytes 8224 | tf_op jit(solution)/shard_map/ppermute | solution.py:728
  14.6 0.0 collective-permute-done.4.refs_7_
  14.6 0.0 collective-permute-done.refs_3_
  14.6 0.0 collective-permute-done.1.refs_4_
  14.6 0.0 collective-permute-done.2.refs_5_
  14.7 0.0 copy-start.2
  14.7 5.6 %pre_smooth.1 = (f32[2,2,1520,128]{3,2,1,0:T(8,128)S(1)}, f32[2,1440,128]{2,1,0:T(8,128)S(1)}, f32[2,2,1280,128]{3,2,1,0:T(8,128)S(1)}, f32[2,2,1280,128]{3,2,1,...) custom-call(f32[2,2,1520,128]{3,2,1,0:T(8,128)S(1)} %get-tuple-eleme, ...), custom_call_target="tpu_custom_call", output_to_operand_aliasing={{0}: (0, {}), {1}: (1, {})} | custom-call | tf_op jit(solution)/shard_map/pre_smooth/pallas_call | solution.py:771
  20.2 0.2 collective-permute-start.5
  20.4 3.8 %collective-permute-start.6 = (f32[528,128]{1,0:T(8,128)S(1)}, f32[528,128]{1,0:T(8,128)S(1)}, u32[]{:S(2)}, u32[]{:S(2)}) collective-permute-start(f32[528,128]{1,0:T(8,128)S(1)} %get-tuple-element.35), channel_id=1, source_target_pairs={{2,4},{6,8},{10,12},{14,16},{18,20},{22,24},{26,28},{4,2},{8,6},{1... | collective-permute-start | bytes 811016 | tf_op jit(solution)/shard_map/ppermute | solution.py:728
  24.3 0.1 collective-permute-start.7
  24.3 1.6 %collective-permute-start.8 = (f32[64,128]{1,0:T(8,128)S(1)}, f32[64,128]{1,0:T(8,128)S(1)}, u32[]{:S(2)}, u32[]{:S(2)}) collective-permute-start(f32[64,128]{1,0:T(8,128)S(1)} %get-tuple-element.37), channel_id=1, source_target_pairs={{0,3},{1,2},{2,1},{3,0},{4,7},{5,6},{6,5},{7,4},{8,11},{9,10},{10,... | collective-permute-start | bytes 98312 | tf_op jit(solution)/shard_map/ppermute | solution.py:728
  26.0 2.9 %collective-permute-start.9 = (f32[64,128]{1,0:T(8,128)S(1)}, f32[64,128]{1,0:T(8,128)S(1)}, u32[]{:S(2)}, u32[]{:S(2)}) collective-permute-start(f32[64,128]{1,0:T(8,128)S(1)} %get-tuple-element.38), channel_id=1, source_target_pairs={{2,5},{3,4},{6,9},{7,8},{10,13},{11,12},{14,17},{15,16},{18,21},{1... | collective-permute-start | bytes 98312 | tf_op jit(solution)/shard_map/ppermute | solution.py:728
  28.8 0.5 %collective-permute-done.8.refs_9_ = f32[64,128]{1,0:T(8,128)S(1)} collective-permute-done((f32[64,128]{1,0:T(8,128)S(1)}, f32[64,128]{1,0:T(8,128)S(1)}, u32[]{:S(2)}, u32[]{:S(2)}) %collective-permute-start.8) | collective-permute-done | bytes 32800 | tf_op jit(solution)/shard_map/ppermute | solution.py:728
  29.4 3.6 %collective-permute-done.9.refs_10_ = f32[64,128]{1,0:T(8,128)S(1)} collective-permute-done((f32[64,128]{1,0:T(8,128)S(1)}, f32[64,128]{1,0:T(8,128)S(1)}, u32[]{:S(2)}, u32[]{:S(2)}) %collective-permute-start.9) | collective-permute-done | bytes 32800 | tf_op jit(solution)/shard_map/ppermute | solution.py:728
  33.0 0.0 collective-permute-done.5.refs_6_
  33.0 0.0 collective-permute-done.6.refs_7_
  33.0 0.0 collective-permute-done.7.refs_8_
  33.0 0.0 copy-done.2
  33.0 9.1 %correct_and_smooth.1 = f32[2,32,32,256]{3,2,1,0:T(8,128)} custom-call(s32[16]{0:T(128)S(1)} %copy-done.2, f32[2,2,1280,128]{3,2,1,0:T(8,128)S(1)} %get-tuple-element.30.refs_1_, f32[2,2,1280,128]{3,2,1,0:T(8,128)S(1)} %get-tuple-element.31.refs_2_, f32[2,1440,128]{2,1,0:T(8,128)S(1)} %get-tuple-element.32.refs_3_, ...), custom_call_target="tpu_custom_call" | custom-call | tf_op jit(solution)/shard_map/correct_and_smooth/pallas_call | solution.py:785
Async XLA Ops:
  0.0 10.9 %copy-start.1 = (f32[32,32,256]{2,1,0:T(8,128)S(1)}, f32[32,32,256]{2,1,0:T(8,128)}, u32[]{:S(2)}) copy-start(f32[32,32,256]{2,1,0:T(8,128)} %refs_1_.1) | copy-start | bytes 3145732
  0.0 10.9 %copy-start = (f32[2,32,32,256]{3,2,1,0:T(8,128)S(1)}, f32[2,32,32,256]{3,2,1,0:T(8,128)}, u32[]{:S(2)}) copy-start(f32[2,32,32,256]{3,2,1,0:T(8,128)} %refs_0_.2) | copy-start | bytes 6291460
  2.2 12.4 %collective-permute-start = (f32[512,128]{1,0:T(8,128)S(1)}, f32[512,128]{1,0:T(8,128)S(1)}, u32[]{:S(2)}, u32[]{:S(2)}) collective-permute-start(f32[512,128]{1,0:T(8,128)S(1)} %get-tuple-element.25), channel_id=1, source_target_pairs={{0,2},{2,0},{4,6},{6,4},{8,10},{10,8},{12,14},{14,12},{16,18},{18,... | collective-permute-start | bytes 786440 | tf_op jit(solution)/shard_map/ppermute | solution.py:728
  2.9 11.7 %collective-permute-start.1 = (f32[512,128]{1,0:T(8,128)S(1)}, f32[512,128]{1,0:T(8,128)S(1)}, u32[]{:S(2)}, u32[]{:S(2)}) collective-permute-start(f32[512,128]{1,0:T(8,128)S(1)} %get-tuple-element.26), channel_id=1, source_target_pairs={{2,4},{6,8},{10,12},{14,16},{18,20},{22,24},{26,28},{4,2},{8,6},{1... | collective-permute-start | bytes 786440 | tf_op jit(solution)/shard_map/ppermute | solution.py:728
  6.0 8.7 %collective-permute-start.2 = (f32[512,128]{1,0:T(8,128)S(1)}, f32[512,128]{1,0:T(8,128)S(1)}, u32[]{:S(2)}, u32[]{:S(2)}) collective-permute-start(f32[512,128]{1,0:T(8,128)S(1)} %get-tuple-element.27), channel_id=1, source_target_pairs={{0,1},{1,0},{2,3},{3,2},{4,5},{5,4},{6,7},{7,6},{8,9},{9,8},{10,11... | collective-permute-start | bytes 786440 | tf_op jit(solution)/shard_map/ppermute | solution.py:728
  6.3 8.4 %collective-permute-start.3 = (f32[16,128]{1,0:T(8,128)S(1)}, f32[16,128]{1,0:T(8,128)S(1)}, u32[]{:S(2)}, u32[]{:S(2)}) collective-permute-start(f32[16,128]{1,0:T(8,128)S(1)} %get-tuple-element.28), channel_id=1, source_target_pairs={{0,3},{1,2},{2,1},{3,0},{4,7},{5,6},{6,5},{7,4},{8,11},{9,10},{10,... | collective-permute-start | bytes 24584 | tf_op jit(solution)/shard_map/ppermute | solution.py:728
  8.1 6.6 %collective-permute-start.4 = (f32[16,128]{1,0:T(8,128)S(1)}, f32[16,128]{1,0:T(8,128)S(1)}, u32[]{:S(2)}, u32[]{:S(2)}) collective-permute-start(f32[16,128]{1,0:T(8,128)S(1)} %get-tuple-element.29), channel_id=1, source_target_pairs={{2,5},{3,4},{6,9},{7,8},{10,13},{11,12},{14,17},{15,16},{18,21},{1... | collective-permute-start | bytes 24584 | tf_op jit(solution)/shard_map/ppermute | solution.py:728
  14.7 18.3 %copy-start.2 = (s32[16]{0:T(128)S(1)}, s32[16]{0:T(128)}, u32[]{:S(2)}) copy-start(s32[16]{0:T(128)} %refs_0_.3) | copy-start | bytes 196
  20.2 12.7 %collective-permute-start.5 = (f32[528,128]{1,0:T(8,128)S(1)}, f32[528,128]{1,0:T(8,128)S(1)}, u32[]{:S(2)}, u32[]{:S(2)}) collective-permute-start(f32[528,128]{1,0:T(8,128)S(1)} %get-tuple-element.34), channel_id=1, source_target_pairs={{0,1},{1,0},{2,3},{3,2},{4,5},{5,4},{6,7},{7,6},{8,9},{9,8},{10,11... | collective-permute-start | bytes 811016 | tf_op jit(solution)/shard_map/ppermute | solution.py:728
  20.4 12.5 %collective-permute-start.6 = (f32[528,128]{1,0:T(8,128)S(1)}, f32[528,128]{1,0:T(8,128)S(1)}, u32[]{:S(2)}, u32[]{:S(2)}) collective-permute-start(f32[528,128]{1,0:T(8,128)S(1)} %get-tuple-element.35), channel_id=1, source_target_pairs={{2,4},{6,8},{10,12},{14,16},{18,20},{22,24},{26,28},{4,2},{8,6},{1... | collective-permute-start | bytes 811016 | tf_op jit(solution)/shard_map/ppermute | solution.py:728
  24.3 8.7 %collective-permute-start.7 = (f32[528,128]{1,0:T(8,128)S(1)}, f32[528,128]{1,0:T(8,128)S(1)}, u32[]{:S(2)}, u32[]{:S(2)}) collective-permute-start(f32[528,128]{1,0:T(8,128)S(1)} %get-tuple-element.36), channel_id=1, source_target_pairs={{0,2},{2,0},{4,6},{6,4},{8,10},{10,8},{12,14},{14,12},{16,18},{18,... | collective-permute-start | bytes 811016 | tf_op jit(solution)/shard_map/ppermute | solution.py:728
  24.3 5.0 %collective-permute-start.8 = (f32[64,128]{1,0:T(8,128)S(1)}, f32[64,128]{1,0:T(8,128)S(1)}, u32[]{:S(2)}, u32[]{:S(2)}) collective-permute-start(f32[64,128]{1,0:T(8,128)S(1)} %get-tuple-element.37), channel_id=1, source_target_pairs={{0,3},{1,2},{2,1},{3,0},{4,7},{5,6},{6,5},{7,4},{8,11},{9,10},{10,... | collective-permute-start | bytes 98312 | tf_op jit(solution)/shard_map/ppermute | solution.py:728
  26.0 7.0 %collective-permute-start.9 = (f32[64,128]{1,0:T(8,128)S(1)}, f32[64,128]{1,0:T(8,128)S(1)}, u32[]{:S(2)}, u32[]{:S(2)}) collective-permute-start(f32[64,128]{1,0:T(8,128)S(1)} %get-tuple-element.38), channel_id=1, source_target_pairs={{2,5},{3,4},{6,9},{7,8},{10,13},{11,12},{14,17},{15,16},{18,21},{1... | collective-permute-start | bytes 98312 | tf_op jit(solution)/shard_map/ppermute | solution.py:728
